TPU v7x, 256 devices: a whole 4x4x8 slice. The times are simulated.
256 devices in a mesh: seq: 64 (over y, z, core), mp: 4 (over x).
Axes of the slice: x: 4, y: 4, z: 8, core: 2. Of those that a mesh axis runs over, the one named last changes fastest.
Arguments:
- tokens: bfloat16 [8192, 3584], P('seq'), may hold values from -6 to 6
- query_weight: bfloat16 [3584, 4096], P('seq', 'mp'), may hold values from -0.09375 to 0.09375
- key_weight: bfloat16 [3584, 4096], P('seq', 'mp'), may hold values from -0.09375 to 0.09375
- value_weight: bfloat16 [3584, 4096], P('seq', 'mp'), may hold values from -0.09375 to 0.09375
- adapter_down_maps: bfloat16 [3584, 128], replicated, may hold values from -0.09375 to 0.09375
- lifting_matrices: bfloat16 [2, 64, 4096], P(None, None, 'mp'), may hold values from -0.75 to 0.75
- decay_logarithms: float32 [32, 8192], P('mp', 'seq'), may hold values from -1 to 0, as said below
- output_gradient: bfloat16 [8192, 4096], P('seq', 'mp'), may hold values from -0.06591797 to 0.06591797
Outputs:
- grad_down: float32 [3584, 128], P(('seq', 'mp'))
- grad_up: float32 [2, 64, 4096], P(None, None, 'mp')
Inputs may be any that keep to these rules, and one draw needn't show every extreme that they name: `decay_logarithms`: every entry is negative.
All inputs are finite; a program needn't handle non-finite values.
Results may differ from a plain program's by a relative error of at most 0.006.
Values may be sent and summed in bfloat16 or wider, within the bound.
No kernel may reach another device: no remote copies, remote signals or barrier semaphores. Data moves between devices by JAX's collectives and lax.ppermute only.
A program may use at most 192 MiB of HBM per device.

v0:
```python
import jax
import jax.numpy as jnp
from jax import lax
from jax.sharding import PartitionSpec as P

adapter_scale = 2.0
eps_norm = 1e-06
exact_arithmetic = lax.Precision.HIGHEST


def carried_in(value, axis, join, neutral, backward):
    count, mine = (lax.axis_size(axis), lax.axis_index(axis))
    pieces = jax.tree.map(lambda part: lax.all_gather(part, axis), value)
    if backward:
        pieces = jax.tree.map(lambda part: part[::-1], pieces)
        mine = count - 1 - mine
    so_far = jax.tree.map(
        lambda part, zero: jnp.full_like(part, 0) + jnp.asarray(zero, part.dtype), value, neutral
    )

    def hop(position, so_far):
        longer = join(so_far, jax.tree.map(lambda part: part[position], pieces))
        return jax.tree.map(lambda new, old: jnp.where(position < mine, new, old), longer, so_far)

    return lax.fori_loop(0, count - 1, hop, so_far)


def combine(earlier, later):
    return (earlier[0] * later[0], later[0][:, None, None] * earlier[1] + later[1])


def split_heads(flat, heads):
    return flat.reshape(flat.shape[0], heads, flat.shape[1] // heads).transpose(1, 0, 2)


def join_heads(arr):
    return arr.transpose(1, 0, 2).reshape(arr.shape[1], arr.shape[0] * arr.shape[2])


def on_device(
    tokens,
    query_weight,
    key_weight,
    value_weight,
    adapter_down_maps,
    lifting_matrices,
    decay_logarithms,
    output_gradient,
):
    length = tokens.shape[0]
    heads = decay_logarithms.shape[0]
    rank_index = lifting_matrices.shape[1]
    low_product = jnp.dot(tokens, adapter_down_maps, preferred_element_type=jnp.float32).astype(
        jnp.bfloat16
    )
    query_low_product = low_product[:, :rank_index]
    value_low_product = low_product[:, rank_index:]
    cumulative = jnp.cumsum(decay_logarithms, axis=1)
    total = cumulative[:, -1]
    gain = jnp.exp(total)
    tail = jnp.exp(total[:, None] - cumulative)
    lead = jnp.exp(cumulative)
    causal = jnp.arange(length)[:, None] >= jnp.arange(length)[None, :]
    spread = cumulative[:, :, None] - cumulative[:, None, :]
    decay_mat = jnp.where(causal[None], jnp.exp(jnp.where(causal[None], spread, 0.0)), 0.0)
    pieces = (
        lax.all_gather(query_weight, "seq", axis=0, tiled=True),
        lax.all_gather(key_weight, "seq", axis=0, tiled=True),
        lax.all_gather(value_weight, "seq", axis=0, tiled=True),
    )
    columns = tokens
    query_frozen_part, key_base, value_frozen_part = tuple(
        (jnp.dot(columns, piece, preferred_element_type=jnp.float32) for piece in pieces)
    )
    value_before_norm = value_frozen_part + adapter_scale * jnp.dot(
        value_low_product, lifting_matrices[1], preferred_element_type=jnp.float32
    )
    key_heads = split_heads(jax.nn.silu(key_base).astype(jnp.bfloat16), heads)
    value_heads = split_heads(value_before_norm.astype(jnp.bfloat16), heads)
    key_f = key_heads.astype(jnp.float32)
    local = jnp.einsum(
        "hsi,hsj->hij",
        key_f * tail[:, :, None],
        value_heads.astype(jnp.float32),
        precision=exact_arithmetic,
    )
    state_in = carried_in(
        (gain, local), "seq", combine, (jnp.ones_like(gain), jnp.zeros_like(local)), False
    )[1]
    key_heads, key_f, value_heads, state_in = (key_heads, key_f, value_heads, state_in)
    query_before_norm = query_frozen_part + adapter_scale * jnp.dot(
        query_low_product, lifting_matrices[0], preferred_element_type=jnp.float32
    )
    query_heads = split_heads(jax.nn.silu(query_before_norm).astype(jnp.bfloat16), heads)
    query_f = query_heads.astype(jnp.float32)
    scores = jnp.einsum("htd,hsd->hts", query_heads, key_heads, preferred_element_type=jnp.float32)
    mixed = (scores * decay_mat).astype(jnp.bfloat16)
    attn = jnp.einsum(
        "hts,hsj->htj", mixed, value_heads, preferred_element_type=jnp.float32
    ) + lead[:, :, None] * jnp.einsum("hti,hij->htj", query_f, state_in, precision=exact_arithmetic)
    rms = jnp.sqrt(jnp.mean(attn * attn, axis=-1, keepdims=True) + eps_norm)
    normed = attn / rms
    upstream = split_heads(output_gradient, heads).astype(jnp.float32)
    d_attn = (upstream - normed * jnp.mean(upstream * normed, axis=-1, keepdims=True)) / rms
    d_attn_b = d_attn.astype(jnp.bfloat16)
    carried = jnp.einsum(
        "hti,htj->hij", query_f * lead[:, :, None], d_attn, precision=exact_arithmetic
    )
    later = carried_in(
        (gain, carried), "seq", combine, (jnp.ones_like(gain), jnp.zeros_like(carried)), True
    )[1]
    d_mixed = (
        jnp.einsum("htj,hsj->hts", d_attn_b, value_heads, preferred_element_type=jnp.float32)
        * decay_mat
    ).astype(jnp.bfloat16)
    d_query = jnp.einsum(
        "hts,hsi->hti", d_mixed, key_heads, preferred_element_type=jnp.float32
    ) + lead[:, :, None] * jnp.einsum("htj,hij->hti", d_attn, state_in, precision=exact_arithmetic)
    d_value = jnp.einsum(
        "hts,htj->hsj", mixed, d_attn_b, preferred_element_type=jnp.float32
    ) + tail[:, :, None] * jnp.einsum("hsi,hij->hsj", key_f, later, precision=exact_arithmetic)
    sig = jax.nn.sigmoid(query_before_norm)
    query_pre_gradient = join_heads(d_query) * (sig * (1.0 + query_before_norm * (1.0 - sig)))
    value_flat_gradient = join_heads(d_value)
    low_product_float = low_product.astype(jnp.float32)
    up_products = jnp.stack(
        [
            adapter_scale
            * jnp.dot(
                low_product_float[:, :rank_index].T, query_pre_gradient, precision=exact_arithmetic
            ),
            adapter_scale
            * jnp.dot(
                low_product_float[:, rank_index:].T, value_flat_gradient, precision=exact_arithmetic
            ),
        ]
    )
    grad_up = lax.psum(up_products, "seq")
    low_gradient = adapter_scale * jnp.concatenate(
        [
            jnp.dot(
                query_pre_gradient,
                lifting_matrices[0].astype(jnp.float32).T,
                precision=exact_arithmetic,
            ),
            jnp.dot(
                value_flat_gradient,
                lifting_matrices[1].astype(jnp.float32).T,
                precision=exact_arithmetic,
            ),
        ],
        axis=1,
    )
    columns = tokens.astype(jnp.float32)
    grad_down = lax.psum_scatter(
        jnp.dot(columns.T, low_gradient, precision=exact_arithmetic),
        ("seq", "mp"),
        scatter_dimension=0,
        tiled=True,
    )
    return (grad_down, grad_up)


def solution(mesh):
    return jax.shard_map(
        on_device,
        mesh=mesh,
        in_specs=(
            P("seq", None),
            P("seq", "mp"),
            P("seq", "mp"),
            P("seq", "mp"),
            P(),
            P(None, None, "mp"),
            P("mp", "seq"),
            P("seq", "mp"),
        ),
        out_specs=(P(("seq", "mp"), None), P(None, None, "mp")),
        check_vma=False,
    )
```

profile of v0, /device:TPU:2, one launch (start us, length us, event | category | flops | bytes accessed | tf_op | source)
XLA Modules:
  0.0 1261.7 jit_solution(11165250688478119228)
XLA Ops:
  10.7 1.7 convolution_convert_fusion
  12.4 83.2 %all-gather.13.cloned.1.call-done = bf16[3584,1024]{1,0:T(8,128)(2,1)} async-done(((bf16[56,1024]{1,0:T(8,128)(2,1)}), bf16[3584,1024]{1,0:T(8,128)(2,1)}) %all-gather.13.cloned.1.call-update) | async-done | bytes 7340048 | tf_op jit(solution)/shard_map/all_gather | solution.py:69
  95.5 4.2 fusion.57
  100.0 76.9 %all-gather.11.cloned.1.call-done = bf16[3584,1024]{1,0:T(8,128)(2,1)} async-done(((bf16[56,1024]{1,0:T(8,128)(2,1)}), bf16[3584,1024]{1,0:T(8,128)(2,1)}) %all-gather.11.cloned.1.call-update) | async-done | bytes 7340048 | tf_op jit(solution)/shard_map/all_gather | solution.py:68
  176.9 4.3 multiply_convert_fusion
  181.2 1.5 fusion.16
  184.2 127.0 %all-reduce = f32[512]{0:T(512)S(1)} all-reduce(f32[512]{0:T(512)S(1)} %dynamic-update-slice), channel_id=2, replica_groups=mesh['seq'=64,'mp'=4] {'seq'}, use_global_device_ids=true, to_apply=%add | all-reduce | flops 512 | bytes 4096
  313.5 4.3 fusion.56
  317.8 1.2 multiply_convert_fusion.1
  320.1 1.8 fusion.9
  321.8 78.4 %all-gather.15.cloned.1.call-done = f32[512,128,128]{2,1,0:T(8,128)} async-done(((f32[8,128,128]{2,1,0:T(8,128)}), f32[512,128,128]{2,1,0:T(8,128)}) %all-gather.15.cloned.1.call-update) | async-done | bytes 33554448 | tf_op jit(solution)/shard_map/all_gather | solution.py:13
  400.3 118.5 %while.28 = (s32[]{:T(128)}, f32[8,128,128]{2,1,0:T(8,128)S(1)}, s32[]{:T(128)}, f32[64,8]{1,0:T(8,128)}, f32[64,8,128,128]{3,2,1,0:T(8,128)}, /*index=5*/s32[]{:T(128)}, s32[]{:T(128)}) while((s32[]{:T(128)}, f32[8,128,128]{2,1,0:T(8,128)S(1)}, s32[]{:T(128)}, f32[64,8]{1,0:T(8,128)}, f32[64,8,128,128]{3,2,1,0:T(8,128)}, ...), condition=%wide.region_2.3_spmd.clone, body=%wide.region_1.2_spmd.clone.sunk | while | flops 524292 | bytes 1573073 | solution.py:25
  400.9 1.2 fusion.87
  402.8 1.2 fusion.87
  414.1 1.2 fusion.87
  459.3 1.2 fusion.87
  491.3 1.2 fusion.87
  519.4 1.4 multiply_reduce_fusion.1
  520.9 2.0 fusion.13
  523.2 1.4 rev.6
  526.2 1.3 fusion.2
  527.6 1.2 multiply_multiply_fusion
  528.9 1.3 fusion.36
  530.2 131.7 %all-gather.17.cloned.1.call-done = f32[512,128,128]{2,1,0:T(8,128)} async-done(((f32[8,128,128]{2,1,0:T(8,128)}), f32[512,128,128]{2,1,0:T(8,128)}) %all-gather.17.cloned.1.call-update) | async-done | bytes 33554448 | tf_op jit(solution)/shard_map/all_gather | solution.py:13
  661.9 23.0 %rev.7 = f32[64,8,128,128]{3,2,1,0:T(8,128)} reverse(f32[64,8,128,128]{3,2,1,0:T(8,128)} %bitcast.144), dimensions={0} | reverse | bytes 67108864 | tf_op jit(solution)/shard_map/rev | solution.py:15
  684.9 118.6 %while.29 = (s32[]{:T(128)}, f32[8,128,128]{2,1,0:T(8,128)S(1)}, s32[]{:T(128)}, f32[64,8]{1,0:T(8,128)}, f32[64,8,128,128]{3,2,1,0:T(8,128)}, /*index=5*/s32[]{:T(128)}, s32[]{:T(128)}) while((s32[]{:T(128)}, f32[8,128,128]{2,1,0:T(8,128)S(1)}, s32[]{:T(128)}, f32[64,8]{1,0:T(8,128)}, f32[64,8,128,128]{3,2,1,0:T(8,128)}, ...), condition=%wide.region_6.7_spmd.clone, body=%wide.region_5.6_spmd.clone.sunk | while | flops 524292 | bytes 1573073 | solution.py:25
  749.6 1.2 fusion.88
  787.3 1.2 fusion.88
  804.6 2.1 convolution_bitcast_fusion
  808.5 258.2 %all-reduce.7.cloned.1.call-done = f32[3584,128]{0,1:T(8,128)} async-done(((f32[3584,128]{0,1:T(8,128)}), f32[3584,128]{0,1:T(8,128)}) %all-reduce.7.cloned.1.call-update) | async-done | bytes 1835024
  1068.3 184.6 %all-reduce.5.cloned.1.call-done = f32[2,64,1024]{2,1,0:T(8,128)} async-done(((f32[2,64,1024]{2,1,0:T(8,128)}), f32[2,64,1024]{2,1,0:T(8,128)}) %all-reduce.5.cloned.1.call-update) | async-done | bytes 524304 | tf_op jit(solution)/shard_map/psum | solution.py:138
  1252.9 1.9 copy.120
  (310 shorter events, 240.8 us)
Async XLA Ops:
  7.2 3.5 copy-start
  7.2 88.4 %all-gather.13.cloned.1.call-start = ((), (), s32[]{:S(2)}) async-start(), calls=%async_computation.2 | async-start | bytes 7454720 | tf_op jit(solution)/shard_map/all_gather | solution.py:69
  7.9 169.0 %all-gather.11.cloned.1.call-start = ((), (), s32[]{:S(2)}) async-start(), calls=%async_computation.1 | async-start | bytes 7454720 | tf_op jit(solution)/shard_map/all_gather | solution.py:68
  8.7 304.8 %all-gather.9.cloned.1.call-start = ((), (), s32[]{:S(2)}) async-start(), calls=%async_computation | async-start | bytes 7454720 | tf_op jit(solution)/shard_map/all_gather | solution.py:67
  9.4 390.9 %all-gather.15.cloned.1.call-start = ((), (), s32[]{:S(2)}) async-start(), calls=%async_computation.4 | async-start | bytes 34078720 | tf_op jit(solution)/shard_map/all_gather | solution.py:13
  12.4 305.4 %copy-start.7 = (bf16[128,128]{0,1:T(8,128)(2,1)}, bf16[128,128]{0,1:T(8,128)(2,1)S(1)}, u32[]{:S(2)}) copy-start(bf16[128,128]{0,1:T(8,128)(2,1)S(1)} %convolution_convert_fusion) | copy-start | bytes 98308
  12.4 87.4 %copy-start.4 = (bf16[2,64,1024]{2,1,0:T(8,128)(2,1)S(1)}, bf16[2,64,1024]{2,1,0:T(8,128)(2,1)}, u32[]{:S(2)}) copy-start(bf16[2,64,1024]{2,1,0:T(8,128)(2,1)} %param.17) | copy-start | bytes 786436
  100.0 82.8 %copy-start.9 = (u32[256]{0:T(256)S(1)}, u32[256]{0:T(256)}, u32[]{:S(2)}) copy-start(u32[256]{0:T(256)} %constant.80) | copy-start | bytes 3076
  100.0 212.0 %copy-start.6 = (bf16[128,1024]{1,0:T(8,128)(2,1)S(1)}, bf16[128,1024]{1,0:T(8,128)(2,1)}, u32[]{:S(2)}) copy-start(bf16[128,1024]{1,0:T(8,128)(2,1)} %param.19) | copy-start | bytes 786436
  181.2 138.9 %copy-start.1 = (bf16[128,1024]{1,0:T(8,128)(2,1)}, bf16[128,1024]{1,0:T(8,128)(2,1)S(1)}, u32[]{:S(2)}) copy-start(bf16[128,1024]{1,0:T(8,128)(2,1)S(1)} %multiply_convert_fusion) | copy-start | bytes 786436
  182.8 479.1 %all-gather.17.cloned.1.call-start = ((), (), s32[]{:S(2)}) async-start(), calls=%async_computation.5 | async-start | bytes 34078720 | tf_op jit(solution)/shard_map/all_gather | solution.py:13
  522.9 543.7 %all-reduce.7.cloned.1.call-start = ((), (), s32[]{:S(2)}) async-start(), calls=%async_computation.6 | async-start | bytes 3670016
  684.9 118.6 %copy-start.2 = (bf16[128,1024]{1,0:T(8,128)(2,1)S(1)}, bf16[128,1024]{1,0:T(8,128)(2,1)}, u32[]{:S(2)}) copy-start(bf16[128,1024]{1,0:T(8,128)(2,1)} %copy-done.1) | copy-start | bytes 786436
  684.9 119.2 %copy-start.3 = (bf16[8,128,128]{2,1,0:T(8,128)(2,1)S(1)}, bf16[8,128,128]{2,1,0:T(8,128)(2,1)}, u32[]{:S(2)}) copy-start(bf16[8,128,128]{2,1,0:T(8,128)(2,1)} %fusion.9) | copy-start | bytes 786436
  684.9 119.4 %copy-start.5 = (bf16[2,64,1024]{2,1,0:T(8,128)(2,1)S(1)}, bf16[2,64,1024]{2,1,0:T(8,128)(2,1)}, u32[]{:S(2)}) copy-start(bf16[2,64,1024]{2,1,0:T(8,128)(2,1)} %param.17) | copy-start | bytes 786436
  684.9 121.9 %copy-start.8 = (bf16[128,128]{0,1:T(8,128)(2,1)S(1)}, bf16[128,128]{0,1:T(8,128)(2,1)}, u32[]{:S(2)}) copy-start(bf16[128,128]{0,1:T(8,128)(2,1)} %copy-done.7) | copy-start | bytes 98308
  806.8 446.2 %all-reduce.5.cloned.1.call-start = ((), (), s32[]{:S(2)}) async-start(), calls=%async_computation.3 | async-start | bytes 1048576 | tf_op jit(solution)/shard_map/psum | solution.py:138
Sparse Core Ops, SparseCore 0:
  10.7 84.7 all-gather.12
  98.3 78.5 all-gather.10
  179.7 78.6 all-gather.8
  261.6 138.6 all-gather.14
  523.1 138.7 all-gather.16
  806.9 259.7 all-reduce.6
  1070.7 182.1 all-reduce.4
where the time goes:
time: 1270 us; the launch traced here: 1260 us
  waiting for transfers between devices  815 us (64%)
  other arithmetic  151 us (12%)
  blocking collectives  127 us (10%)
  local copies, waits for them, and re-layouts  119 us (9%)
  matrix products  30.3 us (2%)
  between operations  15 us (1%)
    unnamed x8, waiting for transfers between devices  260 us
    all_gather x2, waiting for transfers between devices, carried_in(): pieces = jax.tree.map(lambda part: lax.all_gather(part, axis), value)  210 us
    psum x1, waiting for transfers between devices, on_device(): grad_up = lax.psum(up_products, 'seq')  185 us
    select_n x126, other arithmetic, hop(): jnp.where(position < mine, new, old)  147 us
    unnamed x1, blocking collectives  127 us
    mul x126, local copies, waits for them, and re-layouts, combine(): later[0][:, None, None] * earlier[1] + later[1]  86.6 us
    all_gather x1, waiting for transfers between devices, on_device(): lax.all_gather(value_weight, 'seq', axis=0, tiled=True)  83.2 us
    all_gather x1, waiting for transfers between devices, on_device(): lax.all_gather(key_weight, 'seq', axis=0, tiled=True)  76.9 us
  transfers between devices with their start and end apart: 7, of which 6 were waited for; matrix products, arithmetic and copies ran while one was open for 3% of the time, Pallas kernels for 0%

commit v1 on v0

v1 whole, which is shorter than its diff:
```python
import jax
import jax.numpy as jnp
from jax import lax
from jax.experimental import pallas as pl
from jax.experimental.pallas import tpu as pltpu
from jax.sharding import Mesh, PartitionSpec as P

bf16, f32 = jnp.bfloat16, jnp.float32
adapter_scale = 2.0
eps_norm = 1e-06
VMEM = pl.BlockSpec(memory_space=pltpu.VMEM)
SMEM = pl.BlockSpec(memory_space=pltpu.SMEM)
ANY = pl.BlockSpec(memory_space=pl.ANY)


def dot(a, b):
    return jnp.dot(a, b, preferred_element_type=f32)


def dot_t(a, b):
    return lax.dot_general(a, b, (((1,), (1,)), ((), ())), preferred_element_type=f32)


def t_dot(a, b):
    return lax.dot_general(a, b, (((0,), (0,)), ((), ())), preferred_element_type=f32)


def shape(dims, dtype=bf16):
    return jax.ShapeDtypeStruct(dims, dtype)


def call(kernel, outs, *args, mib=6, specs=None, scratch=()):
    return pl.pallas_call(
        kernel,
        out_shape=outs,
        in_specs=specs or [VMEM] * len(args),
        out_specs=jax.tree.map(lambda _: VMEM, outs),
        scratch_shapes=scratch,
        compiler_params=pltpu.CompilerParams(vmem_limit_bytes=mib << 20),
    )(*args)


def pack_kernel(a, b, c, grad, decay, out):
    d = decay[...]
    hi = d.astype(bf16).astype(f32)
    mid = (d - hi).astype(bf16).astype(f32)
    lo = (d - hi - mid).astype(bf16).astype(f32)
    zero = jnp.zeros((13, 128), f32)
    for h in range(out.shape[0]):
        lanes = slice(h * 128, h * 128 + 128)
        out[h, 0:48, 0:128] = grad[0:48, lanes]
        out[h, 0:48, 128:256] = grad[48:96, lanes]
        out[h, 0:32, 256:384] = grad[96:128, lanes]
        logs = jnp.concatenate([hi[h : h + 1], mid[h : h + 1], lo[h : h + 1], zero], axis=0)
        out[h, 32:48, 256:384] = logs.astype(bf16)
        for i, m in enumerate((a, b, c)):
            out[h, 48:, i * 128 : (i + 1) * 128] = m[:, lanes]


def project_kernel(ids, w_all, down, *rest):
    pieces, rest = rest[:10], rest[10:]
    lift, tail, extra, k_ref, v_ref, q_ref, qpre_ref, low_ref, tok, send_ref, wbuf, sems = rest
    ny, nz, deep, wide = wbuf.shape
    y, c = ids[0], ids[1]
    width = tok.shape[2]
    copies = []
    for i in range(ny):
        copies.append((w_all.at[:, i * deep : (i + 1) * deep, :], wbuf.at[i, :, :, : wide - 128]))
    copies.append((down, wbuf.at[:, :, :, wide - 128 :]))
    half = tok.shape[1] // 2
    for i, p in enumerate(pieces):
        rel = (0, 0, ny - 1, ny - 1, 1, 1, 2, 2, 2, 2)[i]
        core = c if i % 2 == 0 else 1 - c
        dst = tok.at[lax.rem(y + rel, ny) * 2 + core]
        if i >= 6:
            dst = dst.at[half * ((i - 6) // 2) : half * ((i - 6) // 2) + half]
        copies.append((p, dst))
    copies = [pltpu.make_async_copy(s, d, sems.at[i]) for i, (s, d) in enumerate(copies)]
    for copy in copies:
        copy.start()
    for i in range(ny + 1):
        copies[i].wait()
    send_ref[:, 96:112, :] = jnp.broadcast_to(extra[...][None], (send_ref.shape[0], 16, 128))
    for rel, used in ((0, (0, 1)), (ny - 1, (2, 3)), (1, (4, 5)), (2, (6, 7, 8, 9))):
        for i in used:
            copies[ny + 1 + i].wait()
        n = lax.rem(y + rel, ny)
        rows = pl.ds(pl.multiple_of(n * 256, 256), 256)
        x = tok[pl.ds(n * 2, 2)].reshape(256, width)
        w = wbuf[...].reshape(width, wide)
        acc = dot(x, w)
        low = acc[:, 384:].astype(bf16)
        low_ref[rows, :] = low
        u = acc[:, :128]
        k = (u * jax.nn.sigmoid(u)).astype(bf16)
        v = (acc[:, 128:256] + adapter_scale * dot(low, lift[1])).astype(bf16)
        u = acc[:, 256:384] + adapter_scale * dot(low, lift[0])
        k_ref[rows, :] = k
        v_ref[rows, :] = v
        qpre_ref[rows, :] = u
        q_ref[rows, :] = (u * jax.nn.sigmoid(u)).astype(bf16)
        faded = (k.astype(f32) * tail[rows, :]).astype(bf16)
        local = t_dot(faded, v).astype(bf16).reshape(-1, 16, 128)
        send_ref[:, pl.ds(pl.multiple_of(n * 16, 16), 16), :] = local
        side = t_dot(low, faded)[64:].reshape(-1, 8, 128)
        send_ref[:, pl.ds(pl.multiple_of(64 + n * 8, 8), 8), :] = side.astype(bf16)


def intra_kernel(q, k, v, dec, mixed, attn):
    for n in range(dec.shape[0]):
        rows = slice(n * 256, n * 256 + 256)
        m = (dot_t(q[rows, :], k[rows, :]) * dec[n]).astype(bf16)
        mixed[n] = m
        attn[rows, :] = dot(m, v[rows, :])


def scan_fwd_kernel(got, out, gains):
    nz, ny = got.shape[0], 4
    logs = got[:, 96:112, :].astype(f32)
    state = jnp.zeros((16, 128), f32)
    side = jnp.zeros((8, 128), f32)
    for y in range(ny):
        for z in range(nz):
            total = logs[z, 3 * y] + (logs[z, 3 * y + 1] + logs[z, 3 * y + 2])
            gain = jnp.exp(total)[None]
            gains[y * nz + z] = gain[0]
            out[z, 16 * y : 16 * y + 16, :] = state.astype(bf16)
            out[z, 64 + 8 * y : 72 + 8 * y, :] = side.astype(bf16)
            state = gain * state + got[z, 16 * y : 16 * y + 16, :].astype(f32)
            side = gain * side + got[z, 64 + 8 * y : 72 + 8 * y, :].astype(f32)


def scan_bwd_kernel(got, gains, out):
    nz, ny = got.shape[0], 4
    state = jnp.zeros((16, 128), f32)
    for y in reversed(range(ny)):
        for z in reversed(range(nz)):
            out[z, 16 * y : 16 * y + 16, :] = state.astype(bf16)
            state = gains[y * nz + z][None] * state + got[z, 16 * y : 16 * y + 16, :].astype(f32)
    up = jnp.sum(got[:, 64:80, :].astype(f32), axis=0).astype(bf16)
    out[:, 64:80, :] = jnp.broadcast_to(up[None], (nz, 16, 128))


def attn_kernel(q, k, v, qpre, low, mixed, attn_in, s_in, lead, bundle, dec, lift, send, dlow, dv):
    total_q = jnp.zeros((128, 128), f32)
    total_v = jnp.zeros((128, 128), f32)
    cross = jnp.zeros((64, 128), f32)
    for n in range(dec.shape[0]):
        rows = slice(n * 256, n * 256 + 256)
        s = s_in[:, n * 16 : n * 16 + 16, :].reshape(128, 128)
        side = s_in[:, 64 + n * 8 : 72 + n * 8, :].astype(f32).reshape(64, 128).astype(bf16)
        qn, vn, ln = q[rows, :], v[rows, :], low[rows, :]
        ahead = lead[rows, :]
        attn = attn_in[rows, :] + ahead * dot(qn, s)
        inv = lax.rsqrt(jnp.mean(attn * attn, axis=-1, keepdims=True) + eps_norm)
        normed = attn * inv
        parts = []
        for b in (2 * n, 2 * n + 1):
            parts += [bundle[b, 0:48, 0:128], bundle[b, 0:48, 128:256], bundle[b, 0:32, 256:384]]
        up = jnp.concatenate(parts, axis=0).astype(f32)
        d = (up - normed * jnp.mean(up * normed, axis=-1, keepdims=True)) * inv
        d = d.astype(bf16)
        carried = t_dot((qn.astype(f32) * ahead).astype(bf16), d).astype(bf16)
        send[:, n * 16 : n * 16 + 16, :] = carried.reshape(-1, 16, 128)
        cross += dot(side, carried)
        dm = (dot_t(d, vn) * dec[n]).astype(bf16)
        dq = dot(dm, k[rows, :]) + ahead * dot_t(d, s)
        u = qpre[rows, :]
        sig = jax.nn.sigmoid(u)
        dq = (dq * (sig * (1.0 + u * (1.0 - sig)))).astype(bf16)
        dlow[rows, :] = adapter_scale * dot_t(dq, lift[0])
        total_q += t_dot(ln, dq)
        dvn = t_dot(mixed[n], d)
        dv[rows, :] = dvn
        total_v += t_dot(ln, dvn.astype(bf16))
    up = adapter_scale * jnp.concatenate([total_q[:64], total_v[64:] + cross], axis=0)
    send[:, 64:80, :] = up.astype(bf16).reshape(-1, 16, 128)


def final_kernel(ids, dv, k, r_in, tail, lift, dlow_q, tok, keep, give, dlow, terms):
    for n in range(4):
        rows = slice(n * 256, n * 256 + 256)
        r = r_in[:, n * 16 : n * 16 + 16, :].reshape(128, 128)
        d = (dv[rows, :] + tail[rows, :] * dot(k[rows, :], r)).astype(bf16)
        dlow[rows, :] = (dlow_q[rows, :] + adapter_scale * dot_t(d, lift[1])).astype(bf16)
    small = dlow[...].astype(f32).T.astype(bf16)
    wide = 512
    tokens = tok.shape[0] * tok.shape[1]
    for m in range(0, tok.shape[2], wide):
        x = tok[:, :, m : m + wide].reshape(tokens, wide)
        terms[m : m + wide, :] = dot(small, x).T
    per = keep.shape[1] // 8
    first = ids[1] == 0
    for b in range(16):
        y, x = b // 4, b % 4
        halves = []
        for c in range(2):
            base = ((y * 16 + c) * 4 + x) * per
            rows = [terms[pl.ds(base + r, 8, stride=8 * per), :] for r in range(per)]
            halves.append(jnp.concatenate(rows, axis=0))
        keep[b] = jnp.where(first, halves[0], halves[1])
        give[b] = jnp.where(first, halves[1], halves[0]).astype(bf16)


def add_kernel(a, b, out):
    out[...] = (a[...] + b[...].astype(f32)).astype(bf16)


def fold_kernel(got, out, tmp):
    tmp[...] = jnp.sum(got[...].astype(f32), axis=0)
    nz = out.shape[0]
    per = tmp.shape[0] // nz
    for z in range(nz):
        out[z] = jnp.concatenate(
            [tmp[pl.ds(z, per, stride=nz), :], jnp.zeros((out.shape[1] - per, 128), f32)], axis=0
        ).astype(bf16)


def last_kernel(got, out):
    out[...] = jnp.sum(got[...].astype(f32), axis=0)[: out.shape[0]]


def up_kernel(ids, own, other, *rest):
    pieces, out = rest[:-1], rest[-1]
    y, c = ids[0], ids[1]

    def put(yy, cc, val):
        out[:, pl.ds(pl.multiple_of((yy * 2 + cc) * 128, 128), 128)] = val.astype(f32)

    put(y, c, own[...])
    put(y, 1 - c, other[...])
    for i, rel in enumerate((3, 1, 2)):
        yy = lax.rem(y + rel, 4)
        put(yy, c, pieces[i][0])
        put(yy, 1 - c, pieces[i][1])


def on_device(tokens, wq, wk, wv, down, lift, decay, grad):
    own, width = tokens.shape
    rank = lift.shape[1]
    heads = decay.shape[0]
    hk = wq.shape[1] // heads
    group = ("y", "c")
    ny, nz, nc, nx = (lax.axis_size(a) for a in ("y", "z", "c", "x"))
    ids = jnp.stack([lax.axis_index("y"), lax.axis_index("c")]).astype(jnp.int32)
    head = lax.axis_index("y") * nc + lax.axis_index("c")
    rows = wq.shape[0]
    span = nc * own
    count = ny * span
    ring = lambda v, s: lax.ppermute(v, "y", [(i, (i + s) % ny) for i in range(ny)])
    swap = lambda v: lax.ppermute(v, "c", [(0, 1), (1, 0)])

    below, above = ring(tokens, 1), ring(tokens, -1)
    far0, far1 = ring(below[: own // 2], 1), ring(above[own // 2 :], -1)
    pieces = []
    for p in (tokens, below, above, far0, far1):
        pieces += [p, swap(p)]

    bundle = call(
        pack_kernel, shape((heads, 48 + rows, 3 * hk)), wk, wv, wq, grad, decay
    )
    bundle = lax.all_to_all(bundle, group, 0, 0, tiled=True)
    w = bundle[:, 48:].reshape(heads * rows, 3 * hk)
    w = lax.all_gather(w, "z")

    logs = bundle[:, 32:35, 2 * hk :].astype(f32)
    logs = (logs[:, 0] + (logs[:, 1] + logs[:, 2])).reshape(ny, span)
    lift = lax.dynamic_slice_in_dim(lift, head * hk, hk, 2)
    zero = jnp.zeros((rank, hk), bf16)
    lift = jnp.stack([jnp.concatenate([lift[0], zero]), jnp.concatenate([zero, lift[1]])])
    cum = jnp.cumsum(logs, axis=1)
    total = cum[:, -1]
    wide = lambda a: jnp.broadcast_to(a.reshape(count, 1), (count, hk))
    lead = wide(jnp.exp(cum))
    tail = wide(jnp.exp(total[:, None] - cum))
    causal = (jnp.arange(span)[:, None] >= jnp.arange(span)[None, :])[None]
    dec = jnp.where(causal, jnp.exp(jnp.where(causal, cum[:, :, None] - cum[:, None, :], 0.0)), 0.0)
    extra = jnp.stack(split3(total), axis=1).reshape(3 * ny, 1)
    extra = jnp.broadcast_to(jnp.pad(extra, ((0, 16 - 3 * ny), (0, 0))), (16, hk))

    deep = nc * rows
    k, v, q, qpre, low, tok, send = call(
        project_kernel,
        (
            shape((count, hk)), shape((count, hk)), shape((count, hk)), shape((count, hk), f32),
            shape((count, hk)), shape((heads, own, width)), shape((nz, 112, hk)),
        ),
        ids, w, down.reshape(ny, nz, deep, 2 * rank), *pieces, lift, tail, extra,
        mib=20,
        specs=[SMEM] + [ANY] * 12 + [VMEM] * 3,
        scratch=[
            pltpu.VMEM((ny, nz, deep, 3 * hk + 2 * rank), bf16),
            pltpu.SemaphoreType.DMA((ny + 11,)),
        ],
    )

    got = lax.all_to_all(send, "z", 0, 0, tiled=True)
    mixed, attn_in = call(intra_kernel, (shape((ny, span, span)), shape((count, hk), f32)), q, k, v, dec)
    back, gains = call(scan_fwd_kernel, (shape((nz, 96, hk)), shape((nz * ny, hk), f32)), got)
    s_in = lax.all_to_all(back, "z", 0, 0, tiled=True)

    send, dlow_q, dv = call(
        attn_kernel,
        (shape((nz, 80, hk)), shape((count, 2 * rank), f32), shape((count, hk), f32)),
        q, k, v, qpre, low, mixed, attn_in, s_in, lead, bundle, dec, lift,
    )
    got = lax.all_to_all(send, "z", 0, 0, tiled=True)
    back = call(scan_bwd_kernel, shape((nz, 80, hk)), got, gains)
    r_in = lax.all_to_all(back, "z", 0, 0, tiled=True)

    up = r_in[:, 64:80].reshape(2 * rank, hk)
    up_other = swap(up)
    pair = jnp.stack([up, up_other])
    ups = [ring(pair, 1), ring(pair, -1), ring(pair, 2)]

    out_rows = width // (ny * nz * nc * nx)
    keep, give = call(
        final_kernel,
        (shape((ny * nx, nz * out_rows, hk), f32), shape((ny * nx, nz * out_rows, hk))),
        ids, dv, k, r_in, tail, lift, dlow_q, tok,
        specs=[SMEM] + [VMEM] * 7,
        scratch=[pltpu.VMEM((count, 2 * rank), bf16), pltpu.VMEM((width, 2 * rank), f32)],
        mib=12,
    )
    down_terms = call(add_kernel, shape(give.shape), keep, swap(give))
    down_terms = lax.all_to_all(down_terms, ("y", "x"), 0, 0, tiled=True)
    down_terms = call(
        fold_kernel, shape((nz, 16, hk)), down_terms,
        scratch=[pltpu.VMEM((nz * out_rows, hk), f32)],
    )
    down_terms = lax.all_to_all(down_terms, "z", 0, 0, tiled=True)
    grad_down = call(last_kernel, shape((out_rows, hk), f32), down_terms)
    grad_up = call(
        up_kernel, shape((2 * rank, heads * hk), f32), ids, up, up_other, *ups,
        specs=[SMEM] + [VMEM] * 5,
    )
    return (grad_down, grad_up.reshape(2, rank, heads * hk))


def split3(v):
    hi = lax.reduce_precision(v, 8, 7)
    mid = lax.reduce_precision(v - hi, 8, 7)
    lo = lax.reduce_precision(v - hi - mid, 8, 7)
    return hi.astype(bf16), mid.astype(bf16), lo.astype(bf16)


def solution(mesh):
    n_mp = mesh.shape["mp"]
    wide = Mesh(mesh.devices.reshape(4, 8, 2, n_mp), ("y", "z", "c", "x"))
    seq = ("y", "z", "c")
    return jax.shard_map(
        on_device,
        mesh=wide,
        in_specs=(
            P(seq, None),
            P(seq, "x"),
            P(seq, "x"),
            P(seq, "x"),
            P(),
            P(None, None, "x"),
            P("x", seq),
            P(seq, "x"),
        ),
        out_specs=(P(("y", "z", "c", "x"), None), P(None, None, "x")),
        check_vma=False,
    )
```

time: 1270 us -> 203 us (0.16)
  waiting for transfers between devices: 815 us -> 47.1 us
  other arithmetic: 151 us -> 2.07 us
  local copies, waits for them, and re-layouts: 119 us -> 34.9 us
  blocking collectives: 127 us -> 56.1 us
  matrix products: 30.3 us -> 0 us
  starting transfers between devices: 0.46 us -> 27.8 us
  Pallas kernels: 0 us -> 19.2 us
    all_gather x5 -> x1, waiting for transfers between devices: 370 us -> 3.09 us  [on_device(): w = lax.all_gather(w, 'z')]
    unnamed x8 -> x1, waiting for transfers between devices: 260 us -> 0.02 us
    psum x1 -> x0, waiting for transfers between devices: 185 us -> none  [on_device(): grad_up = lax.psum(up_products, 'seq')]
    select_n x126 -> x1, other arithmetic: 147 us -> 0.25 us  [on_device(): jnp.where(causal, jnp.exp(jnp.where(causal, cum[:, :, None] - cum[:, None...]
    unnamed x1 -> x0, blocking collectives: 127 us -> none
    mul x126 -> x0, local copies, waits for them, and re-layouts: 86.6 us -> none  [combine(): later[0][:, None, None] * earlier[1] + later[1]]
    all_to_all x0 -> x4, blocking collectives: none -> 56.1 us  [the longest x2 28.4 us: on_device(): got = lax.all_to_all(send, 'z', 0, 0, tiled=True)]
    dot_general x20 -> x0, matrix products: 30.3 us -> none  [the longest x3 12.7 us: on_device(): jnp.dot(columns, piece, preferred_element_type=jnp.float32)]
  transfers between devices with their start and end apart: 7 -> 18, of which waited for: 6 -> 10; matrix products, arithmetic and copies ran while one was open for 3% -> 2% of each run, Pallas kernels for 0% -> 1%
where the time goes in v1:
time: 203 us; the launch traced here: 201 us
  blocking collectives  56.1 us (28%)
  waiting for transfers between devices  47.1 us (23%)
  local copies, waits for them, and re-layouts  34.9 us (17%)
  starting transfers between devices  27.8 us (14%)
  Pallas kernels  19.2 us (9%)
  between operations  14.3 us (7%)
  other arithmetic  2.07 us (1%)
    unnamed x61, local copies, waits for them, and re-layouts  31 us
    all_to_all x2, blocking collectives, on_device(): got = lax.all_to_all(send, 'z', 0, 0, tiled=True)  28.4 us
    ppermute x7, waiting for transfers between devices, on_device(): lax.ppermute(v, 'y', [(i, (i + s) % ny) for i in range(ny)])  25.5 us
    pallas_call x11, Pallas kernels, call(): pl.pallas_call(kernel, out_shape=outs, in_specs=specs or [VMEM] * len(arg...  19.2 us
    all_to_all x1, blocking collectives, on_device(): bundle = lax.all_to_all(bundle, group, 0, 0, tiled=True)  15.9 us
    all_to_all x1, blocking collectives, on_device(): r_in = lax.all_to_all(back, 'z', 0, 0, tiled=True)  11.8 us
    ppermute x7, starting transfers between devices, on_device(): lax.ppermute(v, 'y', [(i, (i + s) % ny) for i in range(ny)])  11.6 us
    all_to_all x1, starting transfers between devices, on_device(): down_terms = lax.all_to_all(down_terms, ('y', 'x'), 0, 0, tiled=True)  8.12 us
  transfers between devices with their start and end apart: 18, of which 10 were waited for; matrix products, arithmetic and copies ran while one was open for 2% of the time, Pallas kernels for 1%

profile of v1, /device:TPU:2, one launch (start us, length us, event | category | flops | bytes accessed | tf_op | source)
XLA Modules:
  0.0 201.4 jit_solution(13571646413230191950)
XLA Ops:
  11.7 15.9 %all_to_all.35.bundle = bf16[8,104,384]{2,1,0:T(8,128)(2,1)S(1)} all-to-all(bf16[8,104,384]{2,1,0:T(8,128)(2,1)S(1)} %shard_map.95), channel_id=1, replica_groups=mesh['y'=4,'z'=8,'c'=2,'x'=4] {'y','c'}, dimensions={0} | all-to-all | bytes 1277952 | tf_op jit(solution)/shard_map/all_to_all | solution.py:262
  28.9 2.7 %collective-permute-start.3 = (bf16[128,3584]{1,0:T(8,128)(2,1)}, bf16[128,3584]{1,0:T(8,128)(2,1)S(1)}, u32[]{:S(2)}, u32[]{:S(2)}) collective-permute-start(bf16[128,3584]{1,0:T(8,128)(2,1)} %rest_0_.1), channel_id=1, source_target_pairs={{0,192},{64,0},{128,64},{192,128},{1,193},{65,1},{129,65},{193,129... | collective-permute-start | bytes 2752520 | tf_op jit(solution)/shard_map/ppermute | solution.py:250
  32.5 1.2 reduce-window.6
  34.1 17.6 %collective-permute-done.1.rest_2_ = bf16[128,3584]{1,0:T(8,128)(2,1)S(1)} collective-permute-done((bf16[128,3584]{1,0:T(8,128)(2,1)}, bf16[128,3584]{1,0:T(8,128)(2,1)S(1)}, u32[]{:S(2)}, u32[]{:S(2)}) %collective-permute-start.1) | collective-permute-done | bytes 917536 | tf_op jit(solution)/shard_map/ppermute | solution.py:250
  53.4 3.2 %collective-permute-start.7 = (bf16[64,3584]{1,0:T(8,128)(2,1)}, bf16[64,3584]{1,0:T(8,128)(2,1)}, u32[]{:S(2)}, u32[]{:S(2)}) collective-permute-start(bf16[64,3584]{1,0:T(8,128)(2,1)} %slice.54), channel_id=1, source_target_pairs={{0,192},{64,0},{128,64},{192,128},{1,193},{65,1},{129,65},{193,129... | collective-permute-start | bytes 1376264 | tf_op jit(solution)/shard_map/ppermute | solution.py:250
  57.5 7.8 %collective-permute-done.5.rest_6_ = bf16[64,3584]{1,0:T(8,128)(2,1)} collective-permute-done((bf16[64,3584]{1,0:T(8,128)(2,1)}, bf16[64,3584]{1,0:T(8,128)(2,1)}, u32[]{:S(2)}, u32[]{:S(2)}) %collective-permute-start.5) | collective-permute-done | bytes 458784 | tf_op jit(solution)/shard_map/ppermute | solution.py:250
  68.9 3.1 %all-gather.2.cloned.1.call-done.w_all = bf16[8,448,384]{2,1,0:T(8,128)(2,1)} async-done(((bf16[1,448,384]{2,1,0:T(8,128)(2,1)}), bf16[8,448,384]{2,1,0:T(8,128)(2,1)}) %all-gather.2.cloned.1.call-update) | async-done | bytes 2752528 | tf_op jit(solution)/shard_map/all_gather | solution.py:264
  72.3 1.8 copy-done.2
  74.1 1.2 copy-done.8
  75.2 1.2 copy-done.9
  76.4 1.2 copy-done.11
  79.6 8.3 %shard_map.96 = (bf16[1024,128]{1,0:T(8,128)(2,1)S(1)}, bf16[1024,128]{1,0:T(8,128)(2,1)S(1)}, bf16[1024,128]{1,0:T(8,128)(2,1)S(1)}, f32[1024,128]{1,0:T(8,128)...) custom-call(s32[2]{0:T(128)S(1)} %pad_add_fusion.ids, ...), custom_call_target="tpu_custom_call" | custom-call | tf_op jit(solution)/shard_map/pallas_call | solution.py:33
  87.9 2.9 %copy-done = bf16[8,128,3584]{2,1,0:T(8,128)(2,1)} copy-done((bf16[8,128,3584]{2,1,0:T(8,128)(2,1)}, bf16[8,128,3584]{2,1,0:T(8,128)(2,1)S(1)}, u32[]{:S(2)}) %copy-start) | copy-done | bytes 7340056
  93.0 16.6 %all_to_all.36.got = bf16[8,112,128]{2,1,0:T(8,128)(2,1)S(1)} all-to-all(bf16[8,112,128]{2,1,0:T(8,128)(2,1)S(1)} %get-tuple-element.25), channel_id=1, replica_groups=mesh['y'=4,'z'=8,'c'=2,'x'=4] {'z'}, dimensions={0} | all-to-all | bytes 458752 | tf_op jit(solution)/shard_map/all_to_all | solution.py:297
  110.3 3.6 %all-to-all-start.2 = ((bf16[8,96,128]{2,1,0:T(8,128)(2,1)}), bf16[8,96,128]{2,1,0:T(8,128)(2,1)S(1)}, u32[]{:S(2)}, u32[]{:S(2)}) async-start(bf16[8,96,128]{2,1,0:T(8,128)(2,1)} %get-tuple-element.26), calls=%async_computation.2 | async-start | bytes 393216 | tf_op jit(solution)/shard_map/all_to_all | solution.py:300
  118.5 5.0 %all-to-all-done.2.s_in = bf16[8,96,128]{2,1,0:T(8,128)(2,1)S(1)} async-done(((bf16[8,96,128]{2,1,0:T(8,128)(2,1)}), bf16[8,96,128]{2,1,0:T(8,128)(2,1)S(1)}, u32[]{:S(2)}, u32[]{:S(2)}) %all-to-all-start.2) | async-done | bytes 196640 | tf_op jit(solution)/shard_map/all_to_all | solution.py:300
  124.6 1.0 copy-done.13
  128.7 3.1 %shard_map.99 = (bf16[8,80,128]{2,1,0:T(8,128)(2,1)S(1)}, f32[1024,128]{1,0:T(8,128)S(1)}, f32[1024,128]{1,0:T(8,128)S(1)}) custom-call(bf16[1024,128]{1,0:T(8,128)(2,1)S(1)} %copy-done.7, bf16[1024,128]{1,0:T(8,128)(2,1)S(1)} %get-tuple-element.19.k, bf16[1024,128]{1,0:T(8,128)(2,1)S(1)} %copy-done.5, f32[1024,128]{1,0:T(8,128)S(1)} %copy-done.13, ...), custom_call_target="tpu_custom_call" | custom-call | tf_op jit(solution)/shard_map/pallas_call | solution.py:33
  131.7 11.8 %all_to_all.37.got = bf16[8,80,128]{2,1,0:T(8,128)(2,1)S(1)} all-to-all(bf16[8,80,128]{2,1,0:T(8,128)(2,1)S(1)} %get-tuple-element.28), channel_id=1, replica_groups=mesh['y'=4,'z'=8,'c'=2,'x'=4] {'z'}, dimensions={0} | all-to-all | bytes 327680 | tf_op jit(solution)/shard_map/all_to_all | solution.py:307
  143.6 11.8 %all_to_all.38.r_in = bf16[8,80,128]{2,1,0:T(8,128)(2,1)S(1)} all-to-all(bf16[8,80,128]{2,1,0:T(8,128)(2,1)S(1)} %shard_map.100), channel_id=1, replica_groups=mesh['y'=4,'z'=8,'c'=2,'x'=4] {'z'}, dimensions={0} | all-to-all | bytes 327680 | tf_op jit(solution)/shard_map/all_to_all | solution.py:309
  155.4 3.1 %copy-done.1 = bf16[8,128,3584]{2,1,0:T(8,128)(2,1)S(1)} copy-done((bf16[8,128,3584]{2,1,0:T(8,128)(2,1)S(1)}, bf16[8,128,3584]{2,1,0:T(8,128)(2,1)}, u32[]{:S(2)}) %copy-start.1) | copy-done | bytes 7340056
  158.5 2.7 %shard_map.101 = (f32[16,112,128]{2,1,0:T(8,128)S(1)}, bf16[16,112,128]{2,1,0:T(8,128)(2,1)S(1)}) custom-call(s32[2]{0:T(128)S(1)} %pad_add_fusion.ids, f32[1024,128]{1,0:T(8,128)S(1)} %get-tuple-element.27.dv, bf16[1024,128]{1,0:T(8,128)(2,1)S(1)} %get-tuple-element.19.k, bf16[8,80,128]{2,1,0:T(8,128)(2,1)S(1)} %all_to_all.38.r_in, ...), custom_call_target="tpu_custom_call" | custom-call | tf_op jit(solution)/shard_map/pallas_call | solution.py:33
  161.3 1.8 collective-permute-done.9.b
  163.9 8.1 %all-to-all-start.5 = ((bf16[16,112,128]{2,1,0:T(8,128)(2,1)}), bf16[16,112,128]{2,1,0:T(8,128)(2,1)S(1)}, u32[]{:S(2)}, u32[]{:S(2)}) async-start(bf16[16,112,128]{2,1,0:T(8,128)(2,1)} %shard_map.102), calls=%async_computation.5 | async-start | bytes 917504 | tf_op jit(solution)/shard_map/all_to_all | solution.py:326
  172.2 1.2 collective-permute-done.10.other
  173.4 1.5 collective-permute-start.11
  174.9 1.8 collective-permute-start.12
  176.7 1.8 collective-permute-start.13
  178.4 3.5 %all-to-all-done.5.got = bf16[16,112,128]{2,1,0:T(8,128)(2,1)S(1)} async-done(((bf16[16,112,128]{2,1,0:T(8,128)(2,1)}), bf16[16,112,128]{2,1,0:T(8,128)(2,1)S(1)}, u32[]{:S(2)}, u32[]{:S(2)}) %all-to-all-start.5) | async-done | bytes 458784 | tf_op jit(solution)/shard_map/all_to_all | solution.py:326
  182.6 3.3 %all-to-all-start.6 = ((bf16[8,16,128]{2,1,0:T(8,128)(2,1)}), bf16[8,16,128]{2,1,0:T(8,128)(2,1)S(1)}, u32[]{:S(2)}, u32[]{:S(2)}) async-start(bf16[8,16,128]{2,1,0:T(8,128)(2,1)} %shard_map.103), calls=%async_computation.6 | async-start | bytes 65536 | tf_op jit(solution)/shard_map/all_to_all | solution.py:331
  186.0 1.4 shard_map.105
  187.4 6.5 %all-to-all-done.6.got = bf16[8,16,128]{2,1,0:T(8,128)(2,1)S(1)} async-done(((bf16[8,16,128]{2,1,0:T(8,128)(2,1)}), bf16[8,16,128]{2,1,0:T(8,128)(2,1)S(1)}, u32[]{:S(2)}, u32[]{:S(2)}) %all-to-all-start.6) | async-done | bytes 32800 | tf_op jit(solution)/shard_map/all_to_all | solution.py:331
  (110 shorter events, 29.6 us)
Async XLA Ops:
  7.2 64.8 %all-gather.2.cloned.1.call-start = ((), (), s32[]{:S(2)}) async-start(), calls=%async_computation.7 | async-start | bytes 3096576 | tf_op jit(solution)/shard_map/all_gather | solution.py:264
  28.3 23.4 %collective-permute-start.1 = (bf16[128,3584]{1,0:T(8,128)(2,1)}, bf16[128,3584]{1,0:T(8,128)(2,1)S(1)}, u32[]{:S(2)}, u32[]{:S(2)}) collective-permute-start(bf16[128,3584]{1,0:T(8,128)(2,1)} %rest_0_.1), channel_id=1, source_target_pairs={{0,64},{64,128},{128,192},{192,0},{1,65},{65,129},{129,193},{193,1... | collective-permute-start | bytes 2752520 | tf_op jit(solution)/shard_map/ppermute | solution.py:250
  28.9 23.6 %collective-permute-start.3 = (bf16[128,3584]{1,0:T(8,128)(2,1)}, bf16[128,3584]{1,0:T(8,128)(2,1)S(1)}, u32[]{:S(2)}, u32[]{:S(2)}) collective-permute-start(bf16[128,3584]{1,0:T(8,128)(2,1)} %rest_0_.1), channel_id=1, source_target_pairs={{0,192},{64,0},{128,64},{192,128},{1,193},{65,1},{129,65},{193,129... | collective-permute-start | bytes 2752520 | tf_op jit(solution)/shard_map/ppermute | solution.py:250
  31.6 34.3 %collective-permute-start = (bf16[128,3584]{1,0:T(8,128)(2,1)}, bf16[128,3584]{1,0:T(8,128)(2,1)S(1)}, u32[]{:S(2)}, u32[]{:S(2)}) collective-permute-start(bf16[128,3584]{1,0:T(8,128)(2,1)} %rest_0_.1), channel_id=1, source_target_pairs={{0,4},{4,0},{1,5},{5,1},{2,6},{6,2},{3,7},{7,3},{8,12},{12,8},{9,1... | collective-permute-start | bytes 2752520 | tf_op jit(solution)/shard_map/ppermute | solution.py:251
  52.5 12.8 %collective-permute-start.5 = (bf16[64,3584]{1,0:T(8,128)(2,1)}, bf16[64,3584]{1,0:T(8,128)(2,1)}, u32[]{:S(2)}, u32[]{:S(2)}) collective-permute-start(bf16[64,3584]{1,0:T(8,128)(2,1)} %slice.53), channel_id=1, source_target_pairs={{0,64},{64,128},{128,192},{192,0},{1,65},{65,129},{129,193},{193,1... | collective-permute-start | bytes 1376264 | tf_op jit(solution)/shard_map/ppermute | solution.py:250
  53.4 12.1 %collective-permute-start.7 = (bf16[64,3584]{1,0:T(8,128)(2,1)}, bf16[64,3584]{1,0:T(8,128)(2,1)}, u32[]{:S(2)}, u32[]{:S(2)}) collective-permute-start(bf16[64,3584]{1,0:T(8,128)(2,1)} %slice.54), channel_id=1, source_target_pairs={{0,192},{64,0},{128,64},{192,128},{1,193},{65,1},{129,65},{193,129... | collective-permute-start | bytes 1376264 | tf_op jit(solution)/shard_map/ppermute | solution.py:250
  56.6 12.3 %collective-permute-start.2 = (bf16[128,3584]{1,0:T(8,128)(2,1)S(1)}, bf16[128,3584]{1,0:T(8,128)(2,1)}, u32[]{:S(2)}, u32[]{:S(2)}) collective-permute-start(bf16[128,3584]{1,0:T(8,128)(2,1)S(1)} %collective-permute-done.1.rest_2_), channel_id=1, source_target_pairs={{0,4},{4,0},{1,5},{5,1},{2,6},{6,2},{3,7},{7,3},{8,12},{12,8},{9,1... | collective-permute-start | bytes 2752520 | tf_op jit(solution)/shard_map/ppermute | solution.py:251
  56.6 12.3 %collective-permute-start.4 = (bf16[128,3584]{1,0:T(8,128)(2,1)S(1)}, bf16[128,3584]{1,0:T(8,128)(2,1)}, u32[]{:S(2)}, u32[]{:S(2)}) collective-permute-start(bf16[128,3584]{1,0:T(8,128)(2,1)S(1)} %collective-permute-done.3.rest_4_), channel_id=1, source_target_pairs={{0,4},{4,0},{1,5},{5,1},{2,6},{6,2},{3,7},{7,3},{8,12},{12,8},{9,1... | collective-permute-start | bytes 2752520 | tf_op jit(solution)/shard_map/ppermute | solution.py:251
  65.3 2.0 %collective-permute-start.6 = (bf16[64,3584]{1,0:T(8,128)(2,1)}, bf16[64,3584]{1,0:T(8,128)(2,1)S(1)}, u32[]{:S(2)}, u32[]{:S(2)}) collective-permute-start(bf16[64,3584]{1,0:T(8,128)(2,1)} %collective-permute-done.5.rest_6_), channel_id=1, source_target_pairs={{0,4},{4,0},{1,5},{5,1},{2,6},{6,2},{3,7},{7,3},{8,12},{12,8},{9,1... | collective-permute-start | bytes 1376264 | tf_op jit(solution)/shard_map/ppermute | solution.py:251
  65.5 2.7 %collective-permute-start.8 = (bf16[64,3584]{1,0:T(8,128)(2,1)}, bf16[64,3584]{1,0:T(8,128)(2,1)S(1)}, u32[]{:S(2)}, u32[]{:S(2)}) collective-permute-start(bf16[64,3584]{1,0:T(8,128)(2,1)} %collective-permute-done.7.rest_8_), channel_id=1, source_target_pairs={{0,4},{4,0},{1,5},{5,1},{2,6},{6,2},{3,7},{7,3},{8,12},{12,8},{9,1... | collective-permute-start | bytes 1376264 | tf_op jit(solution)/shard_map/ppermute | solution.py:251
  66.0 1.0 copy-start.10
  72.3 1.8 copy-start.2
  74.1 1.2 copy-start.8
  75.2 1.2 copy-start.9
  76.4 1.2 copy-start.11
  77.6 1.0 copy-start.19
  78.6 1.0 copy-start.21
  87.9 2.9 %copy-start = (bf16[8,128,3584]{2,1,0:T(8,128)(2,1)}, bf16[8,128,3584]{2,1,0:T(8,128)(2,1)S(1)}, u32[]{:S(2)}) copy-start(bf16[8,128,3584]{2,1,0:T(8,128)(2,1)S(1)} %get-tuple-element.31.tok) | copy-start | bytes 22020100
  93.0 17.4 %copy-start.12 = (f32[1024,128]{1,0:T(8,128)}, f32[1024,128]{1,0:T(8,128)S(1)}, u32[]{:S(2)}) copy-start(f32[1024,128]{1,0:T(8,128)S(1)} %get-tuple-element.21.qpre) | copy-start | bytes 1572868
  110.3 13.1 %all-to-all-start.2 = ((bf16[8,96,128]{2,1,0:T(8,128)(2,1)}), bf16[8,96,128]{2,1,0:T(8,128)(2,1)S(1)}, u32[]{:S(2)}, u32[]{:S(2)}) async-start(bf16[8,96,128]{2,1,0:T(8,128)(2,1)} %get-tuple-element.26), calls=%async_computation.2 | async-start | bytes 393216 | tf_op jit(solution)/shard_map/all_to_all | solution.py:300
  123.6 1.0 copy-start.5
  124.6 1.0 copy-start.13
  125.6 1.0 copy-start.15
  126.7 1.0 copy-start.17
  155.4 3.1 %copy-start.1 = (bf16[8,128,3584]{2,1,0:T(8,128)(2,1)S(1)}, bf16[8,128,3584]{2,1,0:T(8,128)(2,1)}, u32[]{:S(2)}) copy-start(bf16[8,128,3584]{2,1,0:T(8,128)(2,1)} %copy-done) | copy-start | bytes 22020100
  161.2 1.9 collective-permute-start.9
  163.9 18.0 %all-to-all-start.5 = ((bf16[16,112,128]{2,1,0:T(8,128)(2,1)}), bf16[16,112,128]{2,1,0:T(8,128)(2,1)S(1)}, u32[]{:S(2)}, u32[]{:S(2)}) async-start(bf16[16,112,128]{2,1,0:T(8,128)(2,1)} %shard_map.102), calls=%async_computation.5 | async-start | bytes 917504 | tf_op jit(solution)/shard_map/all_to_all | solution.py:326
  172.1 1.3 collective-permute-start.10
  173.4 12.6 %collective-permute-start.11 = (bf16[2,128,128]{2,1,0:T(8,128)(2,1)S(1)}, bf16[2,128,128]{2,1,0:T(8,128)(2,1)S(1)}, u32[]{:S(2)}, u32[]{:S(2)}) collective-permute-start(bf16[2,128,128]{2,1,0:T(8,128)(2,1)S(1)} %pad_maximum_fusion.1), channel_id=1, source_target_pairs={{0,64},{64,128},{128,192},{192,0},{1,65},{65,129},{129,193},{193,1... | collective-permute-start | bytes 196616 | tf_op jit(solution)/shard_map/ppermute | solution.py:250
  174.9 11.1 %collective-permute-start.12 = (bf16[2,128,128]{2,1,0:T(8,128)(2,1)S(1)}, bf16[2,128,128]{2,1,0:T(8,128)(2,1)S(1)}, u32[]{:S(2)}, u32[]{:S(2)}) collective-permute-start(bf16[2,128,128]{2,1,0:T(8,128)(2,1)S(1)} %pad_maximum_fusion.1), channel_id=1, source_target_pairs={{0,192},{64,0},{128,64},{192,128},{1,193},{65,1},{129,65},{193,129... | collective-permute-start | bytes 196616 | tf_op jit(solution)/shard_map/ppermute | solution.py:250
  176.7 9.3 %collective-permute-start.13 = (bf16[2,128,128]{2,1,0:T(8,128)(2,1)S(1)}, bf16[2,128,128]{2,1,0:T(8,128)(2,1)S(1)}, u32[]{:S(2)}, u32[]{:S(2)}) collective-permute-start(bf16[2,128,128]{2,1,0:T(8,128)(2,1)S(1)} %pad_maximum_fusion.1), channel_id=1, source_target_pairs={{0,128},{64,192},{128,0},{192,64},{1,129},{65,193},{129,1},{193,65... | collective-permute-start | bytes 196616 | tf_op jit(solution)/shard_map/ppermute | solution.py:250
  182.6 11.3 %all-to-all-start.6 = ((bf16[8,16,128]{2,1,0:T(8,128)(2,1)}), bf16[8,16,128]{2,1,0:T(8,128)(2,1)S(1)}, u32[]{:S(2)}, u32[]{:S(2)}) async-start(bf16[8,16,128]{2,1,0:T(8,128)(2,1)} %shard_map.103), calls=%async_computation.6 | async-start | bytes 65536 | tf_op jit(solution)/shard_map/all_to_all | solution.py:331
  (15 other events, 12.6 us)
Sparse Core Ops, SparseCore 0:
  28.4 43.5 all-gather.1

commit v2 on v1

v2 whole, which is shorter than its diff:
```python
import jax
import jax.numpy as jnp
from jax import lax
from jax.experimental import pallas as pl
from jax.experimental.pallas import tpu as pltpu
from jax.sharding import Mesh, PartitionSpec as P


bf16, f32 = jnp.bfloat16, jnp.float32
adapter_scale = 2.0
eps_norm = 1e-06
VMEM = pl.BlockSpec(memory_space=pltpu.VMEM)
SMEM = pl.BlockSpec(memory_space=pltpu.SMEM)
ANY = pl.BlockSpec(memory_space=pl.ANY)


def dot(a, b):
    return jnp.dot(a, b, preferred_element_type=f32)


def dot_t(a, b):
    return lax.dot_general(a, b, (((1,), (1,)), ((), ())), preferred_element_type=f32)


def t_dot(a, b):
    return lax.dot_general(a, b, (((0,), (0,)), ((), ())), preferred_element_type=f32)


def shape(dims, dtype=bf16):
    return jax.ShapeDtypeStruct(dims, dtype)


HBM = pl.BlockSpec(memory_space=pltpu.MemorySpace.HBM)


def call(kernel, outs, *args, mib=6, specs=None, out_specs=None, scratch=()):
    return pl.pallas_call(
        kernel,
        out_shape=outs,
        in_specs=specs or [VMEM] * len(args),
        out_specs=out_specs or jax.tree.map(lambda _: VMEM, outs),
        scratch_shapes=scratch,
        compiler_params=pltpu.CompilerParams(vmem_limit_bytes=mib << 20),
    )(*args)


def begin(pairs, sems, first=0):
    copies = [pltpu.make_async_copy(s, d, sems.at[first + i]) for i, (s, d) in enumerate(pairs)]
    for copy in copies:
        copy.start()
    return copies


def split3(d):
    hi = d.astype(bf16).astype(f32)
    mid = (d - hi).astype(bf16).astype(f32)
    return hi, mid, (d - hi - mid).astype(bf16).astype(f32)


def running(logs):
    n = logs.shape[1]
    t = lax.broadcasted_iota(jnp.int32, (n, n), 0)
    causal = lax.broadcasted_iota(jnp.int32, (n, n), 1) <= t
    terms = jnp.where(causal, jnp.broadcast_to(logs, (n, n)), 0.0)
    sums = jnp.dot(terms, jnp.ones((n, 128), f32), precision=lax.Precision.HIGHEST)
    return sums, causal


def pack_kernel(a_hbm, b_hbm, c_hbm, grad_hbm, decay_hbm, out, a, b, c, grad, decay, sems):
    src = (decay_hbm, grad_hbm, a_hbm, b_hbm, c_hbm)
    copies = begin(list(zip(src, (decay, grad, a, b, c))), sems)
    for copy in copies:
        copy.wait()
    hi, mid, lo = split3(decay[...])
    zero = jnp.zeros((13, 128), f32)
    for h in range(out.shape[0]):
        lanes = slice(h * 128, h * 128 + 128)
        out[h, 0:48, 0:128] = grad[0:48, lanes]
        out[h, 0:48, 128:256] = grad[48:96, lanes]
        out[h, 0:32, 256:384] = grad[96:128, lanes]
        logs = jnp.concatenate([hi[h : h + 1], mid[h : h + 1], lo[h : h + 1], zero], axis=0)
        out[h, 32:48, 256:384] = logs.astype(bf16)
        for i, m in enumerate((a, b, c)):
            out[h, 48:, i * 128 : (i + 1) * 128] = m[:, lanes]


def project_kernel(ids, down, *rest):
    weights, pieces, rest = rest[:9], rest[9:19], rest[19:]
    lift, logs, kvql_hbm, qpre_hbm, tok_hbm, send, wbuf, tok, kvql, qpre, tail, sems = rest
    ny, nz, _, wide = wbuf.shape
    y, c, z = ids[0], ids[1], ids[2]
    width = tok.shape[2]
    pairs = [(down, wbuf.at[:, :, :, wide - 128 :])]
    for i, p in enumerate(weights):
        shift = (0, -1, 1, -2, 2, -3, 3, 4, 4)[i]
        src = lax.rem(z + shift + nz, nz)
        span = (slice(0, ny), slice(0, ny // 2), slice(ny // 2, ny))[max(0, i - 6)]
        pairs.append((p, wbuf.at[span, src, :, : wide - 128]))
    half = tok.shape[1] // 2
    for i, p in enumerate(pieces):
        rel = (0, 0, ny - 1, ny - 1, 1, 1, 2, 2, 2, 2)[i]
        core = c if i % 2 == 0 else 1 - c
        dst = tok.at[lax.rem(y + rel, ny) * 2 + core]
        if i >= 6:
            dst = dst.at[half * ((i - 6) // 2) : half * ((i - 6) // 2) + half]
        pairs.append((p, dst))
    copies = begin(pairs, sems)
    ends = []
    for n in range(ny):
        sums, _ = running(logs[n : n + 1, :])
        total = sums[255:256, :]
        tail[n] = jnp.exp(total - sums)
        ends += list(split3(total))
    extra = jnp.concatenate(ends + [jnp.zeros((16 - len(ends), 128), f32)], axis=0).astype(bf16)
    send[:, 96:112, :] = jnp.broadcast_to(extra[None], (send.shape[0], 16, 128))
    for i in range(10):
        copies[i].wait()
    stores = []
    for step, (rel, used) in enumerate(
        ((0, (0, 1)), (ny - 1, (2, 3)), (1, (4, 5)), (2, (6, 7, 8, 9)))
    ):
        for i in used:
            copies[10 + i].wait()
        n = lax.rem(y + rel, ny)
        two = pl.ds(n * 2, 2)
        stores += begin([(tok.at[two], tok_hbm.at[two])], sems, 20 + 3 * step)
        acc = dot(tok[two].reshape(256, width), wbuf[...].reshape(width, wide))
        low = acc[:, 384:].astype(bf16)
        u = acc[:, :128]
        k = (u * jax.nn.sigmoid(u)).astype(bf16)
        v = (acc[:, 128:256] + adapter_scale * dot(low, lift[1])).astype(bf16)
        u = acc[:, 256:384] + adapter_scale * dot(low, lift[0])
        q = (u * jax.nn.sigmoid(u)).astype(bf16)
        faded = (k.astype(f32) * tail[n]).astype(bf16)
        local = t_dot(faded, v).astype(bf16).reshape(-1, 16, 128)
        send[:, pl.ds(pl.multiple_of(n * 16, 16), 16), :] = local
        side = t_dot(low, faded)[64:].reshape(-1, 8, 128)
        send[:, pl.ds(pl.multiple_of(64 + n * 8, 8), 8), :] = side.astype(bf16)
        for i, m in enumerate((k, v, q, low)):
            kvql[step, i] = m
        qpre[step] = u
        stores += begin(
            [(kvql.at[step], kvql_hbm.at[n]), (qpre.at[step], qpre_hbm.at[n])], sems, 21 + 3 * step
        )
    for copy in stores:
        copy.wait()


def scan_fwd_kernel(got, out, gains):
    nz, ny = got.shape[0], 4
    logs = got[:, 96:112, :].astype(f32)
    state = jnp.zeros((16, 128), f32)
    side = jnp.zeros((8, 128), f32)
    for y in range(ny):
        for z in range(nz):
            total = logs[z, 3 * y] + (logs[z, 3 * y + 1] + logs[z, 3 * y + 2])
            gain = jnp.exp(total)[None]
            gains[y * nz + z] = gain[0]
            out[z, 16 * y : 16 * y + 16, :] = state.astype(bf16)
            out[z, 64 + 8 * y : 72 + 8 * y, :] = side.astype(bf16)
            state = gain * state + got[z, 16 * y : 16 * y + 16, :].astype(f32)
            side = gain * side + got[z, 64 + 8 * y : 72 + 8 * y, :].astype(f32)


def scan_bwd_kernel(got, gains, out):
    nz, ny = got.shape[0], 4
    state = jnp.zeros((16, 128), f32)
    for y in reversed(range(ny)):
        for z in reversed(range(nz)):
            out[z, 16 * y : 16 * y + 16, :] = state.astype(bf16)
            state = gains[y * nz + z][None] * state + got[z, 16 * y : 16 * y + 16, :].astype(f32)
    up = jnp.sum(got[:, 64:80, :].astype(f32), axis=0).astype(bf16)
    out[:, 64:80, :] = jnp.broadcast_to(up[None], (nz, 16, 128))


def attn_kernel(s_in, lift, logs, kvql_hbm, qpre_hbm, bundle_hbm, send, back_hbm, kvql, qpre, bundle, back, sems):
    ny = kvql.shape[0]
    copies = []
    for n in range(ny):
        copies += begin(
            [
                (kvql_hbm.at[n], kvql.at[n]),
                (qpre_hbm.at[n], qpre.at[n]),
                (bundle_hbm.at[2 * n : 2 * n + 2, 0:48, :], bundle.at[2 * n : 2 * n + 2]),
            ],
            sems,
            3 * n,
        )
    total_q = jnp.zeros((128, 128), f32)
    total_v = jnp.zeros((128, 128), f32)
    cross = jnp.zeros((64, 128), f32)
    stores = []
    for n in range(ny):
        s = s_in[:, n * 16 : n * 16 + 16, :].reshape(128, 128)
        side = s_in[:, 64 + n * 8 : 72 + n * 8, :].astype(f32).reshape(64, 128).astype(bf16)
        sums, causal = running(logs[n : n + 1, :])
        ahead = jnp.exp(sums)
        spread = jnp.concatenate([sums, sums], axis=1) - sums.T[0:1, :]
        dec = jnp.where(causal, jnp.exp(jnp.where(causal, spread, 0.0)), 0.0)
        for copy in copies[3 * n : 3 * n + 3]:
            copy.wait()
        k, v, q, low = (kvql[n, i] for i in range(4))
        mixed = (dot_t(q, k) * dec).astype(bf16)
        attn = dot(mixed, v) + ahead * dot(q, s)
        inv = lax.rsqrt(jnp.mean(attn * attn, axis=-1, keepdims=True) + eps_norm)
        normed = attn * inv
        parts = []
        for b in (2 * n, 2 * n + 1):
            parts += [bundle[b, :, 0:128], bundle[b, :, 128:256], bundle[b, 0:32, 256:384]]
        up = jnp.concatenate(parts, axis=0).astype(f32)
        d = (up - normed * jnp.mean(up * normed, axis=-1, keepdims=True)) * inv
        d = d.astype(bf16)
        carried = t_dot((q.astype(f32) * ahead).astype(bf16), d).astype(bf16)
        send[:, n * 16 : n * 16 + 16, :] = carried.reshape(-1, 16, 128)
        cross += dot(side, carried)
        dm = (dot_t(d, v) * dec).astype(bf16)
        dq = dot(dm, k) + ahead * dot_t(d, s)
        u = qpre[n]
        sig = jax.nn.sigmoid(u)
        dq = (dq * (sig * (1.0 + u * (1.0 - sig)))).astype(bf16)
        total_q += t_dot(low, dq)
        dv = t_dot(mixed, d)
        total_v += t_dot(low, dv.astype(bf16))
        back[n, 0] = dv
        back[n, 1] = adapter_scale * dot_t(dq, lift[0])
        stores += begin([(back.at[n], back_hbm.at[n])], sems, 12 + n)
    up = adapter_scale * jnp.concatenate([total_q[:64], total_v[64:] + cross], axis=0)
    send[:, 64:80, :] = up.astype(bf16).reshape(-1, 16, 128)
    for copy in stores:
        copy.wait()


def final_kernel(ids, r_in, lift, logs, kvql_hbm, back_hbm, tok_hbm, keep, give, k, back, tok, dlow, terms, sems):
    ny = k.shape[0]
    wide = 512
    blocks = tok.shape[2] // wide
    copies = []
    for n in range(ny):
        copies += begin([(kvql_hbm.at[n, 0], k.at[n]), (back_hbm.at[n], back.at[n])], sems, 2 * n)
    lanes = [slice(m * wide, m * wide + wide) for m in range(blocks)]
    parts = begin([(tok_hbm.at[:, :, m], tok.at[:, :, m]) for m in lanes], sems, 2 * ny)
    for n in range(ny):
        rows = slice(n * 256, n * 256 + 256)
        sums, _ = running(logs[n : n + 1, :])
        tail = jnp.exp(sums[255:256, :] - sums)
        r = r_in[:, n * 16 : n * 16 + 16, :].reshape(128, 128)
        copies[2 * n].wait()
        copies[2 * n + 1].wait()
        d = (back[n, 0] + tail * dot(k[n], r)).astype(bf16)
        dlow[rows, :] = back[n, 1] + adapter_scale * dot_t(d, lift[1])
    small = dlow[...].T.astype(bf16)
    tokens = tok.shape[0] * tok.shape[1]
    for m, part in zip(lanes, parts):
        part.wait()
        terms[m, :] = dot(small, tok[:, :, m].reshape(tokens, wide)).T
    per = keep.shape[1] // 8
    first = ids[1] == 0
    for b in range(16):
        y, x = b // 4, b % 4
        halves = []
        for c in range(2):
            base = ((y * 16 + c) * 4 + x) * per
            rows = [terms[pl.ds(base + r, 8, stride=8 * per), :] for r in range(per)]
            halves.append(jnp.concatenate(rows, axis=0))
        keep[b] = jnp.where(first, halves[0], halves[1])
        give[b] = jnp.where(first, halves[1], halves[0]).astype(bf16)


def add_kernel(a, b, out):
    out[...] = (a[...] + b[...].astype(f32)).astype(bf16)


def fold_kernel(got, out, tmp):
    tmp[...] = jnp.sum(got[...].astype(f32), axis=0)
    nz = out.shape[0]
    per = tmp.shape[0] // nz
    for z in range(nz):
        out[z] = jnp.concatenate(
            [tmp[pl.ds(z, per, stride=nz), :], jnp.zeros((out.shape[1] - per, 128), f32)], axis=0
        ).astype(bf16)


def last_kernel(got, out):
    out[...] = jnp.sum(got[...].astype(f32), axis=0)[: out.shape[0]]


def up_kernel(ids, own, other, *rest):
    pieces, out = rest[:-1], rest[-1]
    y, c = ids[0], ids[1]

    def put(yy, cc, val):
        out[:, pl.ds(pl.multiple_of((yy * 2 + cc) * 128, 128), 128)] = val.astype(f32)

    put(y, c, own[...])
    put(y, 1 - c, other[...])
    for i, rel in enumerate((3, 1, 2)):
        yy = lax.rem(y + rel, 4)
        put(yy, c, pieces[i][0])
        put(yy, 1 - c, pieces[i][1])


def layer(tokens, wq, wk, wv, down, lift, decay, grad):
    own, width = tokens.shape
    rank = lift.shape[1]
    heads = decay.shape[0]
    hk = wq.shape[1] // heads
    group = ("y", "c")
    ny, nz, nc, nx = (lax.axis_size(a) for a in ("y", "z", "c", "x"))
    ids = jnp.stack([lax.axis_index(a) for a in ("y", "c", "z")]).astype(jnp.int32)
    head = lax.axis_index("y") * nc + lax.axis_index("c")
    rows = wq.shape[0]
    span = nc * own
    ring = lambda v, s, a="y", n=ny: lax.ppermute(v, a, [(i, (i + s) % n) for i in range(n)])
    swap = lambda v: lax.ppermute(v, "c", [(0, 1), (1, 0)])
    DMA = pltpu.SemaphoreType.DMA

    below = ring(tokens, 1)
    above = ring(tokens, -1)
    far0, far1 = ring(below[: own // 2], 1), ring(above[own // 2 :], -1)
    pieces = []
    for p in (tokens, below, above, far0, far1):
        pieces += [p, swap(p)]

    bundle = call(
        pack_kernel, shape((heads, 48 + rows, 3 * hk)), wk, wv, wq, grad, decay,
        specs=[HBM] * 5,
        mib=60,
        scratch=[pltpu.VMEM(wk.shape, bf16)] * 3
        + [pltpu.VMEM(grad.shape, bf16), pltpu.VMEM(decay.shape, f32), DMA((5,))],
    )
    bundle = lax.all_to_all(bundle, group, 0, 0, tiled=True)
    w = bundle[:, 48:].reshape(heads * rows, 3 * hk)
    weights, ahead, behind = [w], w, w
    for _ in range(nz // 2 - 1):
        ahead, behind = ring(ahead, 1, "z", nz), ring(behind, -1, "z", nz)
        weights += [ahead, behind]
    half = heads * rows // 2
    weights += [ring(ahead[:half], 1, "z", nz), ring(behind[half:], -1, "z", nz)]
    deep = nc * rows
    weights = [p.reshape(-1, deep, 3 * hk) for p in weights]

    logs = bundle[:, 32:35, 2 * hk :].astype(f32)
    logs = (logs[:, 0] + (logs[:, 1] + logs[:, 2])).reshape(ny, span)
    lift = lax.dynamic_slice_in_dim(lift, head * hk, hk, 2)
    zero = jnp.zeros((rank, hk), bf16)
    lift = jnp.stack([jnp.concatenate([lift[0], zero]), jnp.concatenate([zero, lift[1]])])

    kvql, qpre, tok, send = call(
        project_kernel,
        (
            shape((ny, 4, span, hk)), shape((ny, span, hk), f32),
            shape((heads, own, width)), shape((nz, 112, hk)),
        ),
        ids, down.reshape(ny, nz, deep, 2 * rank), *weights, *pieces, lift, logs,
        mib=60,
        specs=[SMEM] + [HBM] * 20 + [VMEM] * 2,
        out_specs=(HBM, HBM, HBM, VMEM),
        scratch=[
            pltpu.VMEM((ny, nz, deep, 3 * hk + 2 * rank), bf16),
            pltpu.VMEM((heads, own, width), bf16),
            pltpu.VMEM((ny, 4, span, hk), bf16),
            pltpu.VMEM((ny, span, hk), f32),
            pltpu.VMEM((ny, span, hk), f32),
            DMA((32,)),
        ],
    )

    got = lax.all_to_all(send, "z", 0, 0, tiled=True)
    scanned, gains = call(scan_fwd_kernel, (shape((nz, 96, hk)), shape((nz * ny, hk), f32)), got)
    s_in = lax.all_to_all(scanned, "z", 0, 0, tiled=True)

    send, back = call(
        attn_kernel,
        (shape((nz, 80, hk)), shape((ny, 2, span, hk), f32)),
        s_in, lift, logs, kvql, qpre, bundle,
        mib=60,
        specs=[VMEM] * 3 + [HBM] * 3,
        out_specs=(VMEM, HBM),
        scratch=[
            pltpu.VMEM((ny, 4, span, hk), bf16),
            pltpu.VMEM((ny, span, hk), f32),
            pltpu.VMEM((heads, 48, 3 * hk), bf16),
            pltpu.VMEM((ny, 2, span, hk), f32),
            DMA((16,)),
        ],
    )
    got = lax.all_to_all(send, "z", 0, 0, tiled=True)
    scanned = call(scan_bwd_kernel, shape((nz, 80, hk)), got, gains)
    r_in = lax.all_to_all(scanned, "z", 0, 0, tiled=True)

    up = r_in[:, 64:80].reshape(2 * rank, hk)
    up_other = swap(up)
    pair = jnp.stack([up, up_other])
    ups = [ring(pair, 1), ring(pair, -1), ring(pair, 2)]

    out_rows = width // (ny * nz * nc * nx)
    keep, give = call(
        final_kernel,
        (shape((ny * nx, nz * out_rows, hk), f32), shape((ny * nx, nz * out_rows, hk))),
        ids, r_in, lift, logs, kvql, back, tok,
        specs=[SMEM] + [VMEM] * 3 + [HBM] * 3,
        scratch=[
            pltpu.VMEM((ny, span, hk), bf16),
            pltpu.VMEM((ny, 2, span, hk), f32),
            pltpu.VMEM((heads, own, width), bf16),
            pltpu.VMEM((heads * own, 2 * rank), f32),
            pltpu.VMEM((width, 2 * rank), f32),
            DMA((16,)),
        ],
        mib=60,
    )
    down_terms = call(add_kernel, shape(give.shape), keep, swap(give))
    down_terms = lax.all_to_all(down_terms, ("y", "x"), 0, 0, tiled=True)
    down_terms = call(
        fold_kernel, shape((nz, 16, hk)), down_terms,
        scratch=[pltpu.VMEM((nz * out_rows, hk), f32)],
    )
    down_terms = lax.all_to_all(down_terms, "z", 0, 0, tiled=True)
    grad_down = call(last_kernel, shape((out_rows, hk), f32), down_terms)
    grad_up = call(
        up_kernel, shape((2 * rank, heads * hk), f32), ids, up, up_other, *ups,
        specs=[SMEM] + [VMEM] * 5,
    )
    return (grad_down, grad_up.reshape(2, rank, heads * hk))


def solution(mesh):
    n_mp = mesh.shape["mp"]
    wide = Mesh(mesh.devices.reshape(4, 8, 2, n_mp), ("y", "z", "c", "x"))
    seq = ("y", "z", "c")
    return jax.shard_map(
        layer,
        mesh=wide,
        in_specs=(
            P(seq, None),
            P(seq, "x"),
            P(seq, "x"),
            P(seq, "x"),
            P(),
            P(None, None, "x"),
            P("x", seq),
            P(seq, "x"),
        ),
        out_specs=(P(("y", "z", "c", "x"), None), P(None, None, "x")),
        check_vma=False,
    )
```

time: 203 us -> 190 us (0.936)
  local copies, waits for them, and re-layouts: 34.9 us -> 7.46 us
  Pallas kernels: 19.2 us -> 35.2 us
  between operations: 14.3 us -> 0.9 us
  starting transfers between devices: 27.8 us -> 38.1 us
  waiting for transfers between devices: 47.1 us -> 54.4 us
  blocking collectives: 56.1 us -> 51.5 us
    unnamed x61 -> x26, local copies, waits for them, and re-layouts: 31 us -> 2.82 us
    pallas_call x11 -> x10, Pallas kernels: 19.2 us -> 35.2 us  [call(): pl.pallas_call(kernel, out_shape=outs, in_specs=specs or [VMEM] * len(arg...]
    ppermute x14 -> x22, starting transfers between devices: 12.7 us -> 25.4 us  [the longest x15 25 us: layer(): lax.ppermute(v, a, [(i, (i + s) % n) for i in range(n)])]
    ppermute x14 -> x22, waiting for transfers between devices: 29 us -> 36.2 us  [the longest x15 33 us: layer(): lax.ppermute(v, a, [(i, (i + s) % n) for i in range(n)])]
    all_to_all x4, blocking collectives: 56.1 us -> 51.5 us  [the longest x2 26.2 us: layer(): got = lax.all_to_all(send, 'z', 0, 0, tiled=True)]
    all_to_all x3, waiting for transfers between devices: 15 us -> 18.2 us  [the longest x1 8.91 us: layer(): bundle = lax.all_to_all(bundle, group, 0, 0, tiled=True)]
    all_gather x1 -> x0, waiting for transfers between devices: 3.09 us -> none  [on_device(): w = lax.all_gather(w, 'z')]
    all_to_all x3, starting transfers between devices: 15 us -> 12.7 us  [the longest x1 4.84 us: layer(): down_terms = lax.all_to_all(down_terms, ('y', 'x'), 0, 0, tiled=True)]
  transfers between devices with their start and end apart: 18 -> 25, of which waited for: 10 -> 13; matrix products, arithmetic and copies ran while one was open for 2% -> 3% of each run, Pallas kernels for 1% -> 1%
where the time goes in v2:
time: 190 us; the launch traced here: 189 us
  waiting for transfers between devices  54.4 us (29%)
  blocking collectives  51.5 us (27%)
  starting transfers between devices  38.1 us (20%)
  Pallas kernels  35.2 us (19%)
  local copies, waits for them, and re-layouts  7.46 us (4%)
    pallas_call x10, Pallas kernels, call(): pl.pallas_call(kernel, out_shape=outs, in_specs=specs or [VMEM] * len(arg...  35.2 us
    ppermute x15, waiting for transfers between devices, layer(): lax.ppermute(v, a, [(i, (i + s) % n) for i in range(n)])  33 us
    all_to_all x2, blocking collectives, layer(): got = lax.all_to_all(send, 'z', 0, 0, tiled=True)  26.2 us
    ppermute x15, starting transfers between devices, layer(): lax.ppermute(v, a, [(i, (i + s) % n) for i in range(n)])  25 us
    all_to_all x1, blocking collectives, layer(): s_in = lax.all_to_all(scanned, 'z', 0, 0, tiled=True)  12.8 us
    all_to_all x1, blocking collectives, layer(): r_in = lax.all_to_all(scanned, 'z', 0, 0, tiled=True)  12.5 us
    all_to_all x1, waiting for transfers between devices, layer(): bundle = lax.all_to_all(bundle, group, 0, 0, tiled=True)  8.91 us
    all_to_all x1, waiting for transfers between devices, layer(): down_terms = lax.all_to_all(down_terms, 'z', 0, 0, tiled=True)  6.51 us
  transfers between devices with their start and end apart: 25, of which 13 were waited for; matrix products, arithmetic and copies ran while one was open for 3% of the time, Pallas kernels for 1%

profile of v2, /device:TPU:2, one launch (start us, length us, event | category | flops | bytes accessed | tf_op | source)
XLA Modules:
  0.0 188.9 jit_solution(10489733655552166015)
XLA Ops:
  0.6 2.1 %shard_map.95 = bf16[8,104,384]{2,1,0:T(8,128)(2,1)} custom-call(bf16[56,1024]{1,0:T(8,128)(2,1)} %a_hbm.1, bf16[56,1024]{1,0:T(8,128)(2,1)} %b_hbm.1, bf16[56,1024]{1,0:T(8,128)(2,1)} %c_hbm.1, bf16[128,1024]{1,0:T(8,128)(2,1)} %grad_hbm.1, f32[8,128]{1,0:T(8,128)} %decay_hbm.1), custom_call_target="tpu_custom_call" | custom-call | tf_op jit(solution)/shard_map/pallas_call | solution.py:37
  2.7 4.5 %all-to-all-start = ((bf16[8,104,384]{2,1,0:T(8,128)(2,1)}), bf16[8,104,384]{2,1,0:T(8,128)(2,1)S(1)}, u32[]{:S(2)}, u32[]{:S(2)}) async-start(bf16[8,104,384]{2,1,0:T(8,128)(2,1)} %shard_map.95), calls=%async_computation | async-start | bytes 1277952 | tf_op jit(solution)/shard_map/all_to_all | solution.py:331
  7.2 2.0 %collective-permute-start.9 = (bf16[128,3584]{1,0:T(8,128)(2,1)}, bf16[128,3584]{1,0:T(8,128)(2,1)S(1)}, u32[]{:S(2)}, u32[]{:S(2)}) collective-permute-start(bf16[128,3584]{1,0:T(8,128)(2,1)} %rest_9_.1), channel_id=1, source_target_pairs={{0,64},{64,128},{128,192},{192,0},{1,65},{65,129},{129,193},{193,1... | collective-permute-start | bytes 2752520 | tf_op jit(solution)/shard_map/ppermute | solution.py:313
  9.2 1.2 collective-permute-start.11
  10.5 8.9 %all-to-all-done.bundle_hbm = bf16[8,104,384]{2,1,0:T(8,128)(2,1)S(1)} async-done(((bf16[8,104,384]{2,1,0:T(8,128)(2,1)}), bf16[8,104,384]{2,1,0:T(8,128)(2,1)S(1)}, u32[]{:S(2)}, u32[]{:S(2)}) %all-to-all-start) | async-done | bytes 639008 | tf_op jit(solution)/shard_map/all_to_all | solution.py:331
  19.4 5.9 %collective-permute-start.1 = (bf16[448,384]{1,0:T(8,128)(2,1)S(1)}, bf16[448,384]{1,0:T(8,128)(2,1)S(1)}, u32[]{:S(2)}, u32[]{:S(2)}) collective-permute-start(bf16[448,384]{1,0:T(8,128)(2,1)S(1)} %bitcast.30), channel_id=1, source_target_pairs={{0,56},{8,0},{16,8},{24,16},{32,24},{40,32},{48,40},{56,48},{1,57}... | collective-permute-start | bytes 1032200 | tf_op jit(solution)/shard_map/ppermute | solution.py:313
  25.4 6.4 %collective-permute-done.1 = bf16[448,384]{1,0:T(8,128)(2,1)S(1)} collective-permute-done((bf16[448,384]{1,0:T(8,128)(2,1)S(1)}, bf16[448,384]{1,0:T(8,128)(2,1)S(1)}, u32[]{:S(2)}, u32[]{:S(2)}) %collective-permute-start.1) | collective-permute-done | bytes 344096 | tf_op jit(solution)/shard_map/ppermute | solution.py:313
  31.8 3.7 %collective-permute-start.3 = (bf16[448,384]{1,0:T(8,128)(2,1)S(1)}, bf16[448,384]{1,0:T(8,128)(2,1)S(1)}, u32[]{:S(2)}, u32[]{:S(2)}) collective-permute-start(bf16[448,384]{1,0:T(8,128)(2,1)S(1)} %collective-permute-done.1), channel_id=1, source_target_pairs={{0,56},{8,0},{16,8},{24,16},{32,24},{40,32},{48,40},{56,48},{1,57}... | collective-permute-start | bytes 1032200 | tf_op jit(solution)/shard_map/ppermute | solution.py:313
  35.5 1.5 collective-permute-done
  37.1 4.1 %collective-permute-done.3 = bf16[448,384]{1,0:T(8,128)(2,1)S(1)} collective-permute-done((bf16[448,384]{1,0:T(8,128)(2,1)S(1)}, bf16[448,384]{1,0:T(8,128)(2,1)S(1)}, u32[]{:S(2)}, u32[]{:S(2)}) %collective-permute-start.3) | collective-permute-done | bytes 344096 | tf_op jit(solution)/shard_map/ppermute | solution.py:313
  41.1 3.7 %collective-permute-start.5 = (bf16[448,384]{1,0:T(8,128)(2,1)S(1)}, bf16[448,384]{1,0:T(8,128)(2,1)S(1)}, u32[]{:S(2)}, u32[]{:S(2)}) collective-permute-start(bf16[448,384]{1,0:T(8,128)(2,1)S(1)} %collective-permute-done.3), channel_id=1, source_target_pairs={{0,56},{8,0},{16,8},{24,16},{32,24},{40,32},{48,40},{56,48},{1,57}... | collective-permute-start | bytes 1032200 | tf_op jit(solution)/shard_map/ppermute | solution.py:313
  47.2 2.7 %collective-permute-start.15 = (bf16[64,3584]{1,0:T(8,128)(2,1)}, bf16[64,3584]{1,0:T(8,128)(2,1)}, u32[]{:S(2)}, u32[]{:S(2)}) collective-permute-start(bf16[64,3584]{1,0:T(8,128)(2,1)} %slice.52), channel_id=1, source_target_pairs={{0,192},{64,0},{128,64},{192,128},{1,193},{65,1},{129,65},{193,129... | collective-permute-start | bytes 1376264 | tf_op jit(solution)/shard_map/ppermute | solution.py:313
  51.7 4.9 %collective-permute-done.13.rest_15_ = bf16[64,3584]{1,0:T(8,128)(2,1)} collective-permute-done((bf16[64,3584]{1,0:T(8,128)(2,1)}, bf16[64,3584]{1,0:T(8,128)(2,1)}, u32[]{:S(2)}, u32[]{:S(2)}) %collective-permute-start.13) | collective-permute-done | bytes 458784 | tf_op jit(solution)/shard_map/ppermute | solution.py:313
  57.1 5.6 %collective-permute-done.4 = bf16[448,384]{1,0:T(8,128)(2,1)S(1)} collective-permute-done((bf16[448,384]{1,0:T(8,128)(2,1)}, bf16[448,384]{1,0:T(8,128)(2,1)S(1)}, u32[]{:S(2)}, u32[]{:S(2)}) %collective-permute-start.4) | collective-permute-done | bytes 344096 | tf_op jit(solution)/shard_map/ppermute | solution.py:313
  64.8 3.9 %collective-permute-done.7 = bf16[224,384]{1,0:T(8,128)(2,1)S(1)} collective-permute-done((bf16[224,384]{1,0:T(8,128)(2,1)S(1)}, bf16[224,384]{1,0:T(8,128)(2,1)S(1)}, u32[]{:S(2)}, u32[]{:S(2)}) %collective-permute-start.7) | collective-permute-done | bytes 172064 | tf_op jit(solution)/shard_map/ppermute | solution.py:313
  70.0 6.3 %collective-permute-done.6 = bf16[224,384]{1,0:T(8,128)(2,1)} collective-permute-done((bf16[224,384]{1,0:T(8,128)(2,1)}, bf16[224,384]{1,0:T(8,128)(2,1)}, u32[]{:S(2)}, u32[]{:S(2)}) %collective-permute-start.6) | collective-permute-done | bytes 172064 | tf_op jit(solution)/shard_map/ppermute | solution.py:313
  76.4 10.6 %shard_map.96 = (bf16[4,4,256,128]{3,2,1,0:T(8,128)(2,1)}, f32[4,256,128]{2,1,0:T(8,128)}, bf16[8,128,3584]{2,1,0:T(8,128)(2,1)}, bf16[8,112,128]{2,1,0:T(8,128)(2,1)}) custom-call(s32[3]{0:T(128)} %pad_add_fusion.ids, bf16[4,8,112,128]{3,2,1,0:T(8,128)(2,1)} %bitcast.33, bf16[4,112,384]{2,1,0:T(8,128)(2,1)} %bitcast.32, bf16[4,112,384]{2,1,0:T(8,128)(2,1)} %bitcast.38, ...), custom_call_target="tpu_custom_call" | custom-call | tf_op jit(solution)/shard_map/pallas_call | solution.py:37
  87.0 13.4 %all_to_all.35.got = bf16[8,112,128]{2,1,0:T(8,128)(2,1)S(1)} all-to-all(bf16[8,112,128]{2,1,0:T(8,128)(2,1)} %get-tuple-element.12), channel_id=1, replica_groups=mesh['y'=4,'z'=8,'c'=2,'x'=4] {'z'}, dimensions={0} | all-to-all | bytes 458752 | tf_op jit(solution)/shard_map/all_to_all | solution.py:368
  100.5 12.8 %all_to_all.36.s_in = bf16[8,96,128]{2,1,0:T(8,128)(2,1)} all-to-all(bf16[8,96,128]{2,1,0:T(8,128)(2,1)S(1)} %get-tuple-element.13), channel_id=1, replica_groups=mesh['y'=4,'z'=8,'c'=2,'x'=4] {'z'}, dimensions={0} | all-to-all | bytes 393216 | tf_op jit(solution)/shard_map/all_to_all | solution.py:370
  113.4 9.7 %shard_map.98 = (bf16[8,80,128]{2,1,0:T(8,128)(2,1)}, f32[4,2,256,128]{3,2,1,0:T(8,128)}) custom-call(bf16[8,96,128]{2,1,0:T(8,128)(2,1)} %all_to_all.36.s_in, bf16[2,128,128]{2,1,0:T(8,128)(2,1)} %pad_maximum_fusion.rest_19_.lift, f32[4,256]{1,0:T(4,128)} %add.26.rest_20_.logs, bf16[4,4,256,128]{3,2,1,0:T(8,128)(2,1)} %get-tuple-element.14.kvql_hbm, ...), custom_call_target="tpu_custom_call" | custom-call | tf_op jit(solution)/shard_map/pallas_call | solution.py:37
  123.1 12.7 %all_to_all.37.got = bf16[8,80,128]{2,1,0:T(8,128)(2,1)S(1)} all-to-all(bf16[8,80,128]{2,1,0:T(8,128)(2,1)} %get-tuple-element.16), channel_id=1, replica_groups=mesh['y'=4,'z'=8,'c'=2,'x'=4] {'z'}, dimensions={0} | all-to-all | bytes 327680 | tf_op jit(solution)/shard_map/all_to_all | solution.py:387
  135.9 12.5 %all_to_all.38.r_in = bf16[8,80,128]{2,1,0:T(8,128)(2,1)} all-to-all(bf16[8,80,128]{2,1,0:T(8,128)(2,1)S(1)} %shard_map.99), channel_id=1, replica_groups=mesh['y'=4,'z'=8,'c'=2,'x'=4] {'z'}, dimensions={0} | all-to-all | bytes 327680 | tf_op jit(solution)/shard_map/all_to_all | solution.py:389
  148.3 9.0 %shard_map.100 = (f32[16,112,128]{2,1,0:T(8,128)}, bf16[16,112,128]{2,1,0:T(8,128)(2,1)}) custom-call(s32[3]{0:T(128)} %pad_add_fusion.ids, bf16[8,80,128]{2,1,0:T(8,128)(2,1)} %all_to_all.38.r_in, bf16[2,128,128]{2,1,0:T(8,128)(2,1)} %pad_maximum_fusion.rest_19_.lift, f32[4,256]{1,0:T(4,128)} %add.26.rest_20_.logs, ...), custom_call_target="tpu_custom_call" | custom-call | tf_op jit(solution)/shard_map/pallas_call | solution.py:37
  157.5 2.0 %collective-permute-done.17.b = bf16[16,112,128]{2,1,0:T(8,128)(2,1)S(1)} collective-permute-done((bf16[16,112,128]{2,1,0:T(8,128)(2,1)}, bf16[16,112,128]{2,1,0:T(8,128)(2,1)S(1)}, u32[]{:S(2)}, u32[]{:S(2)}) %collective-permute-start.17) | collective-permute-done | bytes 458784 | tf_op jit(solution)/shard_map/ppermute | solution.py:314
  159.5 1.2 copy-done
  161.5 4.8 %all-to-all-start.5 = ((bf16[16,112,128]{2,1,0:T(8,128)(2,1)}), bf16[16,112,128]{2,1,0:T(8,128)(2,1)S(1)}, u32[]{:S(2)}, u32[]{:S(2)}) async-start(bf16[16,112,128]{2,1,0:T(8,128)(2,1)} %shard_map.101), calls=%async_computation.5 | async-start | bytes 917504 | tf_op jit(solution)/shard_map/all_to_all | solution.py:413
  167.1 1.2 collective-permute-done.18.other
  168.4 3.1 %collective-permute-start.21 = (bf16[2,128,128]{2,1,0:T(8,128)(2,1)S(1)}, bf16[2,128,128]{2,1,0:T(8,128)(2,1)S(1)}, u32[]{:S(2)}, u32[]{:S(2)}) collective-permute-start(bf16[2,128,128]{2,1,0:T(8,128)(2,1)S(1)} %pad_maximum_fusion.1), channel_id=1, source_target_pairs={{0,128},{64,192},{128,0},{192,64},{1,129},{65,193},{129,1},{193,65... | collective-permute-start | bytes 196616 | tf_op jit(solution)/shard_map/ppermute | solution.py:313
  173.4 2.8 %all-to-all-done.5.got = bf16[16,112,128]{2,1,0:T(8,128)(2,1)S(1)} async-done(((bf16[16,112,128]{2,1,0:T(8,128)(2,1)}), bf16[16,112,128]{2,1,0:T(8,128)(2,1)S(1)}, u32[]{:S(2)}, u32[]{:S(2)}) %all-to-all-start.5) | async-done | bytes 458784 | tf_op jit(solution)/shard_map/all_to_all | solution.py:413
  177.0 3.3 %all-to-all-start.6 = ((bf16[8,16,128]{2,1,0:T(8,128)(2,1)}), bf16[8,16,128]{2,1,0:T(8,128)(2,1)S(1)}, u32[]{:S(2)}, u32[]{:S(2)}) async-start(bf16[8,16,128]{2,1,0:T(8,128)(2,1)} %shard_map.102), calls=%async_computation.6 | async-start | bytes 65536 | tf_op jit(solution)/shard_map/all_to_all | solution.py:418
  180.3 1.4 shard_map.104
  181.7 6.5 %all-to-all-done.6.got = bf16[8,16,128]{2,1,0:T(8,128)(2,1)S(1)} async-done(((bf16[8,16,128]{2,1,0:T(8,128)(2,1)}), bf16[8,16,128]{2,1,0:T(8,128)(2,1)S(1)}, u32[]{:S(2)}, u32[]{:S(2)}) %all-to-all-start.6) | async-done | bytes 32800 | tf_op jit(solution)/shard_map/all_to_all | solution.py:418
  (72 shorter events, 13.3 us)
Async XLA Ops:
  2.7 16.6 %all-to-all-start = ((bf16[8,104,384]{2,1,0:T(8,128)(2,1)}), bf16[8,104,384]{2,1,0:T(8,128)(2,1)S(1)}, u32[]{:S(2)}, u32[]{:S(2)}) async-start(bf16[8,104,384]{2,1,0:T(8,128)(2,1)} %shard_map.95), calls=%async_computation | async-start | bytes 1277952 | tf_op jit(solution)/shard_map/all_to_all | solution.py:331
  7.2 37.6 %collective-permute-start.9 = (bf16[128,3584]{1,0:T(8,128)(2,1)}, bf16[128,3584]{1,0:T(8,128)(2,1)S(1)}, u32[]{:S(2)}, u32[]{:S(2)}) collective-permute-start(bf16[128,3584]{1,0:T(8,128)(2,1)} %rest_9_.1), channel_id=1, source_target_pairs={{0,64},{64,128},{128,192},{192,0},{1,65},{65,129},{129,193},{193,1... | collective-permute-start | bytes 2752520 | tf_op jit(solution)/shard_map/ppermute | solution.py:313
  9.2 37.0 %collective-permute-start.11 = (bf16[128,3584]{1,0:T(8,128)(2,1)}, bf16[128,3584]{1,0:T(8,128)(2,1)S(1)}, u32[]{:S(2)}, u32[]{:S(2)}) collective-permute-start(bf16[128,3584]{1,0:T(8,128)(2,1)} %rest_9_.1), channel_id=1, source_target_pairs={{0,192},{64,0},{128,64},{192,128},{1,193},{65,1},{129,65},{193,129... | collective-permute-start | bytes 2752520 | tf_op jit(solution)/shard_map/ppermute | solution.py:313
  19.4 67.6 %copy-start.2 = (bf16[8,104,384]{2,1,0:T(8,128)(2,1)}, bf16[8,104,384]{2,1,0:T(8,128)(2,1)S(1)}, u32[]{:S(2)}) copy-start(bf16[8,104,384]{2,1,0:T(8,128)(2,1)S(1)} %all-to-all-done.bundle_hbm) | copy-start | bytes 1916932
  19.4 56.9 %copy-start.5 = (bf16[8,56,384]{2,1,0:T(8,128)(2,1)}, bf16[8,56,384]{2,1,0:T(8,128)(2,1)S(1)}, u32[]{:S(2)}) copy-start(bf16[8,56,384]{2,1,0:T(8,128)(2,1)S(1)} %slice.48) | copy-start | bytes 1032196
  19.4 12.4 %collective-permute-start.1 = (bf16[448,384]{1,0:T(8,128)(2,1)S(1)}, bf16[448,384]{1,0:T(8,128)(2,1)S(1)}, u32[]{:S(2)}, u32[]{:S(2)}) collective-permute-start(bf16[448,384]{1,0:T(8,128)(2,1)S(1)} %bitcast.30), channel_id=1, source_target_pairs={{0,56},{8,0},{16,8},{24,16},{32,24},{40,32},{48,40},{56,48},{1,57}... | collective-permute-start | bytes 1032200 | tf_op jit(solution)/shard_map/ppermute | solution.py:313
  25.4 24.5 %collective-permute-start.8 = (bf16[128,3584]{1,0:T(8,128)(2,1)}, bf16[128,3584]{1,0:T(8,128)(2,1)S(1)}, u32[]{:S(2)}, u32[]{:S(2)}) collective-permute-start(bf16[128,3584]{1,0:T(8,128)(2,1)} %rest_9_.1), channel_id=1, source_target_pairs={{0,4},{4,0},{1,5},{5,1},{2,6},{6,2},{3,7},{7,3},{8,12},{12,8},{9,1... | collective-permute-start | bytes 2752520 | tf_op jit(solution)/shard_map/ppermute | solution.py:314
  25.4 11.7 %collective-permute-start = (bf16[448,384]{1,0:T(8,128)(2,1)S(1)}, bf16[448,384]{1,0:T(8,128)(2,1)S(1)}, u32[]{:S(2)}, u32[]{:S(2)}) collective-permute-start(bf16[448,384]{1,0:T(8,128)(2,1)S(1)} %bitcast.31), channel_id=1, source_target_pairs={{0,8},{8,16},{16,24},{24,32},{32,40},{40,48},{48,56},{56,0},{1,9},... | collective-permute-start | bytes 1032200 | tf_op jit(solution)/shard_map/ppermute | solution.py:313
  31.8 9.3 %collective-permute-start.3 = (bf16[448,384]{1,0:T(8,128)(2,1)S(1)}, bf16[448,384]{1,0:T(8,128)(2,1)S(1)}, u32[]{:S(2)}, u32[]{:S(2)}) collective-permute-start(bf16[448,384]{1,0:T(8,128)(2,1)S(1)} %collective-permute-done.1), channel_id=1, source_target_pairs={{0,56},{8,0},{16,8},{24,16},{32,24},{40,32},{48,40},{56,48},{1,57}... | collective-permute-start | bytes 1032200 | tf_op jit(solution)/shard_map/ppermute | solution.py:313
  37.1 13.7 %copy-start.10 = (bf16[448,384]{1,0:T(8,128)(2,1)}, bf16[448,384]{1,0:T(8,128)(2,1)S(1)}, u32[]{:S(2)}) copy-start(bf16[448,384]{1,0:T(8,128)(2,1)S(1)} %collective-permute-done) | copy-start | bytes 1032196
  37.1 13.7 %collective-permute-start.2 = (bf16[448,384]{1,0:T(8,128)(2,1)S(1)}, bf16[448,384]{1,0:T(8,128)(2,1)}, u32[]{:S(2)}, u32[]{:S(2)}) collective-permute-start(bf16[448,384]{1,0:T(8,128)(2,1)S(1)} %collective-permute-done), channel_id=1, source_target_pairs={{0,8},{8,16},{16,24},{24,32},{32,40},{40,48},{48,56},{56,0},{1,9},... | collective-permute-start | bytes 1032200 | tf_op jit(solution)/shard_map/ppermute | solution.py:313
  41.1 9.7 %collective-permute-start.5 = (bf16[448,384]{1,0:T(8,128)(2,1)S(1)}, bf16[448,384]{1,0:T(8,128)(2,1)S(1)}, u32[]{:S(2)}, u32[]{:S(2)}) collective-permute-start(bf16[448,384]{1,0:T(8,128)(2,1)S(1)} %collective-permute-done.3), channel_id=1, source_target_pairs={{0,56},{8,0},{16,8},{24,16},{32,24},{40,32},{48,40},{56,48},{1,57}... | collective-permute-start | bytes 1032200 | tf_op jit(solution)/shard_map/ppermute | solution.py:313
  44.8 31.5 %copy-start.3 = (bf16[128,3584]{1,0:T(8,128)(2,1)}, bf16[128,3584]{1,0:T(8,128)(2,1)S(1)}, u32[]{:S(2)}) copy-start(bf16[128,3584]{1,0:T(8,128)(2,1)S(1)} %collective-permute-done.9.rest_11_) | copy-start | bytes 2752516
  45.7 10.9 %collective-permute-start.13 = (bf16[64,3584]{1,0:T(8,128)(2,1)}, bf16[64,3584]{1,0:T(8,128)(2,1)}, u32[]{:S(2)}, u32[]{:S(2)}) collective-permute-start(bf16[64,3584]{1,0:T(8,128)(2,1)} %slice.51), channel_id=1, source_target_pairs={{0,64},{64,128},{128,192},{192,0},{1,65},{65,129},{129,193},{193,1... | collective-permute-start | bytes 1376264 | tf_op jit(solution)/shard_map/ppermute | solution.py:313
  46.3 30.1 %copy-start.4 = (bf16[128,3584]{1,0:T(8,128)(2,1)}, bf16[128,3584]{1,0:T(8,128)(2,1)S(1)}, u32[]{:S(2)}) copy-start(bf16[128,3584]{1,0:T(8,128)(2,1)S(1)} %collective-permute-done.11.rest_13_) | copy-start | bytes 2752516
  47.2 9.6 %collective-permute-start.15 = (bf16[64,3584]{1,0:T(8,128)(2,1)}, bf16[64,3584]{1,0:T(8,128)(2,1)}, u32[]{:S(2)}, u32[]{:S(2)}) collective-permute-start(bf16[64,3584]{1,0:T(8,128)(2,1)} %slice.52), channel_id=1, source_target_pairs={{0,192},{64,0},{128,64},{192,128},{1,193},{65,1},{129,65},{193,129... | collective-permute-start | bytes 1376264 | tf_op jit(solution)/shard_map/ppermute | solution.py:313
  49.8 26.4 %collective-permute-start.10 = (bf16[128,3584]{1,0:T(8,128)(2,1)S(1)}, bf16[128,3584]{1,0:T(8,128)(2,1)}, u32[]{:S(2)}, u32[]{:S(2)}) collective-permute-start(bf16[128,3584]{1,0:T(8,128)(2,1)S(1)} %collective-permute-done.9.rest_11_), channel_id=1, source_target_pairs={{0,4},{4,0},{1,5},{5,1},{2,6},{6,2},{3,7},{7,3},{8,12},{12,8},{9,1... | collective-permute-start | bytes 2752520 | tf_op jit(solution)/shard_map/ppermute | solution.py:314
  50.8 25.5 %collective-permute-start.12 = (bf16[128,3584]{1,0:T(8,128)(2,1)S(1)}, bf16[128,3584]{1,0:T(8,128)(2,1)}, u32[]{:S(2)}, u32[]{:S(2)}) collective-permute-start(bf16[128,3584]{1,0:T(8,128)(2,1)S(1)} %collective-permute-done.11.rest_13_), channel_id=1, source_target_pairs={{0,4},{4,0},{1,5},{5,1},{2,6},{6,2},{3,7},{7,3},{8,12},{12,8},{9,1... | collective-permute-start | bytes 2752520 | tf_op jit(solution)/shard_map/ppermute | solution.py:314
  50.8 25.5 %copy-start.7 = (bf16[448,384]{1,0:T(8,128)(2,1)}, bf16[448,384]{1,0:T(8,128)(2,1)S(1)}, u32[]{:S(2)}) copy-start(bf16[448,384]{1,0:T(8,128)(2,1)S(1)} %collective-permute-done.5) | copy-start | bytes 1032196
  50.8 12.0 %collective-permute-start.4 = (bf16[448,384]{1,0:T(8,128)(2,1)}, bf16[448,384]{1,0:T(8,128)(2,1)S(1)}, u32[]{:S(2)}, u32[]{:S(2)}) collective-permute-start(bf16[448,384]{1,0:T(8,128)(2,1)} %collective-permute-done.2), channel_id=1, source_target_pairs={{0,8},{8,16},{16,24},{24,32},{32,40},{40,48},{48,56},{56,0},{1,9},... | collective-permute-start | bytes 1032200 | tf_op jit(solution)/shard_map/ppermute | solution.py:313
  56.6 19.7 %collective-permute-start.14 = (bf16[64,3584]{1,0:T(8,128)(2,1)}, bf16[64,3584]{1,0:T(8,128)(2,1)}, u32[]{:S(2)}, u32[]{:S(2)}) collective-permute-start(bf16[64,3584]{1,0:T(8,128)(2,1)} %collective-permute-done.13.rest_15_), channel_id=1, source_target_pairs={{0,4},{4,0},{1,5},{5,1},{2,6},{6,2},{3,7},{7,3},{8,12},{12,8},{9,1... | collective-permute-start | bytes 1376264 | tf_op jit(solution)/shard_map/ppermute | solution.py:314
  56.8 19.5 %collective-permute-start.16 = (bf16[64,3584]{1,0:T(8,128)(2,1)}, bf16[64,3584]{1,0:T(8,128)(2,1)}, u32[]{:S(2)}, u32[]{:S(2)}) collective-permute-start(bf16[64,3584]{1,0:T(8,128)(2,1)} %collective-permute-done.15.rest_17_), channel_id=1, source_target_pairs={{0,4},{4,0},{1,5},{5,1},{2,6},{6,2},{3,7},{7,3},{8,12},{12,8},{9,1... | collective-permute-start | bytes 1376264 | tf_op jit(solution)/shard_map/ppermute | solution.py:314
  62.8 5.9 %collective-permute-start.7 = (bf16[224,384]{1,0:T(8,128)(2,1)S(1)}, bf16[224,384]{1,0:T(8,128)(2,1)S(1)}, u32[]{:S(2)}, u32[]{:S(2)}) collective-permute-start(bf16[224,384]{1,0:T(8,128)(2,1)S(1)} %slice.50), channel_id=1, source_target_pairs={{0,56},{8,0},{16,8},{24,16},{32,24},{40,32},{48,40},{56,48},{1,57}... | collective-permute-start | bytes 516104 | tf_op jit(solution)/shard_map/ppermute | solution.py:313
  69.3 6.9 %collective-permute-start.6 = (bf16[224,384]{1,0:T(8,128)(2,1)}, bf16[224,384]{1,0:T(8,128)(2,1)}, u32[]{:S(2)}, u32[]{:S(2)}) collective-permute-start(bf16[224,384]{1,0:T(8,128)(2,1)} %slice.49), channel_id=1, source_target_pairs={{0,8},{8,16},{16,24},{24,32},{32,40},{40,48},{48,56},{56,0},{1,9},... | collective-permute-start | bytes 516104 | tf_op jit(solution)/shard_map/ppermute | solution.py:313
  123.1 57.3 %copy-start.1 = (s32[3]{0:T(128)S(1)}, s32[3]{0:T(128)}, u32[]{:S(2)}) copy-start(s32[3]{0:T(128)} %pad_add_fusion.ids) | copy-start | bytes 40
  157.4 2.1 %collective-permute-start.17 = (bf16[16,112,128]{2,1,0:T(8,128)(2,1)}, bf16[16,112,128]{2,1,0:T(8,128)(2,1)S(1)}, u32[]{:S(2)}, u32[]{:S(2)}) collective-permute-start(bf16[16,112,128]{2,1,0:T(8,128)(2,1)} %get-tuple-element.21), channel_id=1, source_target_pairs={{0,4},{4,0},{1,5},{5,1},{2,6},{6,2},{3,7},{7,3},{8,12},{12,8},{9,1... | collective-permute-start | bytes 1376264 | tf_op jit(solution)/shard_map/ppermute | solution.py:314
  161.5 14.7 %all-to-all-start.5 = ((bf16[16,112,128]{2,1,0:T(8,128)(2,1)}), bf16[16,112,128]{2,1,0:T(8,128)(2,1)S(1)}, u32[]{:S(2)}, u32[]{:S(2)}) async-start(bf16[16,112,128]{2,1,0:T(8,128)(2,1)} %shard_map.101), calls=%async_computation.5 | async-start | bytes 917504 | tf_op jit(solution)/shard_map/all_to_all | solution.py:413
  167.1 1.2 collective-permute-start.18
  168.4 11.9 %collective-permute-start.21 = (bf16[2,128,128]{2,1,0:T(8,128)(2,1)S(1)}, bf16[2,128,128]{2,1,0:T(8,128)(2,1)S(1)}, u32[]{:S(2)}, u32[]{:S(2)}) collective-permute-start(bf16[2,128,128]{2,1,0:T(8,128)(2,1)S(1)} %pad_maximum_fusion.1), channel_id=1, source_target_pairs={{0,128},{64,192},{128,0},{192,64},{1,129},{65,193},{129,1},{193,65... | collective-permute-start | bytes 196616 | tf_op jit(solution)/shard_map/ppermute | solution.py:313
  171.4 8.9 %collective-permute-start.20 = (bf16[2,128,128]{2,1,0:T(8,128)(2,1)S(1)}, bf16[2,128,128]{2,1,0:T(8,128)(2,1)S(1)}, u32[]{:S(2)}, u32[]{:S(2)}) collective-permute-start(bf16[2,128,128]{2,1,0:T(8,128)(2,1)S(1)} %pad_maximum_fusion.1), channel_id=1, source_target_pairs={{0,192},{64,0},{128,64},{192,128},{1,193},{65,1},{129,65},{193,129... | collective-permute-start | bytes 196616 | tf_op jit(solution)/shard_map/ppermute | solution.py:313
  172.6 7.7 %collective-permute-start.19 = (bf16[2,128,128]{2,1,0:T(8,128)(2,1)S(1)}, bf16[2,128,128]{2,1,0:T(8,128)(2,1)S(1)}, u32[]{:S(2)}, u32[]{:S(2)}) collective-permute-start(bf16[2,128,128]{2,1,0:T(8,128)(2,1)S(1)} %pad_maximum_fusion.1), channel_id=1, source_target_pairs={{0,64},{64,128},{128,192},{192,0},{1,65},{65,129},{129,193},{193,1... | collective-permute-start | bytes 196616 | tf_op jit(solution)/shard_map/ppermute | solution.py:313
  177.0 11.3 %all-to-all-start.6 = ((bf16[8,16,128]{2,1,0:T(8,128)(2,1)}), bf16[8,16,128]{2,1,0:T(8,128)(2,1)S(1)}, u32[]{:S(2)}, u32[]{:S(2)}) async-start(bf16[8,16,128]{2,1,0:T(8,128)(2,1)} %shard_map.102), calls=%async_computation.6 | async-start | bytes 65536 | tf_op jit(solution)/shard_map/all_to_all | solution.py:418
  (6 other events, 35.5 us)

commit v3 on v2

--- a/solution.py
+++ b/solution.py
@@ -58,12 +58,15 @@
 
 
 def running(logs):
-    n = logs.shape[1]
-    t = lax.broadcasted_iota(jnp.int32, (n, n), 0)
-    causal = lax.broadcasted_iota(jnp.int32, (n, n), 1) <= t
-    terms = jnp.where(causal, jnp.broadcast_to(logs, (n, n)), 0.0)
-    sums = jnp.dot(terms, jnp.ones((n, 128), f32), precision=lax.Precision.HIGHEST)
-    return sums, causal
+    chunks, n = logs.shape
+    parts = jnp.concatenate(list(split3(logs)) + [jnp.zeros((16 - 3 * chunks, n), f32)], axis=0)
+    ones = lax.broadcasted_iota(jnp.int32, (n, n), 0) <= lax.broadcasted_iota(jnp.int32, (n, n), 1)
+    sums = dot(parts.astype(bf16), ones.astype(f32).astype(bf16))
+    return sums[:chunks] + (sums[chunks : 2 * chunks] + sums[2 * chunks : 3 * chunks])
+
+
+def down_rows(row):
+    return jnp.broadcast_to(row, (128, row.shape[1])).T
 
 
 def pack_kernel(a_hbm, b_hbm, c_hbm, grad_hbm, decay_hbm, out, a, b, c, grad, decay, sems):
@@ -106,8 +109,9 @@
         pairs.append((p, dst))
     copies = begin(pairs, sems)
     ends = []
+    cum = running(logs[...])
     for n in range(ny):
-        sums, _ = running(logs[n : n + 1, :])
+        sums = down_rows(cum[n : n + 1, :])
         total = sums[255:256, :]
         tail[n] = jnp.exp(total - sums)
         ends += list(split3(total))
@@ -190,12 +194,15 @@
     total_v = jnp.zeros((128, 128), f32)
     cross = jnp.zeros((64, 128), f32)
     stores = []
+    cum = running(logs[...])
+    square = (cum.shape[1], cum.shape[1])
+    causal = lax.broadcasted_iota(jnp.int32, square, 1) <= lax.broadcasted_iota(jnp.int32, square, 0)
     for n in range(ny):
         s = s_in[:, n * 16 : n * 16 + 16, :].reshape(128, 128)
         side = s_in[:, 64 + n * 8 : 72 + n * 8, :].astype(f32).reshape(64, 128).astype(bf16)
-        sums, causal = running(logs[n : n + 1, :])
+        sums = down_rows(cum[n : n + 1, :])
         ahead = jnp.exp(sums)
-        spread = jnp.concatenate([sums, sums], axis=1) - sums.T[0:1, :]
+        spread = jnp.concatenate([sums, sums], axis=1) - cum[n : n + 1, :]
         dec = jnp.where(causal, jnp.exp(jnp.where(causal, spread, 0.0)), 0.0)
         for copy in copies[3 * n : 3 * n + 3]:
             copy.wait()
@@ -239,9 +246,10 @@
         copies += begin([(kvql_hbm.at[n, 0], k.at[n]), (back_hbm.at[n], back.at[n])], sems, 2 * n)
     lanes = [slice(m * wide, m * wide + wide) for m in range(blocks)]
     parts = begin([(tok_hbm.at[:, :, m], tok.at[:, :, m]) for m in lanes], sems, 2 * ny)
+    cum = running(logs[...])
     for n in range(ny):
         rows = slice(n * 256, n * 256 + 256)
-        sums, _ = running(logs[n : n + 1, :])
+        sums = down_rows(cum[n : n + 1, :])
         tail = jnp.exp(sums[255:256, :] - sums)
         r = r_in[:, n * 16 : n * 16 + 16, :].reshape(128, 128)
         copies[2 * n].wait()
@@ -316,7 +324,8 @@
 
     below = ring(tokens, 1)
     above = ring(tokens, -1)
-    far0, far1 = ring(below[: own // 2], 1), ring(above[own // 2 :], -1)
+    far0 = ring(below[: own // 2], 1)
+    far1 = ring(above[own // 2 :], -1)
     pieces = []
     for p in (tokens, below, above, far0, far1):
         pieces += [p, swap(p)]
@@ -332,10 +341,12 @@
     w = bundle[:, 48:].reshape(heads * rows, 3 * hk)
     weights, ahead, behind = [w], w, w
     for _ in range(nz // 2 - 1):
-        ahead, behind = ring(ahead, 1, "z", nz), ring(behind, -1, "z", nz)
+        ahead = ring(ahead, 1, "z", nz)
+        behind = ring(behind, -1, "z", nz)
         weights += [ahead, behind]
     half = heads * rows // 2
-    weights += [ring(ahead[:half], 1, "z", nz), ring(behind[half:], -1, "z", nz)]
+    weights.append(ring(ahead[:half], 1, "z", nz))
+    weights.append(ring(behind[half:], -1, "z", nz))
     deep = nc * rows
     weights = [p.reshape(-1, deep, 3 * hk) for p in weights]
 

time: 190 us -> 187 us (0.984)
  Pallas kernels: 35.2 us -> 32.7 us
    pallas_call x10, Pallas kernels: 35.2 us -> 32.7 us  [call(): pl.pallas_call(kernel, out_shape=outs, in_specs=specs or [VMEM] * len(arg...]
where the time goes in v3:
time: 187 us; the launch traced here: 186 us
  waiting for transfers between devices  54.4 us (29%)
  blocking collectives  51.5 us (28%)
  starting transfers between devices  38.1 us (20%)
  Pallas kernels  32.7 us (17%)
  local copies, waits for them, and re-layouts  7.43 us (4%)
    ppermute x15, waiting for transfers between devices, layer(): lax.ppermute(v, a, [(i, (i + s) % n) for i in range(n)])  33 us
    pallas_call x10, Pallas kernels, call(): pl.pallas_call(kernel, out_shape=outs, in_specs=specs or [VMEM] * len(arg...  32.7 us
    all_to_all x2, blocking collectives, layer(): got = lax.all_to_all(send, 'z', 0, 0, tiled=True)  26.2 us
    ppermute x15, starting transfers between devices, layer(): lax.ppermute(v, a, [(i, (i + s) % n) for i in range(n)])  25 us
    all_to_all x1, blocking collectives, layer(): s_in = lax.all_to_all(scanned, 'z', 0, 0, tiled=True)  12.8 us
    all_to_all x1, blocking collectives, layer(): r_in = lax.all_to_all(scanned, 'z', 0, 0, tiled=True)  12.5 us
    all_to_all x1, waiting for transfers between devices, layer(): bundle = lax.all_to_all(bundle, group, 0, 0, tiled=True)  8.91 us
    all_to_all x1, waiting for transfers between devices, layer(): down_terms = lax.all_to_all(down_terms, 'z', 0, 0, tiled=True)  6.51 us
  transfers between devices with their start and end apart: 25, of which 13 were waited for; matrix products, arithmetic and copies ran while one was open for 3% of the time, Pallas kernels for 1%

profile of v3, /device:TPU:2, one launch (start us, length us, event | category | flops | bytes accessed | tf_op | source)
XLA Modules:
  0.0 186.3 jit_solution(5488616164450919093)
XLA Ops:
  0.6 2.1 %shard_map.95 = bf16[8,104,384]{2,1,0:T(8,128)(2,1)} custom-call(bf16[56,1024]{1,0:T(8,128)(2,1)} %a_hbm.1, bf16[56,1024]{1,0:T(8,128)(2,1)} %b_hbm.1, bf16[56,1024]{1,0:T(8,128)(2,1)} %c_hbm.1, bf16[128,1024]{1,0:T(8,128)(2,1)} %grad_hbm.1, f32[8,128]{1,0:T(8,128)} %decay_hbm.1), custom_call_target="tpu_custom_call" | custom-call | tf_op jit(solution)/shard_map/pallas_call | solution.py:37
  2.7 4.5 %all-to-all-start = ((bf16[8,104,384]{2,1,0:T(8,128)(2,1)}), bf16[8,104,384]{2,1,0:T(8,128)(2,1)S(1)}, u32[]{:S(2)}, u32[]{:S(2)}) async-start(bf16[8,104,384]{2,1,0:T(8,128)(2,1)} %shard_map.95), calls=%async_computation | async-start | bytes 1277952 | tf_op jit(solution)/shard_map/all_to_all | solution.py:340
  7.2 2.0 %collective-permute-start.9 = (bf16[128,3584]{1,0:T(8,128)(2,1)}, bf16[128,3584]{1,0:T(8,128)(2,1)S(1)}, u32[]{:S(2)}, u32[]{:S(2)}) collective-permute-start(bf16[128,3584]{1,0:T(8,128)(2,1)} %rest_9_.1), channel_id=1, source_target_pairs={{0,64},{64,128},{128,192},{192,0},{1,65},{65,129},{129,193},{193,1... | collective-permute-start | bytes 2752520 | tf_op jit(solution)/shard_map/ppermute | solution.py:321
  9.2 1.2 collective-permute-start.11
  10.5 8.9 %all-to-all-done.bundle_hbm = bf16[8,104,384]{2,1,0:T(8,128)(2,1)S(1)} async-done(((bf16[8,104,384]{2,1,0:T(8,128)(2,1)}), bf16[8,104,384]{2,1,0:T(8,128)(2,1)S(1)}, u32[]{:S(2)}, u32[]{:S(2)}) %all-to-all-start) | async-done | bytes 639008 | tf_op jit(solution)/shard_map/all_to_all | solution.py:340
  19.4 5.9 %collective-permute-start.1 = (bf16[448,384]{1,0:T(8,128)(2,1)S(1)}, bf16[448,384]{1,0:T(8,128)(2,1)S(1)}, u32[]{:S(2)}, u32[]{:S(2)}) collective-permute-start(bf16[448,384]{1,0:T(8,128)(2,1)S(1)} %bitcast.30), channel_id=1, source_target_pairs={{0,56},{8,0},{16,8},{24,16},{32,24},{40,32},{48,40},{56,48},{1,57}... | collective-permute-start | bytes 1032200 | tf_op jit(solution)/shard_map/ppermute | solution.py:321
  25.4 6.4 %collective-permute-done.1 = bf16[448,384]{1,0:T(8,128)(2,1)S(1)} collective-permute-done((bf16[448,384]{1,0:T(8,128)(2,1)S(1)}, bf16[448,384]{1,0:T(8,128)(2,1)S(1)}, u32[]{:S(2)}, u32[]{:S(2)}) %collective-permute-start.1) | collective-permute-done | bytes 344096 | tf_op jit(solution)/shard_map/ppermute | solution.py:321
  31.8 3.7 %collective-permute-start.3 = (bf16[448,384]{1,0:T(8,128)(2,1)S(1)}, bf16[448,384]{1,0:T(8,128)(2,1)S(1)}, u32[]{:S(2)}, u32[]{:S(2)}) collective-permute-start(bf16[448,384]{1,0:T(8,128)(2,1)S(1)} %collective-permute-done.1), channel_id=1, source_target_pairs={{0,56},{8,0},{16,8},{24,16},{32,24},{40,32},{48,40},{56,48},{1,57}... | collective-permute-start | bytes 1032200 | tf_op jit(solution)/shard_map/ppermute | solution.py:321
  35.5 1.5 collective-permute-done
  37.1 4.1 %collective-permute-done.3 = bf16[448,384]{1,0:T(8,128)(2,1)S(1)} collective-permute-done((bf16[448,384]{1,0:T(8,128)(2,1)S(1)}, bf16[448,384]{1,0:T(8,128)(2,1)S(1)}, u32[]{:S(2)}, u32[]{:S(2)}) %collective-permute-start.3) | collective-permute-done | bytes 344096 | tf_op jit(solution)/shard_map/ppermute | solution.py:321
  41.1 3.7 %collective-permute-start.5 = (bf16[448,384]{1,0:T(8,128)(2,1)S(1)}, bf16[448,384]{1,0:T(8,128)(2,1)S(1)}, u32[]{:S(2)}, u32[]{:S(2)}) collective-permute-start(bf16[448,384]{1,0:T(8,128)(2,1)S(1)} %collective-permute-done.3), channel_id=1, source_target_pairs={{0,56},{8,0},{16,8},{24,16},{32,24},{40,32},{48,40},{56,48},{1,57}... | collective-permute-start | bytes 1032200 | tf_op jit(solution)/shard_map/ppermute | solution.py:321
  47.1 2.7 %collective-permute-start.15 = (bf16[64,3584]{1,0:T(8,128)(2,1)}, bf16[64,3584]{1,0:T(8,128)(2,1)}, u32[]{:S(2)}, u32[]{:S(2)}) collective-permute-start(bf16[64,3584]{1,0:T(8,128)(2,1)} %slice.52), channel_id=1, source_target_pairs={{0,192},{64,0},{128,64},{192,128},{1,193},{65,1},{129,65},{193,129... | collective-permute-start | bytes 1376264 | tf_op jit(solution)/shard_map/ppermute | solution.py:321
  51.7 4.9 %collective-permute-done.13.rest_15_ = bf16[64,3584]{1,0:T(8,128)(2,1)} collective-permute-done((bf16[64,3584]{1,0:T(8,128)(2,1)}, bf16[64,3584]{1,0:T(8,128)(2,1)}, u32[]{:S(2)}, u32[]{:S(2)}) %collective-permute-start.13) | collective-permute-done | bytes 458784 | tf_op jit(solution)/shard_map/ppermute | solution.py:321
  57.1 5.6 %collective-permute-done.4 = bf16[448,384]{1,0:T(8,128)(2,1)S(1)} collective-permute-done((bf16[448,384]{1,0:T(8,128)(2,1)}, bf16[448,384]{1,0:T(8,128)(2,1)S(1)}, u32[]{:S(2)}, u32[]{:S(2)}) %collective-permute-start.4) | collective-permute-done | bytes 344096 | tf_op jit(solution)/shard_map/ppermute | solution.py:321
  64.7 3.9 %collective-permute-done.7 = bf16[224,384]{1,0:T(8,128)(2,1)S(1)} collective-permute-done((bf16[224,384]{1,0:T(8,128)(2,1)S(1)}, bf16[224,384]{1,0:T(8,128)(2,1)S(1)}, u32[]{:S(2)}, u32[]{:S(2)}) %collective-permute-start.7) | collective-permute-done | bytes 172064 | tf_op jit(solution)/shard_map/ppermute | solution.py:321
  70.0 6.3 %collective-permute-done.6 = bf16[224,384]{1,0:T(8,128)(2,1)} collective-permute-done((bf16[224,384]{1,0:T(8,128)(2,1)}, bf16[224,384]{1,0:T(8,128)(2,1)}, u32[]{:S(2)}, u32[]{:S(2)}) %collective-permute-start.6) | collective-permute-done | bytes 172064 | tf_op jit(solution)/shard_map/ppermute | solution.py:321
  76.3 10.6 %shard_map.96 = (bf16[4,4,256,128]{3,2,1,0:T(8,128)(2,1)}, f32[4,256,128]{2,1,0:T(8,128)}, bf16[8,128,3584]{2,1,0:T(8,128)(2,1)}, bf16[8,112,128]{2,1,0:T(8,128)(2,1)}) custom-call(s32[3]{0:T(128)} %pad_add_fusion.ids, bf16[4,8,112,128]{3,2,1,0:T(8,128)(2,1)} %bitcast.33, bf16[4,112,384]{2,1,0:T(8,128)(2,1)} %bitcast.32, bf16[4,112,384]{2,1,0:T(8,128)(2,1)} %bitcast.38, ...), custom_call_target="tpu_custom_call" | custom-call | tf_op jit(solution)/shard_map/pallas_call | solution.py:37
  87.0 13.4 %all_to_all.35.got = bf16[8,112,128]{2,1,0:T(8,128)(2,1)S(1)} all-to-all(bf16[8,112,128]{2,1,0:T(8,128)(2,1)} %get-tuple-element.12), channel_id=1, replica_groups=mesh['y'=4,'z'=8,'c'=2,'x'=4] {'z'}, dimensions={0} | all-to-all | bytes 458752 | tf_op jit(solution)/shard_map/all_to_all | solution.py:379
  100.5 12.8 %all_to_all.36.s_in = bf16[8,96,128]{2,1,0:T(8,128)(2,1)} all-to-all(bf16[8,96,128]{2,1,0:T(8,128)(2,1)S(1)} %get-tuple-element.13), channel_id=1, replica_groups=mesh['y'=4,'z'=8,'c'=2,'x'=4] {'z'}, dimensions={0} | all-to-all | bytes 393216 | tf_op jit(solution)/shard_map/all_to_all | solution.py:381
  113.3 8.3 %shard_map.98 = (bf16[8,80,128]{2,1,0:T(8,128)(2,1)}, f32[4,2,256,128]{3,2,1,0:T(8,128)}) custom-call(bf16[8,96,128]{2,1,0:T(8,128)(2,1)} %all_to_all.36.s_in, bf16[2,128,128]{2,1,0:T(8,128)(2,1)} %pad_maximum_fusion.rest_19_.lift, f32[4,256]{1,0:T(4,128)} %add.26.rest_20_.logs, bf16[4,4,256,128]{3,2,1,0:T(8,128)(2,1)} %get-tuple-element.14.kvql_hbm, ...), custom_call_target="tpu_custom_call" | custom-call | tf_op jit(solution)/shard_map/pallas_call | solution.py:37
  121.7 12.7 %all_to_all.37.got = bf16[8,80,128]{2,1,0:T(8,128)(2,1)S(1)} all-to-all(bf16[8,80,128]{2,1,0:T(8,128)(2,1)} %get-tuple-element.16), channel_id=1, replica_groups=mesh['y'=4,'z'=8,'c'=2,'x'=4] {'z'}, dimensions={0} | all-to-all | bytes 327680 | tf_op jit(solution)/shard_map/all_to_all | solution.py:398
  134.5 12.5 %all_to_all.38.r_in = bf16[8,80,128]{2,1,0:T(8,128)(2,1)} all-to-all(bf16[8,80,128]{2,1,0:T(8,128)(2,1)S(1)} %shard_map.99), channel_id=1, replica_groups=mesh['y'=4,'z'=8,'c'=2,'x'=4] {'z'}, dimensions={0} | all-to-all | bytes 327680 | tf_op jit(solution)/shard_map/all_to_all | solution.py:400
  147.0 7.9 %shard_map.100 = (f32[16,112,128]{2,1,0:T(8,128)}, bf16[16,112,128]{2,1,0:T(8,128)(2,1)}) custom-call(s32[3]{0:T(128)} %pad_add_fusion.ids, bf16[8,80,128]{2,1,0:T(8,128)(2,1)} %all_to_all.38.r_in, bf16[2,128,128]{2,1,0:T(8,128)(2,1)} %pad_maximum_fusion.rest_19_.lift, f32[4,256]{1,0:T(4,128)} %add.26.rest_20_.logs, ...), custom_call_target="tpu_custom_call" | custom-call | tf_op jit(solution)/shard_map/pallas_call | solution.py:37
  155.0 2.0 %collective-permute-done.17.b = bf16[16,112,128]{2,1,0:T(8,128)(2,1)S(1)} collective-permute-done((bf16[16,112,128]{2,1,0:T(8,128)(2,1)}, bf16[16,112,128]{2,1,0:T(8,128)(2,1)S(1)}, u32[]{:S(2)}, u32[]{:S(2)}) %collective-permute-start.17) | collective-permute-done | bytes 458784 | tf_op jit(solution)/shard_map/ppermute | solution.py:322
  157.0 1.2 copy-done
  159.0 4.8 %all-to-all-start.5 = ((bf16[16,112,128]{2,1,0:T(8,128)(2,1)}), bf16[16,112,128]{2,1,0:T(8,128)(2,1)S(1)}, u32[]{:S(2)}, u32[]{:S(2)}) async-start(bf16[16,112,128]{2,1,0:T(8,128)(2,1)} %shard_map.101), calls=%async_computation.5 | async-start | bytes 917504 | tf_op jit(solution)/shard_map/all_to_all | solution.py:424
  164.6 1.2 collective-permute-done.18.other
  165.8 3.1 %collective-permute-start.21 = (bf16[2,128,128]{2,1,0:T(8,128)(2,1)S(1)}, bf16[2,128,128]{2,1,0:T(8,128)(2,1)S(1)}, u32[]{:S(2)}, u32[]{:S(2)}) collective-permute-start(bf16[2,128,128]{2,1,0:T(8,128)(2,1)S(1)} %pad_maximum_fusion.1), channel_id=1, source_target_pairs={{0,128},{64,192},{128,0},{192,64},{1,129},{65,193},{129,1},{193,65... | collective-permute-start | bytes 196616 | tf_op jit(solution)/shard_map/ppermute | solution.py:321
  170.9 2.8 %all-to-all-done.5.got = bf16[16,112,128]{2,1,0:T(8,128)(2,1)S(1)} async-done(((bf16[16,112,128]{2,1,0:T(8,128)(2,1)}), bf16[16,112,128]{2,1,0:T(8,128)(2,1)S(1)}, u32[]{:S(2)}, u32[]{:S(2)}) %all-to-all-start.5) | async-done | bytes 458784 | tf_op jit(solution)/shard_map/all_to_all | solution.py:424
  174.4 3.3 %all-to-all-start.6 = ((bf16[8,16,128]{2,1,0:T(8,128)(2,1)}), bf16[8,16,128]{2,1,0:T(8,128)(2,1)S(1)}, u32[]{:S(2)}, u32[]{:S(2)}) async-start(bf16[8,16,128]{2,1,0:T(8,128)(2,1)} %shard_map.102), calls=%async_computation.6 | async-start | bytes 65536 | tf_op jit(solution)/shard_map/all_to_all | solution.py:429
  177.8 1.4 shard_map.104
  179.2 6.5 %all-to-all-done.6.got = bf16[8,16,128]{2,1,0:T(8,128)(2,1)S(1)} async-done(((bf16[8,16,128]{2,1,0:T(8,128)(2,1)}), bf16[8,16,128]{2,1,0:T(8,128)(2,1)S(1)}, u32[]{:S(2)}, u32[]{:S(2)}) %all-to-all-start.6) | async-done | bytes 32800 | tf_op jit(solution)/shard_map/all_to_all | solution.py:429
  (72 shorter events, 13.2 us)
Async XLA Ops:
  2.7 16.6 %all-to-all-start = ((bf16[8,104,384]{2,1,0:T(8,128)(2,1)}), bf16[8,104,384]{2,1,0:T(8,128)(2,1)S(1)}, u32[]{:S(2)}, u32[]{:S(2)}) async-start(bf16[8,104,384]{2,1,0:T(8,128)(2,1)} %shard_map.95), calls=%async_computation | async-start | bytes 1277952 | tf_op jit(solution)/shard_map/all_to_all | solution.py:340
  7.2 37.6 %collective-permute-start.9 = (bf16[128,3584]{1,0:T(8,128)(2,1)}, bf16[128,3584]{1,0:T(8,128)(2,1)S(1)}, u32[]{:S(2)}, u32[]{:S(2)}) collective-permute-start(bf16[128,3584]{1,0:T(8,128)(2,1)} %rest_9_.1), channel_id=1, source_target_pairs={{0,64},{64,128},{128,192},{192,0},{1,65},{65,129},{129,193},{193,1... | collective-permute-start | bytes 2752520 | tf_op jit(solution)/shard_map/ppermute | solution.py:321
  9.2 37.0 %collective-permute-start.11 = (bf16[128,3584]{1,0:T(8,128)(2,1)}, bf16[128,3584]{1,0:T(8,128)(2,1)S(1)}, u32[]{:S(2)}, u32[]{:S(2)}) collective-permute-start(bf16[128,3584]{1,0:T(8,128)(2,1)} %rest_9_.1), channel_id=1, source_target_pairs={{0,192},{64,0},{128,64},{192,128},{1,193},{65,1},{129,65},{193,129... | collective-permute-start | bytes 2752520 | tf_op jit(solution)/shard_map/ppermute | solution.py:321
  19.4 67.6 %copy-start.2 = (bf16[8,104,384]{2,1,0:T(8,128)(2,1)}, bf16[8,104,384]{2,1,0:T(8,128)(2,1)S(1)}, u32[]{:S(2)}) copy-start(bf16[8,104,384]{2,1,0:T(8,128)(2,1)S(1)} %all-to-all-done.bundle_hbm) | copy-start | bytes 1916932
  19.4 56.9 %copy-start.5 = (bf16[8,56,384]{2,1,0:T(8,128)(2,1)}, bf16[8,56,384]{2,1,0:T(8,128)(2,1)S(1)}, u32[]{:S(2)}) copy-start(bf16[8,56,384]{2,1,0:T(8,128)(2,1)S(1)} %slice.48) | copy-start | bytes 1032196
  19.4 12.4 %collective-permute-start.1 = (bf16[448,384]{1,0:T(8,128)(2,1)S(1)}, bf16[448,384]{1,0:T(8,128)(2,1)S(1)}, u32[]{:S(2)}, u32[]{:S(2)}) collective-permute-start(bf16[448,384]{1,0:T(8,128)(2,1)S(1)} %bitcast.30), channel_id=1, source_target_pairs={{0,56},{8,0},{16,8},{24,16},{32,24},{40,32},{48,40},{56,48},{1,57}... | collective-permute-start | bytes 1032200 | tf_op jit(solution)/shard_map/ppermute | solution.py:321
  25.4 24.4 %collective-permute-start.8 = (bf16[128,3584]{1,0:T(8,128)(2,1)}, bf16[128,3584]{1,0:T(8,128)(2,1)S(1)}, u32[]{:S(2)}, u32[]{:S(2)}) collective-permute-start(bf16[128,3584]{1,0:T(8,128)(2,1)} %rest_9_.1), channel_id=1, source_target_pairs={{0,4},{4,0},{1,5},{5,1},{2,6},{6,2},{3,7},{7,3},{8,12},{12,8},{9,1... | collective-permute-start | bytes 2752520 | tf_op jit(solution)/shard_map/ppermute | solution.py:322
  25.4 11.7 %collective-permute-start = (bf16[448,384]{1,0:T(8,128)(2,1)S(1)}, bf16[448,384]{1,0:T(8,128)(2,1)S(1)}, u32[]{:S(2)}, u32[]{:S(2)}) collective-permute-start(bf16[448,384]{1,0:T(8,128)(2,1)S(1)} %bitcast.31), channel_id=1, source_target_pairs={{0,8},{8,16},{16,24},{24,32},{32,40},{40,48},{48,56},{56,0},{1,9},... | collective-permute-start | bytes 1032200 | tf_op jit(solution)/shard_map/ppermute | solution.py:321
  31.8 9.3 %collective-permute-start.3 = (bf16[448,384]{1,0:T(8,128)(2,1)S(1)}, bf16[448,384]{1,0:T(8,128)(2,1)S(1)}, u32[]{:S(2)}, u32[]{:S(2)}) collective-permute-start(bf16[448,384]{1,0:T(8,128)(2,1)S(1)} %collective-permute-done.1), channel_id=1, source_target_pairs={{0,56},{8,0},{16,8},{24,16},{32,24},{40,32},{48,40},{56,48},{1,57}... | collective-permute-start | bytes 1032200 | tf_op jit(solution)/shard_map/ppermute | solution.py:321
  37.1 13.7 %copy-start.10 = (bf16[448,384]{1,0:T(8,128)(2,1)}, bf16[448,384]{1,0:T(8,128)(2,1)S(1)}, u32[]{:S(2)}) copy-start(bf16[448,384]{1,0:T(8,128)(2,1)S(1)} %collective-permute-done) | copy-start | bytes 1032196
  37.1 13.7 %collective-permute-start.2 = (bf16[448,384]{1,0:T(8,128)(2,1)S(1)}, bf16[448,384]{1,0:T(8,128)(2,1)}, u32[]{:S(2)}, u32[]{:S(2)}) collective-permute-start(bf16[448,384]{1,0:T(8,128)(2,1)S(1)} %collective-permute-done), channel_id=1, source_target_pairs={{0,8},{8,16},{16,24},{24,32},{32,40},{40,48},{48,56},{56,0},{1,9},... | collective-permute-start | bytes 1032200 | tf_op jit(solution)/shard_map/ppermute | solution.py:321
  41.1 9.6 %collective-permute-start.5 = (bf16[448,384]{1,0:T(8,128)(2,1)S(1)}, bf16[448,384]{1,0:T(8,128)(2,1)S(1)}, u32[]{:S(2)}, u32[]{:S(2)}) collective-permute-start(bf16[448,384]{1,0:T(8,128)(2,1)S(1)} %collective-permute-done.3), channel_id=1, source_target_pairs={{0,56},{8,0},{16,8},{24,16},{32,24},{40,32},{48,40},{56,48},{1,57}... | collective-permute-start | bytes 1032200 | tf_op jit(solution)/shard_map/ppermute | solution.py:321
  44.8 31.5 %copy-start.3 = (bf16[128,3584]{1,0:T(8,128)(2,1)}, bf16[128,3584]{1,0:T(8,128)(2,1)S(1)}, u32[]{:S(2)}) copy-start(bf16[128,3584]{1,0:T(8,128)(2,1)S(1)} %collective-permute-done.9.rest_11_) | copy-start | bytes 2752516
  45.7 10.9 %collective-permute-start.13 = (bf16[64,3584]{1,0:T(8,128)(2,1)}, bf16[64,3584]{1,0:T(8,128)(2,1)}, u32[]{:S(2)}, u32[]{:S(2)}) collective-permute-start(bf16[64,3584]{1,0:T(8,128)(2,1)} %slice.51), channel_id=1, source_target_pairs={{0,64},{64,128},{128,192},{192,0},{1,65},{65,129},{129,193},{193,1... | collective-permute-start | bytes 1376264 | tf_op jit(solution)/shard_map/ppermute | solution.py:321
  46.2 30.1 %copy-start.4 = (bf16[128,3584]{1,0:T(8,128)(2,1)}, bf16[128,3584]{1,0:T(8,128)(2,1)S(1)}, u32[]{:S(2)}) copy-start(bf16[128,3584]{1,0:T(8,128)(2,1)S(1)} %collective-permute-done.11.rest_13_) | copy-start | bytes 2752516
  47.1 9.6 %collective-permute-start.15 = (bf16[64,3584]{1,0:T(8,128)(2,1)}, bf16[64,3584]{1,0:T(8,128)(2,1)}, u32[]{:S(2)}, u32[]{:S(2)}) collective-permute-start(bf16[64,3584]{1,0:T(8,128)(2,1)} %slice.52), channel_id=1, source_target_pairs={{0,192},{64,0},{128,64},{192,128},{1,193},{65,1},{129,65},{193,129... | collective-permute-start | bytes 1376264 | tf_op jit(solution)/shard_map/ppermute | solution.py:321
  49.8 26.4 %collective-permute-start.10 = (bf16[128,3584]{1,0:T(8,128)(2,1)S(1)}, bf16[128,3584]{1,0:T(8,128)(2,1)}, u32[]{:S(2)}, u32[]{:S(2)}) collective-permute-start(bf16[128,3584]{1,0:T(8,128)(2,1)S(1)} %collective-permute-done.9.rest_11_), channel_id=1, source_target_pairs={{0,4},{4,0},{1,5},{5,1},{2,6},{6,2},{3,7},{7,3},{8,12},{12,8},{9,1... | collective-permute-start | bytes 2752520 | tf_op jit(solution)/shard_map/ppermute | solution.py:322
  50.8 25.5 %collective-permute-start.12 = (bf16[128,3584]{1,0:T(8,128)(2,1)S(1)}, bf16[128,3584]{1,0:T(8,128)(2,1)}, u32[]{:S(2)}, u32[]{:S(2)}) collective-permute-start(bf16[128,3584]{1,0:T(8,128)(2,1)S(1)} %collective-permute-done.11.rest_13_), channel_id=1, source_target_pairs={{0,4},{4,0},{1,5},{5,1},{2,6},{6,2},{3,7},{7,3},{8,12},{12,8},{9,1... | collective-permute-start | bytes 2752520 | tf_op jit(solution)/shard_map/ppermute | solution.py:322
  50.8 25.5 %copy-start.7 = (bf16[448,384]{1,0:T(8,128)(2,1)}, bf16[448,384]{1,0:T(8,128)(2,1)S(1)}, u32[]{:S(2)}) copy-start(bf16[448,384]{1,0:T(8,128)(2,1)S(1)} %collective-permute-done.5) | copy-start | bytes 1032196
  50.8 12.0 %collective-permute-start.4 = (bf16[448,384]{1,0:T(8,128)(2,1)}, bf16[448,384]{1,0:T(8,128)(2,1)S(1)}, u32[]{:S(2)}, u32[]{:S(2)}) collective-permute-start(bf16[448,384]{1,0:T(8,128)(2,1)} %collective-permute-done.2), channel_id=1, source_target_pairs={{0,8},{8,16},{16,24},{24,32},{32,40},{40,48},{48,56},{56,0},{1,9},... | collective-permute-start | bytes 1032200 | tf_op jit(solution)/shard_map/ppermute | solution.py:321
  56.6 19.7 %collective-permute-start.14 = (bf16[64,3584]{1,0:T(8,128)(2,1)}, bf16[64,3584]{1,0:T(8,128)(2,1)}, u32[]{:S(2)}, u32[]{:S(2)}) collective-permute-start(bf16[64,3584]{1,0:T(8,128)(2,1)} %collective-permute-done.13.rest_15_), channel_id=1, source_target_pairs={{0,4},{4,0},{1,5},{5,1},{2,6},{6,2},{3,7},{7,3},{8,12},{12,8},{9,1... | collective-permute-start | bytes 1376264 | tf_op jit(solution)/shard_map/ppermute | solution.py:322
  56.8 19.5 %collective-permute-start.16 = (bf16[64,3584]{1,0:T(8,128)(2,1)}, bf16[64,3584]{1,0:T(8,128)(2,1)}, u32[]{:S(2)}, u32[]{:S(2)}) collective-permute-start(bf16[64,3584]{1,0:T(8,128)(2,1)} %collective-permute-done.15.rest_17_), channel_id=1, source_target_pairs={{0,4},{4,0},{1,5},{5,1},{2,6},{6,2},{3,7},{7,3},{8,12},{12,8},{9,1... | collective-permute-start | bytes 1376264 | tf_op jit(solution)/shard_map/ppermute | solution.py:322
  62.7 5.9 %collective-permute-start.7 = (bf16[224,384]{1,0:T(8,128)(2,1)S(1)}, bf16[224,384]{1,0:T(8,128)(2,1)S(1)}, u32[]{:S(2)}, u32[]{:S(2)}) collective-permute-start(bf16[224,384]{1,0:T(8,128)(2,1)S(1)} %slice.50), channel_id=1, source_target_pairs={{0,56},{8,0},{16,8},{24,16},{32,24},{40,32},{48,40},{56,48},{1,57}... | collective-permute-start | bytes 516104 | tf_op jit(solution)/shard_map/ppermute | solution.py:321
  69.3 6.9 %collective-permute-start.6 = (bf16[224,384]{1,0:T(8,128)(2,1)}, bf16[224,384]{1,0:T(8,128)(2,1)}, u32[]{:S(2)}, u32[]{:S(2)}) collective-permute-start(bf16[224,384]{1,0:T(8,128)(2,1)} %slice.49), channel_id=1, source_target_pairs={{0,8},{8,16},{16,24},{24,32},{32,40},{40,48},{48,56},{56,0},{1,9},... | collective-permute-start | bytes 516104 | tf_op jit(solution)/shard_map/ppermute | solution.py:321
  121.7 56.1 %copy-start.1 = (s32[3]{0:T(128)S(1)}, s32[3]{0:T(128)}, u32[]{:S(2)}) copy-start(s32[3]{0:T(128)} %pad_add_fusion.ids) | copy-start | bytes 40
  154.9 2.1 %collective-permute-start.17 = (bf16[16,112,128]{2,1,0:T(8,128)(2,1)}, bf16[16,112,128]{2,1,0:T(8,128)(2,1)S(1)}, u32[]{:S(2)}, u32[]{:S(2)}) collective-permute-start(bf16[16,112,128]{2,1,0:T(8,128)(2,1)} %get-tuple-element.21), channel_id=1, source_target_pairs={{0,4},{4,0},{1,5},{5,1},{2,6},{6,2},{3,7},{7,3},{8,12},{12,8},{9,1... | collective-permute-start | bytes 1376264 | tf_op jit(solution)/shard_map/ppermute | solution.py:322
  159.0 14.7 %all-to-all-start.5 = ((bf16[16,112,128]{2,1,0:T(8,128)(2,1)}), bf16[16,112,128]{2,1,0:T(8,128)(2,1)S(1)}, u32[]{:S(2)}, u32[]{:S(2)}) async-start(bf16[16,112,128]{2,1,0:T(8,128)(2,1)} %shard_map.101), calls=%async_computation.5 | async-start | bytes 917504 | tf_op jit(solution)/shard_map/all_to_all | solution.py:424
  164.6 1.2 collective-permute-start.18
  165.8 11.9 %collective-permute-start.21 = (bf16[2,128,128]{2,1,0:T(8,128)(2,1)S(1)}, bf16[2,128,128]{2,1,0:T(8,128)(2,1)S(1)}, u32[]{:S(2)}, u32[]{:S(2)}) collective-permute-start(bf16[2,128,128]{2,1,0:T(8,128)(2,1)S(1)} %pad_maximum_fusion.1), channel_id=1, source_target_pairs={{0,128},{64,192},{128,0},{192,64},{1,129},{65,193},{129,1},{193,65... | collective-permute-start | bytes 196616 | tf_op jit(solution)/shard_map/ppermute | solution.py:321
  168.9 8.9 %collective-permute-start.20 = (bf16[2,128,128]{2,1,0:T(8,128)(2,1)S(1)}, bf16[2,128,128]{2,1,0:T(8,128)(2,1)S(1)}, u32[]{:S(2)}, u32[]{:S(2)}) collective-permute-start(bf16[2,128,128]{2,1,0:T(8,128)(2,1)S(1)} %pad_maximum_fusion.1), channel_id=1, source_target_pairs={{0,192},{64,0},{128,64},{192,128},{1,193},{65,1},{129,65},{193,129... | collective-permute-start | bytes 196616 | tf_op jit(solution)/shard_map/ppermute | solution.py:321
  170.1 7.7 %collective-permute-start.19 = (bf16[2,128,128]{2,1,0:T(8,128)(2,1)S(1)}, bf16[2,128,128]{2,1,0:T(8,128)(2,1)S(1)}, u32[]{:S(2)}, u32[]{:S(2)}) collective-permute-start(bf16[2,128,128]{2,1,0:T(8,128)(2,1)S(1)} %pad_maximum_fusion.1), channel_id=1, source_target_pairs={{0,64},{64,128},{128,192},{192,0},{1,65},{65,129},{129,193},{193,1... | collective-permute-start | bytes 196616 | tf_op jit(solution)/shard_map/ppermute | solution.py:321
  174.4 11.3 %all-to-all-start.6 = ((bf16[8,16,128]{2,1,0:T(8,128)(2,1)}), bf16[8,16,128]{2,1,0:T(8,128)(2,1)S(1)}, u32[]{:S(2)}, u32[]{:S(2)}) async-start(bf16[8,16,128]{2,1,0:T(8,128)(2,1)} %shard_map.102), calls=%async_computation.6 | async-start | bytes 65536 | tf_op jit(solution)/shard_map/all_to_all | solution.py:429
  (6 other events, 35.4 us)

commit v4 on v3

--- a/solution.py
+++ b/solution.py
@@ -168,114 +168,128 @@
 
 def scan_bwd_kernel(got, gains, out):
     nz, ny = got.shape[0], 4
-    state = jnp.zeros((16, 128), f32)
+    state = jnp.zeros((8, 128), f32)
     for y in reversed(range(ny)):
         for z in reversed(range(nz)):
-            out[z, 16 * y : 16 * y + 16, :] = state.astype(bf16)
-            state = gains[y * nz + z][None] * state + got[z, 16 * y : 16 * y + 16, :].astype(f32)
-    up = jnp.sum(got[:, 64:80, :].astype(f32), axis=0).astype(bf16)
-    out[:, 64:80, :] = jnp.broadcast_to(up[None], (nz, 16, 128))
+            out[z, 8 * y : 8 * y + 8, :] = state.astype(bf16)
+            state = gains[y * nz + z][None] * state + got[z, 8 * y : 8 * y + 8, :].astype(f32)
+    up = jnp.sum(got[:, 32:48, :].astype(f32), axis=0).astype(bf16)
+    out[:, 32:48, :] = jnp.broadcast_to(up[None], (nz, 16, 128))
 
 
 def attn_kernel(s_in, lift, logs, kvql_hbm, qpre_hbm, bundle_hbm, send, back_hbm, kvql, qpre, bundle, back, sems):
     ny = kvql.shape[0]
-    copies = []
-    for n in range(ny):
-        copies += begin(
-            [
-                (kvql_hbm.at[n], kvql.at[n]),
-                (qpre_hbm.at[n], qpre.at[n]),
-                (bundle_hbm.at[2 * n : 2 * n + 2, 0:48, :], bundle.at[2 * n : 2 * n + 2]),
-            ],
-            sems,
-            3 * n,
-        )
-    total_q = jnp.zeros((128, 128), f32)
-    total_v = jnp.zeros((128, 128), f32)
-    cross = jnp.zeros((64, 128), f32)
-    stores = []
+    copies = begin(
+        [(kvql_hbm, kvql), (bundle_hbm.at[:, 0:48, :], bundle), (qpre_hbm, qpre)], sems
+    )
     cum = running(logs[...])
     square = (cum.shape[1], cum.shape[1])
     causal = lax.broadcasted_iota(jnp.int32, square, 1) <= lax.broadcasted_iota(jnp.int32, square, 0)
-    for n in range(ny):
-        s = s_in[:, n * 16 : n * 16 + 16, :].reshape(128, 128)
-        side = s_in[:, 64 + n * 8 : 72 + n * 8, :].astype(f32).reshape(64, 128).astype(bf16)
+    every = range(ny)
+    ahead, dec = [], []
+    for n in every:
         sums = down_rows(cum[n : n + 1, :])
-        ahead = jnp.exp(sums)
+        ahead.append(jnp.exp(sums))
         spread = jnp.concatenate([sums, sums], axis=1) - cum[n : n + 1, :]
-        dec = jnp.where(causal, jnp.exp(jnp.where(causal, spread, 0.0)), 0.0)
-        for copy in copies[3 * n : 3 * n + 3]:
-            copy.wait()
-        k, v, q, low = (kvql[n, i] for i in range(4))
-        mixed = (dot_t(q, k) * dec).astype(bf16)
-        attn = dot(mixed, v) + ahead * dot(q, s)
-        inv = lax.rsqrt(jnp.mean(attn * attn, axis=-1, keepdims=True) + eps_norm)
-        normed = attn * inv
+        dec.append(jnp.where(causal, jnp.exp(jnp.where(causal, spread, 0.0)), 0.0))
+    s = [s_in[:, n * 16 : n * 16 + 16, :].reshape(128, 128) for n in every]
+    side = [
+        s_in[:, 64 + n * 8 : 72 + n * 8, :].astype(f32).reshape(64, 128).astype(bf16) for n in every
+    ]
+    copies[0].wait()
+    k, v, q, low = ([kvql[n, i] for n in every] for i in range(4))
+    mixed = [(dot_t(q[n], k[n]) * dec[n]).astype(bf16) for n in every]
+    attn = [dot(mixed[n], v[n]) + ahead[n] * dot(q[n], s[n]) for n in every]
+    copies[1].wait()
+    d = []
+    for n in every:
+        inv = lax.rsqrt(jnp.mean(attn[n] * attn[n], axis=-1, keepdims=True) + eps_norm)
+        normed = attn[n] * inv
         parts = []
         for b in (2 * n, 2 * n + 1):
             parts += [bundle[b, :, 0:128], bundle[b, :, 128:256], bundle[b, 0:32, 256:384]]
         up = jnp.concatenate(parts, axis=0).astype(f32)
-        d = (up - normed * jnp.mean(up * normed, axis=-1, keepdims=True)) * inv
-        d = d.astype(bf16)
-        carried = t_dot((q.astype(f32) * ahead).astype(bf16), d).astype(bf16)
-        send[:, n * 16 : n * 16 + 16, :] = carried.reshape(-1, 16, 128)
-        cross += dot(side, carried)
-        dm = (dot_t(d, v) * dec).astype(bf16)
-        dq = dot(dm, k) + ahead * dot_t(d, s)
+        dn = (up - normed * jnp.mean(up * normed, axis=-1, keepdims=True)) * inv
+        d.append(dn.astype(bf16))
+    carried = [t_dot((q[n].astype(f32) * ahead[n]).astype(bf16), d[n]).astype(bf16) for n in every]
+    dm = [(dot_t(d[n], v[n]) * dec[n]).astype(bf16) for n in every]
+    cross = sum(dot(side[n], carried[n]) for n in every)
+    for n in every:
+        image = dot_t(lift[1], carried[n])[64:].reshape(-1, 8, 128)
+        send[:, n * 8 : n * 8 + 8, :] = image.astype(bf16)
+    dv = [t_dot(mixed[n], d[n]).astype(bf16) for n in every]
+    dq = [dot(dm[n], k[n]) + ahead[n] * dot_t(d[n], s[n]) for n in every]
+    copies[2].wait()
+    for n in every:
         u = qpre[n]
         sig = jax.nn.sigmoid(u)
-        dq = (dq * (sig * (1.0 + u * (1.0 - sig)))).astype(bf16)
-        total_q += t_dot(low, dq)
-        dv = t_dot(mixed, d)
-        total_v += t_dot(low, dv.astype(bf16))
-        back[n, 0] = dv
-        back[n, 1] = adapter_scale * dot_t(dq, lift[0])
-        stores += begin([(back.at[n], back_hbm.at[n])], sems, 12 + n)
+        dq[n] = (dq[n] * (sig * (1.0 + u * (1.0 - sig)))).astype(bf16)
+    for n in every:
+        back[n] = adapter_scale * (dot_t(dq[n], lift[0]) + dot_t(dv[n], lift[1]))
+    store = begin([(back, back_hbm)], sems, 3)[0]
+    total_q = sum(t_dot(low[n], dq[n]) for n in every)
+    total_v = sum(t_dot(low[n], dv[n]) for n in every)
     up = adapter_scale * jnp.concatenate([total_q[:64], total_v[64:] + cross], axis=0)
-    send[:, 64:80, :] = up.astype(bf16).reshape(-1, 16, 128)
-    for copy in stores:
+    send[:, 32:48, :] = up.astype(bf16).reshape(-1, 16, 128)
+    store.wait()
+
+
+def final_kernel(ids, r_in, logs, kvql_hbm, back_hbm, tok_hbm, keep, give, k, back, tok, acc, terms, sems):
+    ny = k.shape[0]
+    blocks, own, width = tok.shape
+    copies = begin([(kvql_hbm.at[:, 0], k), (back_hbm, back)], sems)
+    parts = begin([(tok_hbm.at[b], tok.at[b]) for b in range(blocks)], sems, 2)
+    cum = running(logs[...])
+    tails = []
+    for n in range(ny):
+        sums = down_rows(cum[n : n + 1, :])
+        tails.append(adapter_scale * jnp.exp(sums[255:256, :] - sums))
+    rs = []
+    for n in range(ny):
+        r = r_in[:, n * 8 : n * 8 + 8, :].astype(f32).reshape(64, 128)
+        rs.append(jnp.concatenate([jnp.zeros((64, 128), f32), r], axis=0).astype(bf16))
+    up = r_in[:, 32:48, :].reshape(128, 128)
+    give[16] = up[:112]
+    give[17, :16] = up[112:]
+    give[17, 16:] = jnp.zeros((96, 128), bf16)
+    for copy in copies:
         copy.wait()
-
-
-def final_kernel(ids, r_in, lift, logs, kvql_hbm, back_hbm, tok_hbm, keep, give, k, back, tok, dlow, terms, sems):
-    ny = k.shape[0]
-    wide = 512
-    blocks = tok.shape[2] // wide
-    copies = []
-    for n in range(ny):
-        copies += begin([(kvql_hbm.at[n, 0], k.at[n]), (back_hbm.at[n], back.at[n])], sems, 2 * n)
-    lanes = [slice(m * wide, m * wide + wide) for m in range(blocks)]
-    parts = begin([(tok_hbm.at[:, :, m], tok.at[:, :, m]) for m in lanes], sems, 2 * ny)
-    cum = running(logs[...])
-    for n in range(ny):
-        rows = slice(n * 256, n * 256 + 256)
-        sums = down_rows(cum[n : n + 1, :])
-        tail = jnp.exp(sums[255:256, :] - sums)
-        r = r_in[:, n * 16 : n * 16 + 16, :].reshape(128, 128)
-        copies[2 * n].wait()
-        copies[2 * n + 1].wait()
-        d = (back[n, 0] + tail * dot(k[n], r)).astype(bf16)
-        dlow[rows, :] = back[n, 1] + adapter_scale * dot_t(d, lift[1])
-    small = dlow[...].T.astype(bf16)
-    tokens = tok.shape[0] * tok.shape[1]
-    for m, part in zip(lanes, parts):
-        part.wait()
-        terms[m, :] = dot(small, tok[:, :, m].reshape(tokens, wide)).T
+    small = [(back[n] + tails[n] * dot_t(k[n], rs[n])).T.astype(bf16) for n in range(ny)]
+    small = [jnp.concatenate(small[i : i + 2], axis=1) for i in (0, 2)]
+    half = blocks // 2
+    wide = width // 4
     per = keep.shape[1] // 8
     first = ids[1] == 0
-    for b in range(16):
-        y, x = b // 4, b % 4
-        halves = []
-        for c in range(2):
-            base = ((y * 16 + c) * 4 + x) * per
-            rows = [terms[pl.ds(base + r, 8, stride=8 * per), :] for r in range(per)]
-            halves.append(jnp.concatenate(rows, axis=0))
-        keep[b] = jnp.where(first, halves[0], halves[1])
-        give[b] = jnp.where(first, halves[1], halves[0]).astype(bf16)
-
-
-def add_kernel(a, b, out):
-    out[...] = (a[...] + b[...].astype(f32)).astype(bf16)
+    for part in parts[:half]:
+        part.wait()
+    for y in range(4):
+        m = slice(y * wide, y * wide + wide)
+        acc[:, m] = dot(small[0], tok[:half, :, m].reshape(half * own, wide))
+    for part in parts[half:]:
+        part.wait()
+    for y in range(4):
+        m = slice(y * wide, y * wide + wide)
+        terms[m, :] = (acc[:, m] + dot(small[1], tok[half:, :, m].reshape(half * own, wide))).T
+        for x in range(4):
+            halves = []
+            for c in range(2):
+                base = ((y * 16 + c) * 4 + x) * per
+                rows = [terms[pl.ds(base + r, 8, stride=8 * per), :] for r in range(per)]
+                halves.append(jnp.concatenate(rows, axis=0))
+            b = y * 4 + x
+            keep[b] = jnp.where(first, halves[0], halves[1])
+            give[b] = jnp.where(first, halves[1], halves[0]).astype(bf16)
+
+
+def add_kernel(keep_hbm, give, got, out, pair, keep, sems):
+    copies = begin([(keep_hbm.at[4 * i : 4 * i + 4], keep.at[4 * i : 4 * i + 4]) for i in range(4)], sems)
+    for i, ref in enumerate((give, got)):
+        pair[i, :112] = ref[16]
+        pair[i, 112:] = ref[17, :16]
+    for i, copy in enumerate(copies):
+        copy.wait()
+        rows = slice(4 * i, 4 * i + 4)
+        out[rows] = (keep[rows] + got[rows].astype(f32)).astype(bf16)
 
 
 def fold_kernel(got, out, tmp):
@@ -292,15 +306,15 @@
     out[...] = jnp.sum(got[...].astype(f32), axis=0)[: out.shape[0]]
 
 
-def up_kernel(ids, own, other, *rest):
+def up_kernel(ids, pair, *rest):
     pieces, out = rest[:-1], rest[-1]
     y, c = ids[0], ids[1]
 
     def put(yy, cc, val):
         out[:, pl.ds(pl.multiple_of((yy * 2 + cc) * 128, 128), 128)] = val.astype(f32)
 
-    put(y, c, own[...])
-    put(y, 1 - c, other[...])
+    put(y, c, pair[0])
+    put(y, 1 - c, pair[1])
     for i, rel in enumerate((3, 1, 2)):
         yy = lax.rem(y + rel, 4)
         put(yy, c, pieces[i][0])
@@ -382,7 +396,7 @@
 
     send, back = call(
         attn_kernel,
-        (shape((nz, 80, hk)), shape((ny, 2, span, hk), f32)),
+        (shape((nz, 48, hk)), shape((ny, span, hk), f32)),
         s_in, lift, logs, kvql, qpre, bundle,
         mib=60,
         specs=[VMEM] * 3 + [HBM] * 3,
@@ -391,36 +405,41 @@
             pltpu.VMEM((ny, 4, span, hk), bf16),
             pltpu.VMEM((ny, span, hk), f32),
             pltpu.VMEM((heads, 48, 3 * hk), bf16),
-            pltpu.VMEM((ny, 2, span, hk), f32),
-            DMA((16,)),
+            pltpu.VMEM((ny, span, hk), f32),
+            DMA((4,)),
         ],
     )
     got = lax.all_to_all(send, "z", 0, 0, tiled=True)
-    scanned = call(scan_bwd_kernel, shape((nz, 80, hk)), got, gains)
+    scanned = call(scan_bwd_kernel, shape((nz, 48, hk)), got, gains)
     r_in = lax.all_to_all(scanned, "z", 0, 0, tiled=True)
-
-    up = r_in[:, 64:80].reshape(2 * rank, hk)
-    up_other = swap(up)
-    pair = jnp.stack([up, up_other])
-    ups = [ring(pair, 1), ring(pair, -1), ring(pair, 2)]
 
     out_rows = width // (ny * nz * nc * nx)
     keep, give = call(
         final_kernel,
-        (shape((ny * nx, nz * out_rows, hk), f32), shape((ny * nx, nz * out_rows, hk))),
-        ids, r_in, lift, logs, kvql, back, tok,
-        specs=[SMEM] + [VMEM] * 3 + [HBM] * 3,
+        (
+            shape((ny * nx, nz * out_rows, hk), f32),
+            shape((ny * nx + 2, nz * out_rows, hk)),
+        ),
+        ids, r_in, logs, kvql, back, tok,
+        specs=[SMEM] + [VMEM] * 2 + [HBM] * 3,
         scratch=[
             pltpu.VMEM((ny, span, hk), bf16),
-            pltpu.VMEM((ny, 2, span, hk), f32),
+            pltpu.VMEM((ny, span, hk), f32),
             pltpu.VMEM((heads, own, width), bf16),
-            pltpu.VMEM((heads * own, 2 * rank), f32),
+            pltpu.VMEM((2 * rank, width), f32),
             pltpu.VMEM((width, 2 * rank), f32),
-            DMA((16,)),
+            DMA((10,)),
         ],
         mib=60,
     )
-    down_terms = call(add_kernel, shape(give.shape), keep, swap(give))
+    down_terms, pair = call(
+        add_kernel,
+        (shape(keep.shape), shape((2, 2 * rank, hk))),
+        keep, give, swap(give),
+        specs=[HBM, VMEM, VMEM],
+        scratch=[pltpu.VMEM(keep.shape, f32), DMA((4,))],
+    )
+    ups = [ring(pair, 1), ring(pair, -1), ring(pair, 2)]
     down_terms = lax.all_to_all(down_terms, ("y", "x"), 0, 0, tiled=True)
     down_terms = call(
         fold_kernel, shape((nz, 16, hk)), down_terms,
@@ -429,8 +448,8 @@
     down_terms = lax.all_to_all(down_terms, "z", 0, 0, tiled=True)
     grad_down = call(last_kernel, shape((out_rows, hk), f32), down_terms)
     grad_up = call(
-        up_kernel, shape((2 * rank, heads * hk), f32), ids, up, up_other, *ups,
-        specs=[SMEM] + [VMEM] * 5,
+        up_kernel, shape((2 * rank, heads * hk), f32), ids, pair, *ups,
+        specs=[SMEM] + [VMEM] * 4,
     )
     return (grad_down, grad_up.reshape(2, rank, heads * hk))
 

time: 187 us -> 184 us (0.984)
  Pallas kernels: 32.7 us -> 30.3 us
    pallas_call x10, Pallas kernels: 32.7 us -> 30.3 us  [call(): pl.pallas_call(kernel, out_shape=outs, in_specs=specs or [VMEM] * len(arg...]
    all_to_all x1, waiting for transfers between devices: 2.81 us -> 4.88 us  [layer(): down_terms = lax.all_to_all(down_terms, ('y', 'x'), 0, 0, tiled=True)]
    unnamed x26 -> x28, local copies, waits for them, and re-layouts: 2.82 us -> 3.84 us
  transfers between devices with their start and end apart: 25 -> 24, of which waited for: 13 -> 12; matrix products, arithmetic and copies ran while one was open for 3% -> 3% of each run, Pallas kernels for 1% -> 1%
where the time goes in v4:
time: 184 us
  waiting for transfers between devices  55.3 us (30%)
  blocking collectives  50.1 us (27%)
  starting transfers between devices  38 us (21%)
  Pallas kernels  30.3 us (16%)
  local copies, waits for them, and re-layouts  7.66 us (4%)
    ppermute x15, waiting for transfers between devices, layer(): lax.ppermute(v, a, [(i, (i + s) % n) for i in range(n)])  32.9 us
    pallas_call x10, Pallas kernels, call(): pl.pallas_call(kernel, out_shape=outs, in_specs=specs or [VMEM] * len(arg...  30.3 us
    all_to_all x2, blocking collectives, layer(): got = lax.all_to_all(send, 'z', 0, 0, tiled=True)  25.4 us
    ppermute x15, starting transfers between devices, layer(): lax.ppermute(v, a, [(i, (i + s) % n) for i in range(n)])  24.9 us
    all_to_all x1, blocking collectives, layer(): s_in = lax.all_to_all(scanned, 'z', 0, 0, tiled=True)  12.8 us
    all_to_all x1, blocking collectives, layer(): r_in = lax.all_to_all(scanned, 'z', 0, 0, tiled=True)  11.8 us
    all_to_all x1, waiting for transfers between devices, layer(): bundle = lax.all_to_all(bundle, group, 0, 0, tiled=True)  8.91 us
    all_to_all x1, waiting for transfers between devices, layer(): down_terms = lax.all_to_all(down_terms, 'z', 0, 0, tiled=True)  6.51 us
  transfers between devices with their start and end apart: 24, of which 12 were waited for; matrix products, arithmetic and copies ran while one was open for 3% of the time, Pallas kernels for 1%

profile of v4, /device:TPU:2, one launch (start us, length us, event | category | flops | bytes accessed | tf_op | source)
XLA Modules:
  0.0 183.6 jit_solution(5713674978171565036)
XLA Ops:
  0.6 2.1 %shard_map.95 = bf16[8,104,384]{2,1,0:T(8,128)(2,1)} custom-call(bf16[56,1024]{1,0:T(8,128)(2,1)} %a_hbm.1, bf16[56,1024]{1,0:T(8,128)(2,1)} %b_hbm.1, bf16[56,1024]{1,0:T(8,128)(2,1)} %c_hbm.1, bf16[128,1024]{1,0:T(8,128)(2,1)} %grad_hbm.1, f32[8,128]{1,0:T(8,128)} %decay_hbm.1), custom_call_target="tpu_custom_call" | custom-call | tf_op jit(solution)/shard_map/pallas_call | solution.py:37
  2.7 4.5 %all-to-all-start = ((bf16[8,104,384]{2,1,0:T(8,128)(2,1)}), bf16[8,104,384]{2,1,0:T(8,128)(2,1)S(1)}, u32[]{:S(2)}, u32[]{:S(2)}) async-start(bf16[8,104,384]{2,1,0:T(8,128)(2,1)} %shard_map.95), calls=%async_computation | async-start | bytes 1277952 | tf_op jit(solution)/shard_map/all_to_all | solution.py:354
  7.2 2.0 %collective-permute-start.9 = (bf16[128,3584]{1,0:T(8,128)(2,1)}, bf16[128,3584]{1,0:T(8,128)(2,1)S(1)}, u32[]{:S(2)}, u32[]{:S(2)}) collective-permute-start(bf16[128,3584]{1,0:T(8,128)(2,1)} %rest_9_.1), channel_id=1, source_target_pairs={{0,64},{64,128},{128,192},{192,0},{1,65},{65,129},{129,193},{193,1... | collective-permute-start | bytes 2752520 | tf_op jit(solution)/shard_map/ppermute | solution.py:335
  9.2 1.2 collective-permute-start.11
  10.5 8.9 %all-to-all-done.bundle_hbm = bf16[8,104,384]{2,1,0:T(8,128)(2,1)S(1)} async-done(((bf16[8,104,384]{2,1,0:T(8,128)(2,1)}), bf16[8,104,384]{2,1,0:T(8,128)(2,1)S(1)}, u32[]{:S(2)}, u32[]{:S(2)}) %all-to-all-start) | async-done | bytes 639008 | tf_op jit(solution)/shard_map/all_to_all | solution.py:354
  19.4 5.9 %collective-permute-start.1 = (bf16[448,384]{1,0:T(8,128)(2,1)S(1)}, bf16[448,384]{1,0:T(8,128)(2,1)S(1)}, u32[]{:S(2)}, u32[]{:S(2)}) collective-permute-start(bf16[448,384]{1,0:T(8,128)(2,1)S(1)} %bitcast.23), channel_id=1, source_target_pairs={{0,56},{8,0},{16,8},{24,16},{32,24},{40,32},{48,40},{56,48},{1,57}... | collective-permute-start | bytes 1032200 | tf_op jit(solution)/shard_map/ppermute | solution.py:335
  25.4 6.4 %collective-permute-done.1 = bf16[448,384]{1,0:T(8,128)(2,1)S(1)} collective-permute-done((bf16[448,384]{1,0:T(8,128)(2,1)S(1)}, bf16[448,384]{1,0:T(8,128)(2,1)S(1)}, u32[]{:S(2)}, u32[]{:S(2)}) %collective-permute-start.1) | collective-permute-done | bytes 344096 | tf_op jit(solution)/shard_map/ppermute | solution.py:335
  31.8 3.7 %collective-permute-start.3 = (bf16[448,384]{1,0:T(8,128)(2,1)S(1)}, bf16[448,384]{1,0:T(8,128)(2,1)S(1)}, u32[]{:S(2)}, u32[]{:S(2)}) collective-permute-start(bf16[448,384]{1,0:T(8,128)(2,1)S(1)} %collective-permute-done.1), channel_id=1, source_target_pairs={{0,56},{8,0},{16,8},{24,16},{32,24},{40,32},{48,40},{56,48},{1,57}... | collective-permute-start | bytes 1032200 | tf_op jit(solution)/shard_map/ppermute | solution.py:335
  35.5 1.5 collective-permute-done
  37.1 4.1 %collective-permute-done.3 = bf16[448,384]{1,0:T(8,128)(2,1)S(1)} collective-permute-done((bf16[448,384]{1,0:T(8,128)(2,1)S(1)}, bf16[448,384]{1,0:T(8,128)(2,1)S(1)}, u32[]{:S(2)}, u32[]{:S(2)}) %collective-permute-start.3) | collective-permute-done | bytes 344096 | tf_op jit(solution)/shard_map/ppermute | solution.py:335
  41.1 3.7 %collective-permute-start.5 = (bf16[448,384]{1,0:T(8,128)(2,1)S(1)}, bf16[448,384]{1,0:T(8,128)(2,1)S(1)}, u32[]{:S(2)}, u32[]{:S(2)}) collective-permute-start(bf16[448,384]{1,0:T(8,128)(2,1)S(1)} %collective-permute-done.3), channel_id=1, source_target_pairs={{0,56},{8,0},{16,8},{24,16},{32,24},{40,32},{48,40},{56,48},{1,57}... | collective-permute-start | bytes 1032200 | tf_op jit(solution)/shard_map/ppermute | solution.py:335
  47.1 2.7 %collective-permute-start.15 = (bf16[64,3584]{1,0:T(8,128)(2,1)}, bf16[64,3584]{1,0:T(8,128)(2,1)}, u32[]{:S(2)}, u32[]{:S(2)}) collective-permute-start(bf16[64,3584]{1,0:T(8,128)(2,1)} %slice.48), channel_id=1, source_target_pairs={{0,192},{64,0},{128,64},{192,128},{1,193},{65,1},{129,65},{193,129... | collective-permute-start | bytes 1376264 | tf_op jit(solution)/shard_map/ppermute | solution.py:335
  51.6 5.0 %collective-permute-done.13.rest_15_ = bf16[64,3584]{1,0:T(8,128)(2,1)} collective-permute-done((bf16[64,3584]{1,0:T(8,128)(2,1)}, bf16[64,3584]{1,0:T(8,128)(2,1)}, u32[]{:S(2)}, u32[]{:S(2)}) %collective-permute-start.13) | collective-permute-done | bytes 458784 | tf_op jit(solution)/shard_map/ppermute | solution.py:335
  57.1 5.6 %collective-permute-done.4 = bf16[448,384]{1,0:T(8,128)(2,1)S(1)} collective-permute-done((bf16[448,384]{1,0:T(8,128)(2,1)}, bf16[448,384]{1,0:T(8,128)(2,1)S(1)}, u32[]{:S(2)}, u32[]{:S(2)}) %collective-permute-start.4) | collective-permute-done | bytes 344096 | tf_op jit(solution)/shard_map/ppermute | solution.py:335
  64.7 3.9 %collective-permute-done.7 = bf16[224,384]{1,0:T(8,128)(2,1)S(1)} collective-permute-done((bf16[224,384]{1,0:T(8,128)(2,1)S(1)}, bf16[224,384]{1,0:T(8,128)(2,1)S(1)}, u32[]{:S(2)}, u32[]{:S(2)}) %collective-permute-start.7) | collective-permute-done | bytes 172064 | tf_op jit(solution)/shard_map/ppermute | solution.py:335
  69.9 6.3 %collective-permute-done.6 = bf16[224,384]{1,0:T(8,128)(2,1)} collective-permute-done((bf16[224,384]{1,0:T(8,128)(2,1)}, bf16[224,384]{1,0:T(8,128)(2,1)}, u32[]{:S(2)}, u32[]{:S(2)}) %collective-permute-start.6) | collective-permute-done | bytes 172064 | tf_op jit(solution)/shard_map/ppermute | solution.py:335
  76.3 10.6 %shard_map.96 = (bf16[4,4,256,128]{3,2,1,0:T(8,128)(2,1)}, f32[4,256,128]{2,1,0:T(8,128)}, bf16[8,128,3584]{2,1,0:T(8,128)(2,1)}, bf16[8,112,128]{2,1,0:T(8,128)(2,1)}) custom-call(s32[3]{0:T(128)} %pad_add_fusion.ids, bf16[4,8,112,128]{3,2,1,0:T(8,128)(2,1)} %bitcast.26, bf16[4,112,384]{2,1,0:T(8,128)(2,1)} %bitcast.25, bf16[4,112,384]{2,1,0:T(8,128)(2,1)} %bitcast.31, ...), custom_call_target="tpu_custom_call" | custom-call | tf_op jit(solution)/shard_map/pallas_call | solution.py:37
  86.9 13.4 %all_to_all.35.got = bf16[8,112,128]{2,1,0:T(8,128)(2,1)S(1)} all-to-all(bf16[8,112,128]{2,1,0:T(8,128)(2,1)} %get-tuple-element.14), channel_id=1, replica_groups=mesh['y'=4,'z'=8,'c'=2,'x'=4] {'z'}, dimensions={0} | all-to-all | bytes 458752 | tf_op jit(solution)/shard_map/all_to_all | solution.py:393
  100.5 12.8 %all_to_all.36.s_in = bf16[8,96,128]{2,1,0:T(8,128)(2,1)} all-to-all(bf16[8,96,128]{2,1,0:T(8,128)(2,1)S(1)} %get-tuple-element.15), channel_id=1, replica_groups=mesh['y'=4,'z'=8,'c'=2,'x'=4] {'z'}, dimensions={0} | all-to-all | bytes 393216 | tf_op jit(solution)/shard_map/all_to_all | solution.py:395
  113.3 5.8 %shard_map.98 = (bf16[8,48,128]{2,1,0:T(8,128)(2,1)}, f32[4,256,128]{2,1,0:T(8,128)}) custom-call(bf16[8,96,128]{2,1,0:T(8,128)(2,1)} %all_to_all.36.s_in, bf16[2,128,128]{2,1,0:T(8,128)(2,1)} %pad_maximum_fusion.rest_19_.lift, f32[4,256]{1,0:T(4,128)} %add.26.rest_20_.logs, bf16[4,4,256,128]{3,2,1,0:T(8,128)(2,1)} %get-tuple-element.16.kvql_hbm, ...), custom_call_target="tpu_custom_call" | custom-call | tf_op jit(solution)/shard_map/pallas_call | solution.py:37
  119.1 12.0 %all_to_all.37.got = bf16[8,48,128]{2,1,0:T(8,128)(2,1)S(1)} all-to-all(bf16[8,48,128]{2,1,0:T(8,128)(2,1)} %get-tuple-element.18), channel_id=1, replica_groups=mesh['y'=4,'z'=8,'c'=2,'x'=4] {'z'}, dimensions={0} | all-to-all | bytes 196608 | tf_op jit(solution)/shard_map/all_to_all | solution.py:412
  131.1 11.8 %all_to_all.38.r_in = bf16[8,48,128]{2,1,0:T(8,128)(2,1)} all-to-all(bf16[8,48,128]{2,1,0:T(8,128)(2,1)S(1)} %shard_map.99), channel_id=1, replica_groups=mesh['y'=4,'z'=8,'c'=2,'x'=4] {'z'}, dimensions={0} | all-to-all | bytes 196608 | tf_op jit(solution)/shard_map/all_to_all | solution.py:414
  142.9 6.9 %shard_map.100 = (f32[16,112,128]{2,1,0:T(8,128)}, bf16[18,112,128]{2,1,0:T(8,128)(2,1)}) custom-call(s32[3]{0:T(128)} %pad_add_fusion.ids, bf16[8,48,128]{2,1,0:T(8,128)(2,1)} %all_to_all.38.r_in, f32[4,256]{1,0:T(4,128)} %add.26.rest_20_.logs, bf16[4,4,256,128]{3,2,1,0:T(8,128)(2,1)} %get-tuple-element.16.kvql_hbm, ...), custom_call_target="tpu_custom_call" | custom-call | tf_op jit(solution)/shard_map/pallas_call | solution.py:37
  149.9 2.1 %collective-permute-done.17.got = bf16[18,112,128]{2,1,0:T(8,128)(2,1)S(1)} collective-permute-done((bf16[18,112,128]{2,1,0:T(8,128)(2,1)}, bf16[18,112,128]{2,1,0:T(8,128)(2,1)S(1)}, u32[]{:S(2)}, u32[]{:S(2)}) %collective-permute-start.17) | collective-permute-done | bytes 516128 | tf_op jit(solution)/shard_map/ppermute | solution.py:336
  152.0 1.2 copy-done
  154.2 2.1 %shard_map.101 = (bf16[16,112,128]{2,1,0:T(8,128)(2,1)}, bf16[2,128,128]{2,1,0:T(8,128)(2,1)S(1)}) custom-call(f32[16,112,128]{2,1,0:T(8,128)S(1)} %copy-done, bf16[18,112,128]{2,1,0:T(8,128)(2,1)S(1)} %copy-done.1, bf16[18,112,128]{2,1,0:T(8,128)(2,1)S(1)} %collective-permute-done.17.got), custom_call_target="tpu_custom_call" | custom-call | tf_op jit(solution)/shard_map/pallas_call | solution.py:37
  156.3 4.9 %all-to-all-start.5 = ((bf16[16,112,128]{2,1,0:T(8,128)(2,1)}), bf16[16,112,128]{2,1,0:T(8,128)(2,1)S(1)}, u32[]{:S(2)}, u32[]{:S(2)}) async-start(bf16[16,112,128]{2,1,0:T(8,128)(2,1)} %get-tuple-element.24), calls=%async_computation.5 | async-start | bytes 917504 | tf_op jit(solution)/shard_map/all_to_all | solution.py:443
  161.1 3.0 %collective-permute-start.20 = (bf16[2,128,128]{2,1,0:T(8,128)(2,1)S(1)}, bf16[2,128,128]{2,1,0:T(8,128)(2,1)S(1)}, u32[]{:S(2)}, u32[]{:S(2)}) collective-permute-start(bf16[2,128,128]{2,1,0:T(8,128)(2,1)S(1)} %get-tuple-element.25.pair), channel_id=1, source_target_pairs={{0,128},{64,192},{128,0},{192,64},{1,129},{65,193},{129,1},{193,65... | collective-permute-start | bytes 196616 | tf_op jit(solution)/shard_map/ppermute | solution.py:335
  166.1 4.9 %all-to-all-done.5.got = bf16[16,112,128]{2,1,0:T(8,128)(2,1)S(1)} async-done(((bf16[16,112,128]{2,1,0:T(8,128)(2,1)}), bf16[16,112,128]{2,1,0:T(8,128)(2,1)S(1)}, u32[]{:S(2)}, u32[]{:S(2)}) %all-to-all-start.5) | async-done | bytes 458784 | tf_op jit(solution)/shard_map/all_to_all | solution.py:443
  171.7 3.3 %all-to-all-start.6 = ((bf16[8,16,128]{2,1,0:T(8,128)(2,1)}), bf16[8,16,128]{2,1,0:T(8,128)(2,1)S(1)}, u32[]{:S(2)}, u32[]{:S(2)}) async-start(bf16[8,16,128]{2,1,0:T(8,128)(2,1)} %shard_map.102), calls=%async_computation.6 | async-start | bytes 65536 | tf_op jit(solution)/shard_map/all_to_all | solution.py:448
  175.1 1.4 shard_map.104
  176.4 6.5 %all-to-all-done.6.got = bf16[8,16,128]{2,1,0:T(8,128)(2,1)S(1)} async-done(((bf16[8,16,128]{2,1,0:T(8,128)(2,1)}), bf16[8,16,128]{2,1,0:T(8,128)(2,1)S(1)}, u32[]{:S(2)}, u32[]{:S(2)}) %all-to-all-start.6) | async-done | bytes 32800 | tf_op jit(solution)/shard_map/all_to_all | solution.py:448
  (70 shorter events, 12.6 us)
Async XLA Ops:
  2.7 16.6 %all-to-all-start = ((bf16[8,104,384]{2,1,0:T(8,128)(2,1)}), bf16[8,104,384]{2,1,0:T(8,128)(2,1)S(1)}, u32[]{:S(2)}, u32[]{:S(2)}) async-start(bf16[8,104,384]{2,1,0:T(8,128)(2,1)} %shard_map.95), calls=%async_computation | async-start | bytes 1277952 | tf_op jit(solution)/shard_map/all_to_all | solution.py:354
  7.2 37.6 %collective-permute-start.9 = (bf16[128,3584]{1,0:T(8,128)(2,1)}, bf16[128,3584]{1,0:T(8,128)(2,1)S(1)}, u32[]{:S(2)}, u32[]{:S(2)}) collective-permute-start(bf16[128,3584]{1,0:T(8,128)(2,1)} %rest_9_.1), channel_id=1, source_target_pairs={{0,64},{64,128},{128,192},{192,0},{1,65},{65,129},{129,193},{193,1... | collective-permute-start | bytes 2752520 | tf_op jit(solution)/shard_map/ppermute | solution.py:335
  9.2 37.0 %collective-permute-start.11 = (bf16[128,3584]{1,0:T(8,128)(2,1)}, bf16[128,3584]{1,0:T(8,128)(2,1)S(1)}, u32[]{:S(2)}, u32[]{:S(2)}) collective-permute-start(bf16[128,3584]{1,0:T(8,128)(2,1)} %rest_9_.1), channel_id=1, source_target_pairs={{0,192},{64,0},{128,64},{192,128},{1,193},{65,1},{129,65},{193,129... | collective-permute-start | bytes 2752520 | tf_op jit(solution)/shard_map/ppermute | solution.py:335
  19.4 67.5 %copy-start.3 = (bf16[8,104,384]{2,1,0:T(8,128)(2,1)}, bf16[8,104,384]{2,1,0:T(8,128)(2,1)S(1)}, u32[]{:S(2)}) copy-start(bf16[8,104,384]{2,1,0:T(8,128)(2,1)S(1)} %all-to-all-done.bundle_hbm) | copy-start | bytes 1916932
  19.4 56.8 %copy-start.6 = (bf16[8,56,384]{2,1,0:T(8,128)(2,1)}, bf16[8,56,384]{2,1,0:T(8,128)(2,1)S(1)}, u32[]{:S(2)}) copy-start(bf16[8,56,384]{2,1,0:T(8,128)(2,1)S(1)} %slice.44) | copy-start | bytes 1032196
  19.4 12.4 %collective-permute-start.1 = (bf16[448,384]{1,0:T(8,128)(2,1)S(1)}, bf16[448,384]{1,0:T(8,128)(2,1)S(1)}, u32[]{:S(2)}, u32[]{:S(2)}) collective-permute-start(bf16[448,384]{1,0:T(8,128)(2,1)S(1)} %bitcast.23), channel_id=1, source_target_pairs={{0,56},{8,0},{16,8},{24,16},{32,24},{40,32},{48,40},{56,48},{1,57}... | collective-permute-start | bytes 1032200 | tf_op jit(solution)/shard_map/ppermute | solution.py:335
  25.4 24.4 %collective-permute-start.8 = (bf16[128,3584]{1,0:T(8,128)(2,1)}, bf16[128,3584]{1,0:T(8,128)(2,1)S(1)}, u32[]{:S(2)}, u32[]{:S(2)}) collective-permute-start(bf16[128,3584]{1,0:T(8,128)(2,1)} %rest_9_.1), channel_id=1, source_target_pairs={{0,4},{4,0},{1,5},{5,1},{2,6},{6,2},{3,7},{7,3},{8,12},{12,8},{9,1... | collective-permute-start | bytes 2752520 | tf_op jit(solution)/shard_map/ppermute | solution.py:336
  25.4 11.7 %collective-permute-start = (bf16[448,384]{1,0:T(8,128)(2,1)S(1)}, bf16[448,384]{1,0:T(8,128)(2,1)S(1)}, u32[]{:S(2)}, u32[]{:S(2)}) collective-permute-start(bf16[448,384]{1,0:T(8,128)(2,1)S(1)} %bitcast.24), channel_id=1, source_target_pairs={{0,8},{8,16},{16,24},{24,32},{32,40},{40,48},{48,56},{56,0},{1,9},... | collective-permute-start | bytes 1032200 | tf_op jit(solution)/shard_map/ppermute | solution.py:335
  31.8 9.3 %collective-permute-start.3 = (bf16[448,384]{1,0:T(8,128)(2,1)S(1)}, bf16[448,384]{1,0:T(8,128)(2,1)S(1)}, u32[]{:S(2)}, u32[]{:S(2)}) collective-permute-start(bf16[448,384]{1,0:T(8,128)(2,1)S(1)} %collective-permute-done.1), channel_id=1, source_target_pairs={{0,56},{8,0},{16,8},{24,16},{32,24},{40,32},{48,40},{56,48},{1,57}... | collective-permute-start | bytes 1032200 | tf_op jit(solution)/shard_map/ppermute | solution.py:335
  37.0 13.7 %copy-start.11 = (bf16[448,384]{1,0:T(8,128)(2,1)}, bf16[448,384]{1,0:T(8,128)(2,1)S(1)}, u32[]{:S(2)}) copy-start(bf16[448,384]{1,0:T(8,128)(2,1)S(1)} %collective-permute-done) | copy-start | bytes 1032196
  37.1 13.6 %collective-permute-start.2 = (bf16[448,384]{1,0:T(8,128)(2,1)S(1)}, bf16[448,384]{1,0:T(8,128)(2,1)}, u32[]{:S(2)}, u32[]{:S(2)}) collective-permute-start(bf16[448,384]{1,0:T(8,128)(2,1)S(1)} %collective-permute-done), channel_id=1, source_target_pairs={{0,8},{8,16},{16,24},{24,32},{32,40},{40,48},{48,56},{56,0},{1,9},... | collective-permute-start | bytes 1032200 | tf_op jit(solution)/shard_map/ppermute | solution.py:335
  41.1 9.6 %collective-permute-start.5 = (bf16[448,384]{1,0:T(8,128)(2,1)S(1)}, bf16[448,384]{1,0:T(8,128)(2,1)S(1)}, u32[]{:S(2)}, u32[]{:S(2)}) collective-permute-start(bf16[448,384]{1,0:T(8,128)(2,1)S(1)} %collective-permute-done.3), channel_id=1, source_target_pairs={{0,56},{8,0},{16,8},{24,16},{32,24},{40,32},{48,40},{56,48},{1,57}... | collective-permute-start | bytes 1032200 | tf_op jit(solution)/shard_map/ppermute | solution.py:335
  44.8 31.4 %copy-start.4 = (bf16[128,3584]{1,0:T(8,128)(2,1)}, bf16[128,3584]{1,0:T(8,128)(2,1)S(1)}, u32[]{:S(2)}) copy-start(bf16[128,3584]{1,0:T(8,128)(2,1)S(1)} %collective-permute-done.9.rest_11_) | copy-start | bytes 2752516
  45.7 10.9 %collective-permute-start.13 = (bf16[64,3584]{1,0:T(8,128)(2,1)}, bf16[64,3584]{1,0:T(8,128)(2,1)}, u32[]{:S(2)}, u32[]{:S(2)}) collective-permute-start(bf16[64,3584]{1,0:T(8,128)(2,1)} %slice.47), channel_id=1, source_target_pairs={{0,64},{64,128},{128,192},{192,0},{1,65},{65,129},{129,193},{193,1... | collective-permute-start | bytes 1376264 | tf_op jit(solution)/shard_map/ppermute | solution.py:335
  46.2 30.0 %copy-start.5 = (bf16[128,3584]{1,0:T(8,128)(2,1)}, bf16[128,3584]{1,0:T(8,128)(2,1)S(1)}, u32[]{:S(2)}) copy-start(bf16[128,3584]{1,0:T(8,128)(2,1)S(1)} %collective-permute-done.11.rest_13_) | copy-start | bytes 2752516
  47.1 9.6 %collective-permute-start.15 = (bf16[64,3584]{1,0:T(8,128)(2,1)}, bf16[64,3584]{1,0:T(8,128)(2,1)}, u32[]{:S(2)}, u32[]{:S(2)}) collective-permute-start(bf16[64,3584]{1,0:T(8,128)(2,1)} %slice.48), channel_id=1, source_target_pairs={{0,192},{64,0},{128,64},{192,128},{1,193},{65,1},{129,65},{193,129... | collective-permute-start | bytes 1376264 | tf_op jit(solution)/shard_map/ppermute | solution.py:335
  49.8 26.4 %collective-permute-start.10 = (bf16[128,3584]{1,0:T(8,128)(2,1)S(1)}, bf16[128,3584]{1,0:T(8,128)(2,1)}, u32[]{:S(2)}, u32[]{:S(2)}) collective-permute-start(bf16[128,3584]{1,0:T(8,128)(2,1)S(1)} %collective-permute-done.9.rest_11_), channel_id=1, source_target_pairs={{0,4},{4,0},{1,5},{5,1},{2,6},{6,2},{3,7},{7,3},{8,12},{12,8},{9,1... | collective-permute-start | bytes 2752520 | tf_op jit(solution)/shard_map/ppermute | solution.py:336
  50.7 25.5 %collective-permute-start.12 = (bf16[128,3584]{1,0:T(8,128)(2,1)S(1)}, bf16[128,3584]{1,0:T(8,128)(2,1)}, u32[]{:S(2)}, u32[]{:S(2)}) collective-permute-start(bf16[128,3584]{1,0:T(8,128)(2,1)S(1)} %collective-permute-done.11.rest_13_), channel_id=1, source_target_pairs={{0,4},{4,0},{1,5},{5,1},{2,6},{6,2},{3,7},{7,3},{8,12},{12,8},{9,1... | collective-permute-start | bytes 2752520 | tf_op jit(solution)/shard_map/ppermute | solution.py:336
  50.7 25.5 %copy-start.8 = (bf16[448,384]{1,0:T(8,128)(2,1)}, bf16[448,384]{1,0:T(8,128)(2,1)S(1)}, u32[]{:S(2)}) copy-start(bf16[448,384]{1,0:T(8,128)(2,1)S(1)} %collective-permute-done.5) | copy-start | bytes 1032196
  50.7 12.0 %collective-permute-start.4 = (bf16[448,384]{1,0:T(8,128)(2,1)}, bf16[448,384]{1,0:T(8,128)(2,1)S(1)}, u32[]{:S(2)}, u32[]{:S(2)}) collective-permute-start(bf16[448,384]{1,0:T(8,128)(2,1)} %collective-permute-done.2), channel_id=1, source_target_pairs={{0,8},{8,16},{16,24},{24,32},{32,40},{40,48},{48,56},{56,0},{1,9},... | collective-permute-start | bytes 1032200 | tf_op jit(solution)/shard_map/ppermute | solution.py:335
  56.6 19.6 %collective-permute-start.14 = (bf16[64,3584]{1,0:T(8,128)(2,1)}, bf16[64,3584]{1,0:T(8,128)(2,1)}, u32[]{:S(2)}, u32[]{:S(2)}) collective-permute-start(bf16[64,3584]{1,0:T(8,128)(2,1)} %collective-permute-done.13.rest_15_), channel_id=1, source_target_pairs={{0,4},{4,0},{1,5},{5,1},{2,6},{6,2},{3,7},{7,3},{8,12},{12,8},{9,1... | collective-permute-start | bytes 1376264 | tf_op jit(solution)/shard_map/ppermute | solution.py:336
  56.7 19.5 %collective-permute-start.16 = (bf16[64,3584]{1,0:T(8,128)(2,1)}, bf16[64,3584]{1,0:T(8,128)(2,1)}, u32[]{:S(2)}, u32[]{:S(2)}) collective-permute-start(bf16[64,3584]{1,0:T(8,128)(2,1)} %collective-permute-done.15.rest_17_), channel_id=1, source_target_pairs={{0,4},{4,0},{1,5},{5,1},{2,6},{6,2},{3,7},{7,3},{8,12},{12,8},{9,1... | collective-permute-start | bytes 1376264 | tf_op jit(solution)/shard_map/ppermute | solution.py:336
  62.7 13.6 %copy-start.9 = (bf16[448,384]{1,0:T(8,128)(2,1)}, bf16[448,384]{1,0:T(8,128)(2,1)S(1)}, u32[]{:S(2)}) copy-start(bf16[448,384]{1,0:T(8,128)(2,1)S(1)} %collective-permute-done.4) | copy-start | bytes 1032196
  62.7 5.9 %collective-permute-start.7 = (bf16[224,384]{1,0:T(8,128)(2,1)S(1)}, bf16[224,384]{1,0:T(8,128)(2,1)S(1)}, u32[]{:S(2)}, u32[]{:S(2)}) collective-permute-start(bf16[224,384]{1,0:T(8,128)(2,1)S(1)} %slice.46), channel_id=1, source_target_pairs={{0,56},{8,0},{16,8},{24,16},{32,24},{40,32},{48,40},{56,48},{1,57}... | collective-permute-start | bytes 516104 | tf_op jit(solution)/shard_map/ppermute | solution.py:335
  69.3 6.9 %collective-permute-start.6 = (bf16[224,384]{1,0:T(8,128)(2,1)}, bf16[224,384]{1,0:T(8,128)(2,1)}, u32[]{:S(2)}, u32[]{:S(2)}) collective-permute-start(bf16[224,384]{1,0:T(8,128)(2,1)} %slice.45), channel_id=1, source_target_pairs={{0,8},{8,16},{16,24},{24,32},{32,40},{40,48},{48,56},{56,0},{1,9},... | collective-permute-start | bytes 516104 | tf_op jit(solution)/shard_map/ppermute | solution.py:335
  113.3 61.8 %copy-start.2 = (s32[3]{0:T(128)S(1)}, s32[3]{0:T(128)}, u32[]{:S(2)}) copy-start(s32[3]{0:T(128)} %pad_add_fusion.ids) | copy-start | bytes 40
  149.8 2.2 %collective-permute-start.17 = (bf16[18,112,128]{2,1,0:T(8,128)(2,1)}, bf16[18,112,128]{2,1,0:T(8,128)(2,1)S(1)}, u32[]{:S(2)}, u32[]{:S(2)}) collective-permute-start(bf16[18,112,128]{2,1,0:T(8,128)(2,1)} %get-tuple-element.23.give), channel_id=1, source_target_pairs={{0,4},{4,0},{1,5},{5,1},{2,6},{6,2},{3,7},{7,3},{8,12},{12,8},{9,1... | collective-permute-start | bytes 1548296 | tf_op jit(solution)/shard_map/ppermute | solution.py:336
  156.3 14.7 %all-to-all-start.5 = ((bf16[16,112,128]{2,1,0:T(8,128)(2,1)}), bf16[16,112,128]{2,1,0:T(8,128)(2,1)S(1)}, u32[]{:S(2)}, u32[]{:S(2)}) async-start(bf16[16,112,128]{2,1,0:T(8,128)(2,1)} %get-tuple-element.24), calls=%async_computation.5 | async-start | bytes 917504 | tf_op jit(solution)/shard_map/all_to_all | solution.py:443
  161.1 13.9 %collective-permute-start.20 = (bf16[2,128,128]{2,1,0:T(8,128)(2,1)S(1)}, bf16[2,128,128]{2,1,0:T(8,128)(2,1)S(1)}, u32[]{:S(2)}, u32[]{:S(2)}) collective-permute-start(bf16[2,128,128]{2,1,0:T(8,128)(2,1)S(1)} %get-tuple-element.25.pair), channel_id=1, source_target_pairs={{0,128},{64,192},{128,0},{192,64},{1,129},{65,193},{129,1},{193,65... | collective-permute-start | bytes 196616 | tf_op jit(solution)/shard_map/ppermute | solution.py:335
  164.1 10.9 %collective-permute-start.19 = (bf16[2,128,128]{2,1,0:T(8,128)(2,1)S(1)}, bf16[2,128,128]{2,1,0:T(8,128)(2,1)S(1)}, u32[]{:S(2)}, u32[]{:S(2)}) collective-permute-start(bf16[2,128,128]{2,1,0:T(8,128)(2,1)S(1)} %get-tuple-element.25.pair), channel_id=1, source_target_pairs={{0,192},{64,0},{128,64},{192,128},{1,193},{65,1},{129,65},{193,129... | collective-permute-start | bytes 196616 | tf_op jit(solution)/shard_map/ppermute | solution.py:335
  165.3 9.8 %collective-permute-start.18 = (bf16[2,128,128]{2,1,0:T(8,128)(2,1)S(1)}, bf16[2,128,128]{2,1,0:T(8,128)(2,1)S(1)}, u32[]{:S(2)}, u32[]{:S(2)}) collective-permute-start(bf16[2,128,128]{2,1,0:T(8,128)(2,1)S(1)} %get-tuple-element.25.pair), channel_id=1, source_target_pairs={{0,64},{64,128},{128,192},{192,0},{1,65},{65,129},{129,193},{193,1... | collective-permute-start | bytes 196616 | tf_op jit(solution)/shard_map/ppermute | solution.py:335
  171.7 11.3 %all-to-all-start.6 = ((bf16[8,16,128]{2,1,0:T(8,128)(2,1)}), bf16[8,16,128]{2,1,0:T(8,128)(2,1)S(1)}, u32[]{:S(2)}, u32[]{:S(2)}) async-start(bf16[8,16,128]{2,1,0:T(8,128)(2,1)} %shard_map.102), calls=%async_computation.6 | async-start | bytes 65536 | tf_op jit(solution)/shard_map/all_to_all | solution.py:448
  (6 other events, 22.8 us)

commit v5 on v4

--- a/solution.py
+++ b/solution.py
@@ -281,14 +281,17 @@
             give[b] = jnp.where(first, halves[1], halves[0]).astype(bf16)
 
 
-def add_kernel(keep_hbm, give, got, out, pair, keep, sems):
-    copies = begin([(keep_hbm.at[4 * i : 4 * i + 4], keep.at[4 * i : 4 * i + 4]) for i in range(4)], sems)
-    for i, ref in enumerate((give, got)):
-        pair[i, :112] = ref[16]
-        pair[i, 112:] = ref[17, :16]
-    for i, copy in enumerate(copies):
+def add_kernel(keep_hbm, give_hbm, got, out, pair, keep, own, sems):
+    quarter = [slice(4 * i, 4 * i + 4) for i in range(4)]
+    copies = begin([(give_hbm.at[16:18], own)], sems)
+    copies += begin([(keep_hbm.at[rows], keep.at[rows]) for rows in quarter], sems, 1)
+    pair[1, :112] = got[16]
+    pair[1, 112:] = got[17, :16]
+    copies[0].wait()
+    pair[0, :112] = own[0]
+    pair[0, 112:] = own[1, :16]
+    for rows, copy in zip(quarter, copies[1:]):
         copy.wait()
-        rows = slice(4 * i, 4 * i + 4)
         out[rows] = (keep[rows] + got[rows].astype(f32)).astype(bf16)
 
 
@@ -436,10 +439,15 @@
         add_kernel,
         (shape(keep.shape), shape((2, 2 * rank, hk))),
         keep, give, swap(give),
-        specs=[HBM, VMEM, VMEM],
-        scratch=[pltpu.VMEM(keep.shape, f32), DMA((4,))],
-    )
-    ups = [ring(pair, 1), ring(pair, -1), ring(pair, 2)]
+        specs=[HBM, HBM, VMEM],
+        mib=60,
+        scratch=[
+            pltpu.VMEM(keep.shape, f32),
+            pltpu.VMEM((2,) + keep.shape[1:], bf16),
+            DMA((5,)),
+        ],
+    )
+    ups = [ring(pair, i) for i in (1, 3, 2)]
     down_terms = lax.all_to_all(down_terms, ("y", "x"), 0, 0, tiled=True)
     down_terms = call(
         fold_kernel, shape((nz, 16, hk)), down_terms,

time: 184 us -> 184 us (level)
  no operation moved by 1% of the time
where the time goes in v5:
time: 184 us; the launch traced here: 183 us
  waiting for transfers between devices  54.5 us (30%)
  blocking collectives  50.1 us (27%)
  starting transfers between devices  38 us (21%)
  Pallas kernels  31.4 us (17%)
  local copies, waits for them, and re-layouts  7.06 us (4%)
    ppermute x15, waiting for transfers between devices, layer(): lax.ppermute(v, a, [(i, (i + s) % n) for i in range(n)])  32.9 us
    pallas_call x10, Pallas kernels, call(): pl.pallas_call(kernel, out_shape=outs, in_specs=specs or [VMEM] * len(arg...  31.4 us
    all_to_all x2, blocking collectives, layer(): got = lax.all_to_all(send, 'z', 0, 0, tiled=True)  25.4 us
    ppermute x15, starting transfers between devices, layer(): lax.ppermute(v, a, [(i, (i + s) % n) for i in range(n)])  24.9 us
    all_to_all x1, blocking collectives, layer(): s_in = lax.all_to_all(scanned, 'z', 0, 0, tiled=True)  12.8 us
    all_to_all x1, blocking collectives, layer(): r_in = lax.all_to_all(scanned, 'z', 0, 0, tiled=True)  11.8 us
    all_to_all x1, waiting for transfers between devices, layer(): bundle = lax.all_to_all(bundle, group, 0, 0, tiled=True)  8.91 us
    all_to_all x1, waiting for transfers between devices, layer(): down_terms = lax.all_to_all(down_terms, 'z', 0, 0, tiled=True)  5.67 us
  transfers between devices with their start and end apart: 24, of which 12 were waited for; matrix products, arithmetic and copies ran while one was open for 3% of the time, Pallas kernels for 1%

profile of v5, /device:TPU:2, one launch (start us, length us, event | category | flops | bytes accessed | tf_op | source)
XLA Modules:
  0.0 183.3 jit_solution(12678769570191948021)
XLA Ops:
  0.6 2.1 %shard_map.95 = bf16[8,104,384]{2,1,0:T(8,128)(2,1)} custom-call(bf16[56,1024]{1,0:T(8,128)(2,1)} %a_hbm.1, bf16[56,1024]{1,0:T(8,128)(2,1)} %b_hbm.1, bf16[56,1024]{1,0:T(8,128)(2,1)} %c_hbm.1, bf16[128,1024]{1,0:T(8,128)(2,1)} %grad_hbm.1, f32[8,128]{1,0:T(8,128)} %decay_hbm.1), custom_call_target="tpu_custom_call" | custom-call | tf_op jit(solution)/shard_map/pallas_call | solution.py:37
  2.7 4.5 %all-to-all-start = ((bf16[8,104,384]{2,1,0:T(8,128)(2,1)}), bf16[8,104,384]{2,1,0:T(8,128)(2,1)S(1)}, u32[]{:S(2)}, u32[]{:S(2)}) async-start(bf16[8,104,384]{2,1,0:T(8,128)(2,1)} %shard_map.95), calls=%async_computation | async-start | bytes 1277952 | tf_op jit(solution)/shard_map/all_to_all | solution.py:357
  7.2 2.0 %collective-permute-start.9 = (bf16[128,3584]{1,0:T(8,128)(2,1)}, bf16[128,3584]{1,0:T(8,128)(2,1)S(1)}, u32[]{:S(2)}, u32[]{:S(2)}) collective-permute-start(bf16[128,3584]{1,0:T(8,128)(2,1)} %rest_9_.1), channel_id=1, source_target_pairs={{0,64},{64,128},{128,192},{192,0},{1,65},{65,129},{129,193},{193,1... | collective-permute-start | bytes 2752520 | tf_op jit(solution)/shard_map/ppermute | solution.py:338
  9.2 1.2 collective-permute-start.11
  10.5 8.9 %all-to-all-done.bundle_hbm = bf16[8,104,384]{2,1,0:T(8,128)(2,1)S(1)} async-done(((bf16[8,104,384]{2,1,0:T(8,128)(2,1)}), bf16[8,104,384]{2,1,0:T(8,128)(2,1)S(1)}, u32[]{:S(2)}, u32[]{:S(2)}) %all-to-all-start) | async-done | bytes 639008 | tf_op jit(solution)/shard_map/all_to_all | solution.py:357
  19.4 5.9 %collective-permute-start.1 = (bf16[448,384]{1,0:T(8,128)(2,1)S(1)}, bf16[448,384]{1,0:T(8,128)(2,1)S(1)}, u32[]{:S(2)}, u32[]{:S(2)}) collective-permute-start(bf16[448,384]{1,0:T(8,128)(2,1)S(1)} %bitcast.23), channel_id=1, source_target_pairs={{0,56},{8,0},{16,8},{24,16},{32,24},{40,32},{48,40},{56,48},{1,57}... | collective-permute-start | bytes 1032200 | tf_op jit(solution)/shard_map/ppermute | solution.py:338
  25.4 6.4 %collective-permute-done.1 = bf16[448,384]{1,0:T(8,128)(2,1)S(1)} collective-permute-done((bf16[448,384]{1,0:T(8,128)(2,1)S(1)}, bf16[448,384]{1,0:T(8,128)(2,1)S(1)}, u32[]{:S(2)}, u32[]{:S(2)}) %collective-permute-start.1) | collective-permute-done | bytes 344096 | tf_op jit(solution)/shard_map/ppermute | solution.py:338
  31.8 3.7 %collective-permute-start.3 = (bf16[448,384]{1,0:T(8,128)(2,1)S(1)}, bf16[448,384]{1,0:T(8,128)(2,1)S(1)}, u32[]{:S(2)}, u32[]{:S(2)}) collective-permute-start(bf16[448,384]{1,0:T(8,128)(2,1)S(1)} %collective-permute-done.1), channel_id=1, source_target_pairs={{0,56},{8,0},{16,8},{24,16},{32,24},{40,32},{48,40},{56,48},{1,57}... | collective-permute-start | bytes 1032200 | tf_op jit(solution)/shard_map/ppermute | solution.py:338
  35.5 1.5 collective-permute-done
  37.1 4.1 %collective-permute-done.3 = bf16[448,384]{1,0:T(8,128)(2,1)S(1)} collective-permute-done((bf16[448,384]{1,0:T(8,128)(2,1)S(1)}, bf16[448,384]{1,0:T(8,128)(2,1)S(1)}, u32[]{:S(2)}, u32[]{:S(2)}) %collective-permute-start.3) | collective-permute-done | bytes 344096 | tf_op jit(solution)/shard_map/ppermute | solution.py:338
  41.1 3.7 %collective-permute-start.5 = (bf16[448,384]{1,0:T(8,128)(2,1)S(1)}, bf16[448,384]{1,0:T(8,128)(2,1)S(1)}, u32[]{:S(2)}, u32[]{:S(2)}) collective-permute-start(bf16[448,384]{1,0:T(8,128)(2,1)S(1)} %collective-permute-done.3), channel_id=1, source_target_pairs={{0,56},{8,0},{16,8},{24,16},{32,24},{40,32},{48,40},{56,48},{1,57}... | collective-permute-start | bytes 1032200 | tf_op jit(solution)/shard_map/ppermute | solution.py:338
  47.1 2.7 %collective-permute-start.15 = (bf16[64,3584]{1,0:T(8,128)(2,1)}, bf16[64,3584]{1,0:T(8,128)(2,1)}, u32[]{:S(2)}, u32[]{:S(2)}) collective-permute-start(bf16[64,3584]{1,0:T(8,128)(2,1)} %slice.48), channel_id=1, source_target_pairs={{0,192},{64,0},{128,64},{192,128},{1,193},{65,1},{129,65},{193,129... | collective-permute-start | bytes 1376264 | tf_op jit(solution)/shard_map/ppermute | solution.py:338
  51.6 5.0 %collective-permute-done.13.rest_15_ = bf16[64,3584]{1,0:T(8,128)(2,1)} collective-permute-done((bf16[64,3584]{1,0:T(8,128)(2,1)}, bf16[64,3584]{1,0:T(8,128)(2,1)}, u32[]{:S(2)}, u32[]{:S(2)}) %collective-permute-start.13) | collective-permute-done | bytes 458784 | tf_op jit(solution)/shard_map/ppermute | solution.py:338
  57.1 5.6 %collective-permute-done.4 = bf16[448,384]{1,0:T(8,128)(2,1)S(1)} collective-permute-done((bf16[448,384]{1,0:T(8,128)(2,1)}, bf16[448,384]{1,0:T(8,128)(2,1)S(1)}, u32[]{:S(2)}, u32[]{:S(2)}) %collective-permute-start.4) | collective-permute-done | bytes 344096 | tf_op jit(solution)/shard_map/ppermute | solution.py:338
  64.7 3.9 %collective-permute-done.7 = bf16[224,384]{1,0:T(8,128)(2,1)S(1)} collective-permute-done((bf16[224,384]{1,0:T(8,128)(2,1)S(1)}, bf16[224,384]{1,0:T(8,128)(2,1)S(1)}, u32[]{:S(2)}, u32[]{:S(2)}) %collective-permute-start.7) | collective-permute-done | bytes 172064 | tf_op jit(solution)/shard_map/ppermute | solution.py:338
  69.9 6.3 %collective-permute-done.6 = bf16[224,384]{1,0:T(8,128)(2,1)} collective-permute-done((bf16[224,384]{1,0:T(8,128)(2,1)}, bf16[224,384]{1,0:T(8,128)(2,1)}, u32[]{:S(2)}, u32[]{:S(2)}) %collective-permute-start.6) | collective-permute-done | bytes 172064 | tf_op jit(solution)/shard_map/ppermute | solution.py:338
  76.3 10.6 %shard_map.96 = (bf16[4,4,256,128]{3,2,1,0:T(8,128)(2,1)}, f32[4,256,128]{2,1,0:T(8,128)}, bf16[8,128,3584]{2,1,0:T(8,128)(2,1)}, bf16[8,112,128]{2,1,0:T(8,128)(2,1)}) custom-call(s32[3]{0:T(128)} %pad_add_fusion.ids, bf16[4,8,112,128]{3,2,1,0:T(8,128)(2,1)} %bitcast.26, bf16[4,112,384]{2,1,0:T(8,128)(2,1)} %bitcast.25, bf16[4,112,384]{2,1,0:T(8,128)(2,1)} %bitcast.31, ...), custom_call_target="tpu_custom_call" | custom-call | tf_op jit(solution)/shard_map/pallas_call | solution.py:37
  86.9 13.4 %all_to_all.35.got = bf16[8,112,128]{2,1,0:T(8,128)(2,1)S(1)} all-to-all(bf16[8,112,128]{2,1,0:T(8,128)(2,1)} %get-tuple-element.14), channel_id=1, replica_groups=mesh['y'=4,'z'=8,'c'=2,'x'=4] {'z'}, dimensions={0} | all-to-all | bytes 458752 | tf_op jit(solution)/shard_map/all_to_all | solution.py:396
  100.5 12.8 %all_to_all.36.s_in = bf16[8,96,128]{2,1,0:T(8,128)(2,1)} all-to-all(bf16[8,96,128]{2,1,0:T(8,128)(2,1)S(1)} %get-tuple-element.15), channel_id=1, replica_groups=mesh['y'=4,'z'=8,'c'=2,'x'=4] {'z'}, dimensions={0} | all-to-all | bytes 393216 | tf_op jit(solution)/shard_map/all_to_all | solution.py:398
  113.3 5.8 %shard_map.98 = (bf16[8,48,128]{2,1,0:T(8,128)(2,1)}, f32[4,256,128]{2,1,0:T(8,128)}) custom-call(bf16[8,96,128]{2,1,0:T(8,128)(2,1)} %all_to_all.36.s_in, bf16[2,128,128]{2,1,0:T(8,128)(2,1)} %pad_maximum_fusion.rest_19_.lift, f32[4,256]{1,0:T(4,128)} %add.26.rest_20_.logs, bf16[4,4,256,128]{3,2,1,0:T(8,128)(2,1)} %get-tuple-element.16.kvql_hbm, ...), custom_call_target="tpu_custom_call" | custom-call | tf_op jit(solution)/shard_map/pallas_call | solution.py:37
  119.1 12.0 %all_to_all.37.got = bf16[8,48,128]{2,1,0:T(8,128)(2,1)S(1)} all-to-all(bf16[8,48,128]{2,1,0:T(8,128)(2,1)} %get-tuple-element.18), channel_id=1, replica_groups=mesh['y'=4,'z'=8,'c'=2,'x'=4] {'z'}, dimensions={0} | all-to-all | bytes 196608 | tf_op jit(solution)/shard_map/all_to_all | solution.py:415
  131.1 11.8 %all_to_all.38.r_in = bf16[8,48,128]{2,1,0:T(8,128)(2,1)} all-to-all(bf16[8,48,128]{2,1,0:T(8,128)(2,1)S(1)} %shard_map.99), channel_id=1, replica_groups=mesh['y'=4,'z'=8,'c'=2,'x'=4] {'z'}, dimensions={0} | all-to-all | bytes 196608 | tf_op jit(solution)/shard_map/all_to_all | solution.py:417
  142.9 6.9 %shard_map.100 = (f32[16,112,128]{2,1,0:T(8,128)}, bf16[18,112,128]{2,1,0:T(8,128)(2,1)}) custom-call(s32[3]{0:T(128)} %pad_add_fusion.ids, bf16[8,48,128]{2,1,0:T(8,128)(2,1)} %all_to_all.38.r_in, f32[4,256]{1,0:T(4,128)} %add.26.rest_20_.logs, bf16[4,4,256,128]{3,2,1,0:T(8,128)(2,1)} %get-tuple-element.16.kvql_hbm, ...), custom_call_target="tpu_custom_call" | custom-call | tf_op jit(solution)/shard_map/pallas_call | solution.py:37
  149.9 2.1 %collective-permute-done.17.got = bf16[18,112,128]{2,1,0:T(8,128)(2,1)S(1)} collective-permute-done((bf16[18,112,128]{2,1,0:T(8,128)(2,1)}, bf16[18,112,128]{2,1,0:T(8,128)(2,1)S(1)}, u32[]{:S(2)}, u32[]{:S(2)}) %collective-permute-start.17) | collective-permute-done | bytes 516128 | tf_op jit(solution)/shard_map/ppermute | solution.py:339
  152.8 3.2 %shard_map.101 = (bf16[16,112,128]{2,1,0:T(8,128)(2,1)}, bf16[2,128,128]{2,1,0:T(8,128)(2,1)}) custom-call(f32[16,112,128]{2,1,0:T(8,128)} %get-tuple-element.22.keep_hbm, bf16[18,112,128]{2,1,0:T(8,128)(2,1)} %get-tuple-element.23.give_hbm, bf16[18,112,128]{2,1,0:T(8,128)(2,1)} %copy-done.9), custom_call_target="tpu_custom_call" | custom-call | tf_op jit(solution)/shard_map/pallas_call | solution.py:37
  156.0 4.9 %all-to-all-start.5 = ((bf16[16,112,128]{2,1,0:T(8,128)(2,1)}), bf16[16,112,128]{2,1,0:T(8,128)(2,1)S(1)}, u32[]{:S(2)}, u32[]{:S(2)}) async-start(bf16[16,112,128]{2,1,0:T(8,128)(2,1)} %get-tuple-element.24), calls=%async_computation.5 | async-start | bytes 917504 | tf_op jit(solution)/shard_map/all_to_all | solution.py:451
  160.8 3.0 %collective-permute-start.20 = (bf16[2,128,128]{2,1,0:T(8,128)(2,1)}, bf16[2,128,128]{2,1,0:T(8,128)(2,1)S(1)}, u32[]{:S(2)}, u32[]{:S(2)}) collective-permute-start(bf16[2,128,128]{2,1,0:T(8,128)(2,1)} %get-tuple-element.25.pair), channel_id=1, source_target_pairs={{0,128},{64,192},{128,0},{192,64},{1,129},{65,193},{129,1},{193,65... | collective-permute-start | bytes 196616 | tf_op jit(solution)/shard_map/ppermute | solution.py:338
  163.8 1.2 collective-permute-start.19
  165.8 4.9 %all-to-all-done.5.got = bf16[16,112,128]{2,1,0:T(8,128)(2,1)S(1)} async-done(((bf16[16,112,128]{2,1,0:T(8,128)(2,1)}), bf16[16,112,128]{2,1,0:T(8,128)(2,1)S(1)}, u32[]{:S(2)}, u32[]{:S(2)}) %all-to-all-start.5) | async-done | bytes 458784 | tf_op jit(solution)/shard_map/all_to_all | solution.py:451
  171.4 3.3 %all-to-all-start.6 = ((bf16[8,16,128]{2,1,0:T(8,128)(2,1)}), bf16[8,16,128]{2,1,0:T(8,128)(2,1)S(1)}, u32[]{:S(2)}, u32[]{:S(2)}) async-start(bf16[8,16,128]{2,1,0:T(8,128)(2,1)} %shard_map.102), calls=%async_computation.6 | async-start | bytes 65536 | tf_op jit(solution)/shard_map/all_to_all | solution.py:456
  175.6 1.4 shard_map.104
  177.0 5.7 %all-to-all-done.6.got = bf16[8,16,128]{2,1,0:T(8,128)(2,1)S(1)} async-done(((bf16[8,16,128]{2,1,0:T(8,128)(2,1)}), bf16[8,16,128]{2,1,0:T(8,128)(2,1)S(1)}, u32[]{:S(2)}, u32[]{:S(2)}) %all-to-all-start.6) | async-done | bytes 32800 | tf_op jit(solution)/shard_map/all_to_all | solution.py:456
  (70 shorter events, 12.0 us)
Async XLA Ops:
  2.7 16.6 %all-to-all-start = ((bf16[8,104,384]{2,1,0:T(8,128)(2,1)}), bf16[8,104,384]{2,1,0:T(8,128)(2,1)S(1)}, u32[]{:S(2)}, u32[]{:S(2)}) async-start(bf16[8,104,384]{2,1,0:T(8,128)(2,1)} %shard_map.95), calls=%async_computation | async-start | bytes 1277952 | tf_op jit(solution)/shard_map/all_to_all | solution.py:357
  7.2 37.6 %collective-permute-start.9 = (bf16[128,3584]{1,0:T(8,128)(2,1)}, bf16[128,3584]{1,0:T(8,128)(2,1)S(1)}, u32[]{:S(2)}, u32[]{:S(2)}) collective-permute-start(bf16[128,3584]{1,0:T(8,128)(2,1)} %rest_9_.1), channel_id=1, source_target_pairs={{0,64},{64,128},{128,192},{192,0},{1,65},{65,129},{129,193},{193,1... | collective-permute-start | bytes 2752520 | tf_op jit(solution)/shard_map/ppermute | solution.py:338
  9.2 37.0 %collective-permute-start.11 = (bf16[128,3584]{1,0:T(8,128)(2,1)}, bf16[128,3584]{1,0:T(8,128)(2,1)S(1)}, u32[]{:S(2)}, u32[]{:S(2)}) collective-permute-start(bf16[128,3584]{1,0:T(8,128)(2,1)} %rest_9_.1), channel_id=1, source_target_pairs={{0,192},{64,0},{128,64},{192,128},{1,193},{65,1},{129,65},{193,129... | collective-permute-start | bytes 2752520 | tf_op jit(solution)/shard_map/ppermute | solution.py:338
  19.4 67.5 %copy-start.2 = (bf16[8,104,384]{2,1,0:T(8,128)(2,1)}, bf16[8,104,384]{2,1,0:T(8,128)(2,1)S(1)}, u32[]{:S(2)}) copy-start(bf16[8,104,384]{2,1,0:T(8,128)(2,1)S(1)} %all-to-all-done.bundle_hbm) | copy-start | bytes 1916932
  19.4 56.8 %copy-start.5 = (bf16[8,56,384]{2,1,0:T(8,128)(2,1)}, bf16[8,56,384]{2,1,0:T(8,128)(2,1)S(1)}, u32[]{:S(2)}) copy-start(bf16[8,56,384]{2,1,0:T(8,128)(2,1)S(1)} %slice.44) | copy-start | bytes 1032196
  19.4 12.4 %collective-permute-start.1 = (bf16[448,384]{1,0:T(8,128)(2,1)S(1)}, bf16[448,384]{1,0:T(8,128)(2,1)S(1)}, u32[]{:S(2)}, u32[]{:S(2)}) collective-permute-start(bf16[448,384]{1,0:T(8,128)(2,1)S(1)} %bitcast.23), channel_id=1, source_target_pairs={{0,56},{8,0},{16,8},{24,16},{32,24},{40,32},{48,40},{56,48},{1,57}... | collective-permute-start | bytes 1032200 | tf_op jit(solution)/shard_map/ppermute | solution.py:338
  25.4 24.4 %collective-permute-start.8 = (bf16[128,3584]{1,0:T(8,128)(2,1)}, bf16[128,3584]{1,0:T(8,128)(2,1)S(1)}, u32[]{:S(2)}, u32[]{:S(2)}) collective-permute-start(bf16[128,3584]{1,0:T(8,128)(2,1)} %rest_9_.1), channel_id=1, source_target_pairs={{0,4},{4,0},{1,5},{5,1},{2,6},{6,2},{3,7},{7,3},{8,12},{12,8},{9,1... | collective-permute-start | bytes 2752520 | tf_op jit(solution)/shard_map/ppermute | solution.py:339
  25.4 11.7 %collective-permute-start = (bf16[448,384]{1,0:T(8,128)(2,1)S(1)}, bf16[448,384]{1,0:T(8,128)(2,1)S(1)}, u32[]{:S(2)}, u32[]{:S(2)}) collective-permute-start(bf16[448,384]{1,0:T(8,128)(2,1)S(1)} %bitcast.24), channel_id=1, source_target_pairs={{0,8},{8,16},{16,24},{24,32},{32,40},{40,48},{48,56},{56,0},{1,9},... | collective-permute-start | bytes 1032200 | tf_op jit(solution)/shard_map/ppermute | solution.py:338
  31.8 9.3 %collective-permute-start.3 = (bf16[448,384]{1,0:T(8,128)(2,1)S(1)}, bf16[448,384]{1,0:T(8,128)(2,1)S(1)}, u32[]{:S(2)}, u32[]{:S(2)}) collective-permute-start(bf16[448,384]{1,0:T(8,128)(2,1)S(1)} %collective-permute-done.1), channel_id=1, source_target_pairs={{0,56},{8,0},{16,8},{24,16},{32,24},{40,32},{48,40},{56,48},{1,57}... | collective-permute-start | bytes 1032200 | tf_op jit(solution)/shard_map/ppermute | solution.py:338
  37.0 13.7 %copy-start.11 = (bf16[448,384]{1,0:T(8,128)(2,1)}, bf16[448,384]{1,0:T(8,128)(2,1)S(1)}, u32[]{:S(2)}) copy-start(bf16[448,384]{1,0:T(8,128)(2,1)S(1)} %collective-permute-done) | copy-start | bytes 1032196
  37.1 13.6 %collective-permute-start.2 = (bf16[448,384]{1,0:T(8,128)(2,1)S(1)}, bf16[448,384]{1,0:T(8,128)(2,1)}, u32[]{:S(2)}, u32[]{:S(2)}) collective-permute-start(bf16[448,384]{1,0:T(8,128)(2,1)S(1)} %collective-permute-done), channel_id=1, source_target_pairs={{0,8},{8,16},{16,24},{24,32},{32,40},{40,48},{48,56},{56,0},{1,9},... | collective-permute-start | bytes 1032200 | tf_op jit(solution)/shard_map/ppermute | solution.py:338
  41.1 9.6 %collective-permute-start.5 = (bf16[448,384]{1,0:T(8,128)(2,1)S(1)}, bf16[448,384]{1,0:T(8,128)(2,1)S(1)}, u32[]{:S(2)}, u32[]{:S(2)}) collective-permute-start(bf16[448,384]{1,0:T(8,128)(2,1)S(1)} %collective-permute-done.3), channel_id=1, source_target_pairs={{0,56},{8,0},{16,8},{24,16},{32,24},{40,32},{48,40},{56,48},{1,57}... | collective-permute-start | bytes 1032200 | tf_op jit(solution)/shard_map/ppermute | solution.py:338
  44.8 31.4 %copy-start.3 = (bf16[128,3584]{1,0:T(8,128)(2,1)}, bf16[128,3584]{1,0:T(8,128)(2,1)S(1)}, u32[]{:S(2)}) copy-start(bf16[128,3584]{1,0:T(8,128)(2,1)S(1)} %collective-permute-done.9.rest_11_) | copy-start | bytes 2752516
  45.7 10.9 %collective-permute-start.13 = (bf16[64,3584]{1,0:T(8,128)(2,1)}, bf16[64,3584]{1,0:T(8,128)(2,1)}, u32[]{:S(2)}, u32[]{:S(2)}) collective-permute-start(bf16[64,3584]{1,0:T(8,128)(2,1)} %slice.47), channel_id=1, source_target_pairs={{0,64},{64,128},{128,192},{192,0},{1,65},{65,129},{129,193},{193,1... | collective-permute-start | bytes 1376264 | tf_op jit(solution)/shard_map/ppermute | solution.py:338
  46.2 30.0 %copy-start.4 = (bf16[128,3584]{1,0:T(8,128)(2,1)}, bf16[128,3584]{1,0:T(8,128)(2,1)S(1)}, u32[]{:S(2)}) copy-start(bf16[128,3584]{1,0:T(8,128)(2,1)S(1)} %collective-permute-done.11.rest_13_) | copy-start | bytes 2752516
  47.1 9.6 %collective-permute-start.15 = (bf16[64,3584]{1,0:T(8,128)(2,1)}, bf16[64,3584]{1,0:T(8,128)(2,1)}, u32[]{:S(2)}, u32[]{:S(2)}) collective-permute-start(bf16[64,3584]{1,0:T(8,128)(2,1)} %slice.48), channel_id=1, source_target_pairs={{0,192},{64,0},{128,64},{192,128},{1,193},{65,1},{129,65},{193,129... | collective-permute-start | bytes 1376264 | tf_op jit(solution)/shard_map/ppermute | solution.py:338
  49.8 26.4 %collective-permute-start.10 = (bf16[128,3584]{1,0:T(8,128)(2,1)S(1)}, bf16[128,3584]{1,0:T(8,128)(2,1)}, u32[]{:S(2)}, u32[]{:S(2)}) collective-permute-start(bf16[128,3584]{1,0:T(8,128)(2,1)S(1)} %collective-permute-done.9.rest_11_), channel_id=1, source_target_pairs={{0,4},{4,0},{1,5},{5,1},{2,6},{6,2},{3,7},{7,3},{8,12},{12,8},{9,1... | collective-permute-start | bytes 2752520 | tf_op jit(solution)/shard_map/ppermute | solution.py:339
  50.7 25.5 %collective-permute-start.12 = (bf16[128,3584]{1,0:T(8,128)(2,1)S(1)}, bf16[128,3584]{1,0:T(8,128)(2,1)}, u32[]{:S(2)}, u32[]{:S(2)}) collective-permute-start(bf16[128,3584]{1,0:T(8,128)(2,1)S(1)} %collective-permute-done.11.rest_13_), channel_id=1, source_target_pairs={{0,4},{4,0},{1,5},{5,1},{2,6},{6,2},{3,7},{7,3},{8,12},{12,8},{9,1... | collective-permute-start | bytes 2752520 | tf_op jit(solution)/shard_map/ppermute | solution.py:339
  50.7 25.5 %copy-start.7 = (bf16[448,384]{1,0:T(8,128)(2,1)}, bf16[448,384]{1,0:T(8,128)(2,1)S(1)}, u32[]{:S(2)}) copy-start(bf16[448,384]{1,0:T(8,128)(2,1)S(1)} %collective-permute-done.5) | copy-start | bytes 1032196
  50.7 12.0 %collective-permute-start.4 = (bf16[448,384]{1,0:T(8,128)(2,1)}, bf16[448,384]{1,0:T(8,128)(2,1)S(1)}, u32[]{:S(2)}, u32[]{:S(2)}) collective-permute-start(bf16[448,384]{1,0:T(8,128)(2,1)} %collective-permute-done.2), channel_id=1, source_target_pairs={{0,8},{8,16},{16,24},{24,32},{32,40},{40,48},{48,56},{56,0},{1,9},... | collective-permute-start | bytes 1032200 | tf_op jit(solution)/shard_map/ppermute | solution.py:338
  56.6 19.6 %collective-permute-start.14 = (bf16[64,3584]{1,0:T(8,128)(2,1)}, bf16[64,3584]{1,0:T(8,128)(2,1)}, u32[]{:S(2)}, u32[]{:S(2)}) collective-permute-start(bf16[64,3584]{1,0:T(8,128)(2,1)} %collective-permute-done.13.rest_15_), channel_id=1, source_target_pairs={{0,4},{4,0},{1,5},{5,1},{2,6},{6,2},{3,7},{7,3},{8,12},{12,8},{9,1... | collective-permute-start | bytes 1376264 | tf_op jit(solution)/shard_map/ppermute | solution.py:339
  56.7 19.5 %collective-permute-start.16 = (bf16[64,3584]{1,0:T(8,128)(2,1)}, bf16[64,3584]{1,0:T(8,128)(2,1)}, u32[]{:S(2)}, u32[]{:S(2)}) collective-permute-start(bf16[64,3584]{1,0:T(8,128)(2,1)} %collective-permute-done.15.rest_17_), channel_id=1, source_target_pairs={{0,4},{4,0},{1,5},{5,1},{2,6},{6,2},{3,7},{7,3},{8,12},{12,8},{9,1... | collective-permute-start | bytes 1376264 | tf_op jit(solution)/shard_map/ppermute | solution.py:339
  62.7 13.6 %copy-start.8 = (bf16[448,384]{1,0:T(8,128)(2,1)}, bf16[448,384]{1,0:T(8,128)(2,1)S(1)}, u32[]{:S(2)}) copy-start(bf16[448,384]{1,0:T(8,128)(2,1)S(1)} %collective-permute-done.4) | copy-start | bytes 1032196
  62.7 5.9 %collective-permute-start.7 = (bf16[224,384]{1,0:T(8,128)(2,1)S(1)}, bf16[224,384]{1,0:T(8,128)(2,1)S(1)}, u32[]{:S(2)}, u32[]{:S(2)}) collective-permute-start(bf16[224,384]{1,0:T(8,128)(2,1)S(1)} %slice.46), channel_id=1, source_target_pairs={{0,56},{8,0},{16,8},{24,16},{32,24},{40,32},{48,40},{56,48},{1,57}... | collective-permute-start | bytes 516104 | tf_op jit(solution)/shard_map/ppermute | solution.py:338
  69.3 6.9 %collective-permute-start.6 = (bf16[224,384]{1,0:T(8,128)(2,1)}, bf16[224,384]{1,0:T(8,128)(2,1)}, u32[]{:S(2)}, u32[]{:S(2)}) collective-permute-start(bf16[224,384]{1,0:T(8,128)(2,1)} %slice.45), channel_id=1, source_target_pairs={{0,8},{8,16},{16,24},{24,32},{32,40},{40,48},{48,56},{56,0},{1,9},... | collective-permute-start | bytes 516104 | tf_op jit(solution)/shard_map/ppermute | solution.py:338
  113.3 61.5 %copy-start.1 = (s32[3]{0:T(128)S(1)}, s32[3]{0:T(128)}, u32[]{:S(2)}) copy-start(s32[3]{0:T(128)} %pad_add_fusion.ids) | copy-start | bytes 40
  149.8 2.2 %collective-permute-start.17 = (bf16[18,112,128]{2,1,0:T(8,128)(2,1)}, bf16[18,112,128]{2,1,0:T(8,128)(2,1)S(1)}, u32[]{:S(2)}, u32[]{:S(2)}) collective-permute-start(bf16[18,112,128]{2,1,0:T(8,128)(2,1)} %get-tuple-element.23.give_hbm), channel_id=1, source_target_pairs={{0,4},{4,0},{1,5},{5,1},{2,6},{6,2},{3,7},{7,3},{8,12},{12,8},{9,1... | collective-permute-start | bytes 1548296 | tf_op jit(solution)/shard_map/ppermute | solution.py:339
  156.0 14.7 %all-to-all-start.5 = ((bf16[16,112,128]{2,1,0:T(8,128)(2,1)}), bf16[16,112,128]{2,1,0:T(8,128)(2,1)S(1)}, u32[]{:S(2)}, u32[]{:S(2)}) async-start(bf16[16,112,128]{2,1,0:T(8,128)(2,1)} %get-tuple-element.24), calls=%async_computation.5 | async-start | bytes 917504 | tf_op jit(solution)/shard_map/all_to_all | solution.py:451
  160.8 13.9 %collective-permute-start.20 = (bf16[2,128,128]{2,1,0:T(8,128)(2,1)}, bf16[2,128,128]{2,1,0:T(8,128)(2,1)S(1)}, u32[]{:S(2)}, u32[]{:S(2)}) collective-permute-start(bf16[2,128,128]{2,1,0:T(8,128)(2,1)} %get-tuple-element.25.pair), channel_id=1, source_target_pairs={{0,128},{64,192},{128,0},{192,64},{1,129},{65,193},{129,1},{193,65... | collective-permute-start | bytes 196616 | tf_op jit(solution)/shard_map/ppermute | solution.py:338
  163.8 10.9 %collective-permute-start.19 = (bf16[2,128,128]{2,1,0:T(8,128)(2,1)}, bf16[2,128,128]{2,1,0:T(8,128)(2,1)S(1)}, u32[]{:S(2)}, u32[]{:S(2)}) collective-permute-start(bf16[2,128,128]{2,1,0:T(8,128)(2,1)} %get-tuple-element.25.pair), channel_id=1, source_target_pairs={{0,192},{64,0},{128,64},{192,128},{1,193},{65,1},{129,65},{193,129... | collective-permute-start | bytes 196616 | tf_op jit(solution)/shard_map/ppermute | solution.py:338
  165.0 9.8 %collective-permute-start.18 = (bf16[2,128,128]{2,1,0:T(8,128)(2,1)}, bf16[2,128,128]{2,1,0:T(8,128)(2,1)S(1)}, u32[]{:S(2)}, u32[]{:S(2)}) collective-permute-start(bf16[2,128,128]{2,1,0:T(8,128)(2,1)} %get-tuple-element.25.pair), channel_id=1, source_target_pairs={{0,64},{64,128},{128,192},{192,0},{1,65},{65,129},{129,193},{193,1... | collective-permute-start | bytes 196616 | tf_op jit(solution)/shard_map/ppermute | solution.py:338
  171.4 11.3 %all-to-all-start.6 = ((bf16[8,16,128]{2,1,0:T(8,128)(2,1)}), bf16[8,16,128]{2,1,0:T(8,128)(2,1)S(1)}, u32[]{:S(2)}, u32[]{:S(2)}) async-start(bf16[8,16,128]{2,1,0:T(8,128)(2,1)} %shard_map.102), calls=%async_computation.6 | async-start | bytes 65536 | tf_op jit(solution)/shard_map/all_to_all | solution.py:456
  (6 other events, 22.2 us)
